TPU v7x, 32 devices: a whole 2x2x4 slice. The times are simulated.
32 devices in a mesh: dp: 8 (over z, core), fsdp: 4 (over y, x).
Axes of the slice: x: 2, y: 2, z: 4, core: 2. Of those that a mesh axis runs over, the one named last changes fastest.
Arguments:
- hidden_in: bfloat16 [32, 256, 2048], P(('dp', 'fsdp')), may hold values from -48 to 48
- segment_ids: int32 [32, 256], P(('dp', 'fsdp')), may hold values from 0 to 2, never falling along the last dimension, each value on 1 to 128 neighbouring positions
- valid_mask: int32 [32, 256], P(('dp', 'fsdp')), may hold values from 0 to 1, as said below
- cotangent: bfloat16 [32, 256, 2048], P(('dp', 'fsdp')), may hold values from -6 to 6
- norm_attn: bfloat16 [2048], P('fsdp'), may hold values from 0.099609375 to 1.8984375
- w_query: bfloat16 [2048, 2048], P('fsdp'), may hold values from -0.4375 to 0.4375
- w_key: bfloat16 [2048, 512], P('fsdp'), may hold values from -0.4375 to 0.4375
- w_value: bfloat16 [2048, 512], P('fsdp'), may hold values from -0.125 to 0.125
- w_output: bfloat16 [2048, 2048], P('fsdp'), may hold values from -1.5 to 1.5
- norm_mlp: bfloat16 [2048], P('fsdp'), may hold values from 0.099609375 to 1.8984375
- w_gate: bfloat16 [2048, 8192], P('fsdp'), may hold values from -0.125 to 0.125
- w_up: bfloat16 [2048, 8192], P('fsdp'), may hold values from -0.125 to 0.125
- w_down: bfloat16 [8192, 2048], P('fsdp'), may hold values from -0.375 to 0.375
Outputs:
- hidden_out: bfloat16 [32, 256, 2048], P(('dp', 'fsdp'))
- input_grad: bfloat16 [32, 256, 2048], P(('dp', 'fsdp'))
- norm_attn_grad: float32 [2048], P('fsdp')
- w_query_grad: float32 [2048, 2048], P('fsdp')
- w_key_grad: float32 [2048, 512], P('fsdp')
- w_value_grad: float32 [2048, 512], P('fsdp')
- w_output_grad: float32 [2048, 2048], P('fsdp')
- norm_mlp_grad: float32 [2048], P('fsdp')
- w_gate_grad: float32 [2048, 8192], P('fsdp')
- w_up_grad: float32 [2048, 8192], P('fsdp')
- w_down_grad: float32 [8192, 2048], P('fsdp')
- statistics: float32 [5], replicated
Inputs may be any that keep to these rules, and one draw needn't show every extreme that they name: `segment_ids`: segment numbers start at 0 in each sequence and never fall; each of the 3 documents has 1 to 128 tokens. `valid_mask`: each sequence ends in a tail of 1 to 64 padded tokens marked 0; all others are 1.
All inputs are finite; a program needn't handle non-finite values.
Results may differ from a plain program's by a relative error of at most 0.015.
Values may be sent and summed in bfloat16 or wider, within the bound.
A program may use at most 576 MiB of HBM per device.

v0:
```python
import jax
import jax.numpy as jnp
from jax import lax
from jax.sharding import PartitionSpec as P

H = 32
KV = 8
HD = 64


EPSILON = 1e-05
RESIDUAL_SCALE = 0.22
SCORE_SCALE = 1.0 / 64.0
MASKED_SCORE = -1e30
ROPE_BASE = 10000000.0


def rope_tables(length, head_size):
    half_size = head_size // 2
    frequency = ROPE_BASE ** (-(jnp.arange(half_size, dtype=jnp.float32) * 2.0 / head_size))
    angles = jnp.arange(length, dtype=jnp.float32)[:, None] * frequency[None, :]
    return (jnp.cos(angles), jnp.sin(angles))


def rotate(tensor, cos_table, sin_table):
    half_size = tensor.shape[-1] // 2
    front_half = tensor[..., :half_size]
    back_half = tensor[..., half_size:]
    return jnp.concatenate(
        [
            front_half * cos_table - back_half * sin_table,
            back_half * cos_table + front_half * sin_table,
        ],
        axis=-1,
    )


def allowed_of(segments, validity):
    length = segments.shape[0]
    row_index = jnp.arange(length, dtype=jnp.int32)[:, None]
    col_index = jnp.arange(length, dtype=jnp.int32)[None, :]
    same_doc = segments[:, None] == segments[None, :]
    return (
        same_doc & (col_index <= row_index) & ((validity[None, :] == 1) | (col_index == row_index))
    )


def norm_forward(source, gain):
    scale_row = lax.rsqrt(jnp.mean(source * source, axis=-1, keepdims=True) + EPSILON)
    unit_rows = source * scale_row
    return (scale_row, unit_rows, (unit_rows * gain.astype(jnp.float32)).astype(jnp.bfloat16))


def norm_backward(grad_norm, scale_row, unit_rows, gain):
    gain_grad = jnp.sum(grad_norm * unit_rows, axis=0)
    scaled = grad_norm * gain.astype(jnp.float32)
    source_grad = scale_row * (
        scaled - unit_rows * jnp.mean(scaled * unit_rows, axis=-1, keepdims=True)
    )
    return (gain_grad, source_grad)


def scores_for(queries_grp, keys_grp, allowed):
    raw_scores = (
        jnp.einsum("tgd,ud->gtu", queries_grp, keys_grp, preferred_element_type=jnp.float32)
        * SCORE_SCALE
    )
    return jnp.where(allowed[None], raw_scores, MASKED_SCORE)


def attention_forward(queries_grp, keys_grp, values_grp, allowed):
    scores = scores_for(queries_grp, keys_grp, allowed)
    row_max = jnp.max(scores, axis=-1, keepdims=True)
    shifted = jnp.exp(scores - row_max)
    row_sum = jnp.sum(shifted, axis=-1, keepdims=True)
    weights_low = (shifted / row_sum).astype(jnp.bfloat16)
    combined = jnp.einsum(
        "gtu,ud->tgd", weights_low, values_grp, preferred_element_type=jnp.float32
    )
    return (combined, (row_max + jnp.log(row_sum))[..., 0])


def attention_backward(queries_grp, keys_grp, values_grp, grad_grp, log_total, allowed):
    scores = scores_for(queries_grp, keys_grp, allowed)
    probs = jnp.exp(scores - log_total[..., None])
    weights_low = probs.astype(jnp.bfloat16)
    prob_grad = jnp.einsum("tgd,ud->gtu", grad_grp, values_grp, preferred_element_type=jnp.float32)
    row_dot = jnp.sum(probs * prob_grad, axis=-1, keepdims=True)
    score_grad = (probs * (prob_grad - row_dot)).astype(jnp.bfloat16)
    query_grad = (
        jnp.einsum("gtu,ud->tgd", score_grad, keys_grp, preferred_element_type=jnp.float32)
        * SCORE_SCALE
    )
    key_grad = (
        jnp.einsum("gtu,tgd->ud", score_grad, queries_grp, preferred_element_type=jnp.float32)
        * SCORE_SCALE
    )
    value_grad = jnp.einsum(
        "gtu,tgd->ud", weights_low, grad_grp, preferred_element_type=jnp.float32
    )
    return (query_grad, key_grad, value_grad)


def owner_blocks(term, owners, replicas):
    row_total = term.shape[0]
    blocked = term.reshape((owners, replicas, row_total // (owners * replicas)) + term.shape[1:])
    return jnp.swapaxes(blocked, 0, 1).reshape(term.shape)


def contract_rows(left, right):
    return jnp.einsum("sa,sb->ab", left, right, preferred_element_type=jnp.float32)


def contract_cols(left, right):
    return jnp.einsum("sb,ab->sa", left, right, preferred_element_type=jnp.float32)


def global_statistics(tensors, valid_mask):
    validity = valid_mask[0].astype(jnp.float32)[:, None]
    squares = jnp.stack([jnp.sum(tensor * tensor * validity) for tensor in tensors])
    total_squares, total_valid = lax.psum((squares, jnp.sum(validity)), ("dp", "fsdp"))
    return jnp.sqrt(total_squares / (total_valid * tensors[0].shape[-1]))


def plan_gather(
    hidden_in,
    segment_ids,
    valid_mask,
    cotangent,
    norm_attn,
    w_query,
    w_key,
    w_value,
    w_output,
    norm_mlp,
    w_gate,
    w_up,
    w_down,
):
    hidden = hidden_in[0].astype(jnp.float32)
    length, model_width = hidden.shape
    groups = H // KV
    owners = lax.axis_size("fsdp")
    replicas = lax.axis_size("dp")
    allowed = allowed_of(segment_ids[0], valid_mask[0])
    cos_table, sin_table = rope_tables(length, HD)
    cos_heads = cos_table[:, None, :]
    sin_heads = sin_table[:, None, :]
    full_query, full_key, full_value, full_output, gain_attn = (
        lax.all_gather(w_query, "fsdp", axis=0, tiled=True),
        lax.all_gather(w_key, "fsdp", axis=0, tiled=True),
        lax.all_gather(w_value, "fsdp", axis=0, tiled=True),
        lax.all_gather(w_output, "fsdp", axis=0, tiled=True),
        lax.all_gather(norm_attn, "fsdp", axis=0, tiled=True),
    )
    scale_one, unit_one, normed_one = norm_forward(hidden, gain_attn)
    query_pre = jnp.dot(normed_one, full_query, preferred_element_type=jnp.float32)
    key_pre = jnp.dot(normed_one, full_key, preferred_element_type=jnp.float32)
    values = jnp.dot(normed_one, full_value, preferred_element_type=jnp.float32).astype(
        jnp.bfloat16
    )
    queries = rotate(query_pre.reshape(length, H, HD), cos_heads, sin_heads).astype(jnp.bfloat16)
    keys = rotate(key_pre.reshape(length, KV, HD), cos_heads, sin_heads).astype(jnp.bfloat16)
    queries_kv = jnp.transpose(queries.reshape(length, KV, groups, HD), (1, 0, 2, 3))
    keys_kv = jnp.transpose(keys, (1, 0, 2))
    values_kv = jnp.transpose(values.reshape(length, KV, HD), (1, 0, 2))

    def forward_group(pieces):
        return attention_forward(pieces[0], pieces[1], pieces[2], allowed)

    combined, log_totals = lax.map(forward_group, (queries_kv, keys_kv, values_kv))
    attended = jnp.transpose(combined, (1, 0, 2, 3)).reshape(length, H * HD).astype(jnp.bfloat16)
    attn_branch = jnp.dot(attended, full_output, preferred_element_type=jnp.float32)
    middle = hidden + RESIDUAL_SCALE * attn_branch
    full_gate, full_up, full_down, gain_mlp = (
        lax.all_gather(w_gate, "fsdp", axis=0, tiled=True),
        lax.all_gather(w_up, "fsdp", axis=0, tiled=True),
        lax.all_gather(w_down, "fsdp", axis=0, tiled=True),
        lax.all_gather(norm_mlp, "fsdp", axis=0, tiled=True),
    )
    scale_two, unit_two, normed_two = norm_forward(middle, gain_mlp)
    gate_proj = jnp.dot(normed_two, full_gate, preferred_element_type=jnp.float32)
    up_proj = jnp.dot(normed_two, full_up, preferred_element_type=jnp.float32)
    sigma = jax.nn.sigmoid(gate_proj)
    silu_gate = gate_proj * sigma
    mixed_act = (silu_gate * up_proj).astype(jnp.bfloat16)
    mlp_branch = jnp.dot(mixed_act, full_down, preferred_element_type=jnp.float32)
    result = middle + RESIDUAL_SCALE * mlp_branch
    statistics = global_statistics((hidden, middle, result, attn_branch, mlp_branch), valid_mask)
    back_gate, back_up, back_down, back_gain_mlp = (
        lax.all_gather(w_gate, "fsdp", axis=0, tiled=True),
        lax.all_gather(w_up, "fsdp", axis=0, tiled=True),
        lax.all_gather(w_down, "fsdp", axis=0, tiled=True),
        lax.all_gather(norm_mlp, "fsdp", axis=0, tiled=True),
    )
    result_grad = cotangent[0].astype(jnp.float32)
    mlp_out_grad = (RESIDUAL_SCALE * result_grad).astype(jnp.bfloat16)
    mixed_grad = contract_cols(mlp_out_grad, back_down)
    down_w_grad = contract_rows(mixed_act, mlp_out_grad)
    down_piece = lax.psum_scatter(
        owner_blocks(down_w_grad, owners, replicas), ("dp", "fsdp"), scatter_dimension=0, tiled=True
    )
    slope = sigma * (1.0 + gate_proj * (1.0 - sigma))
    gate_grad = (mixed_grad * up_proj * slope).astype(jnp.bfloat16)
    up_grad = (mixed_grad * silu_gate).astype(jnp.bfloat16)
    gate_w_grad = contract_rows(normed_two, gate_grad)
    up_w_grad = contract_rows(normed_two, up_grad)
    normed_two_grad = contract_cols(gate_grad, back_gate) + contract_cols(up_grad, back_up)
    gain_mlp_grad, middle_part = norm_backward(normed_two_grad, scale_two, unit_two, back_gain_mlp)
    middle_grad = result_grad + middle_part
    gain_mlp_piece, gate_piece, up_piece = (
        lax.psum_scatter(
            owner_blocks(gain_mlp_grad, owners, replicas),
            ("dp", "fsdp"),
            scatter_dimension=0,
            tiled=True,
        ),
        lax.psum_scatter(
            owner_blocks(gate_w_grad, owners, replicas),
            ("dp", "fsdp"),
            scatter_dimension=0,
            tiled=True,
        ),
        lax.psum_scatter(
            owner_blocks(up_w_grad, owners, replicas),
            ("dp", "fsdp"),
            scatter_dimension=0,
            tiled=True,
        ),
    )
    back_query, back_key, back_value, back_output, back_gain_attn = (
        lax.all_gather(w_query, "fsdp", axis=0, tiled=True),
        lax.all_gather(w_key, "fsdp", axis=0, tiled=True),
        lax.all_gather(w_value, "fsdp", axis=0, tiled=True),
        lax.all_gather(w_output, "fsdp", axis=0, tiled=True),
        lax.all_gather(norm_attn, "fsdp", axis=0, tiled=True),
    )
    attn_out_grad = (RESIDUAL_SCALE * middle_grad).astype(jnp.bfloat16)
    output_w_grad = contract_rows(attended, attn_out_grad)
    attended_grad = contract_cols(attn_out_grad, back_output).astype(jnp.bfloat16)
    attended_kv = jnp.transpose(attended_grad.reshape(length, KV, groups, HD), (1, 0, 2, 3))

    def backward_group(pieces):
        return attention_backward(pieces[0], pieces[1], pieces[2], pieces[3], pieces[4], allowed)

    query_grad, key_grad, value_grad = lax.map(
        backward_group, (queries_kv, keys_kv, values_kv, attended_kv, log_totals)
    )
    query_pre_grad = (
        rotate(
            jnp.transpose(query_grad, (1, 0, 2, 3)).reshape(length, H, HD), cos_heads, -sin_heads
        )
        .reshape(length, H * HD)
        .astype(jnp.bfloat16)
    )
    key_pre_grad = (
        rotate(jnp.transpose(key_grad, (1, 0, 2)), cos_heads, -sin_heads)
        .reshape(length, KV * HD)
        .astype(jnp.bfloat16)
    )
    value_pre_grad = (
        jnp.transpose(value_grad, (1, 0, 2)).reshape(length, KV * HD).astype(jnp.bfloat16)
    )
    query_w_grad = contract_rows(normed_one, query_pre_grad)
    key_w_grad = contract_rows(normed_one, key_pre_grad)
    value_w_grad = contract_rows(normed_one, value_pre_grad)
    normed_one_grad = (
        contract_cols(query_pre_grad, back_query)
        + contract_cols(key_pre_grad, back_key)
        + contract_cols(value_pre_grad, back_value)
    )
    gain_attn_grad, hidden_part = norm_backward(
        normed_one_grad, scale_one, unit_one, back_gain_attn
    )
    input_grad = (middle_grad + hidden_part).astype(jnp.bfloat16)
    gain_attn_piece, query_piece, key_piece, value_piece, output_piece = (
        lax.psum_scatter(
            owner_blocks(gain_attn_grad, owners, replicas),
            ("dp", "fsdp"),
            scatter_dimension=0,
            tiled=True,
        ),
        lax.psum_scatter(
            owner_blocks(query_w_grad, owners, replicas),
            ("dp", "fsdp"),
            scatter_dimension=0,
            tiled=True,
        ),
        lax.psum_scatter(
            owner_blocks(key_w_grad, owners, replicas),
            ("dp", "fsdp"),
            scatter_dimension=0,
            tiled=True,
        ),
        lax.psum_scatter(
            owner_blocks(value_w_grad, owners, replicas),
            ("dp", "fsdp"),
            scatter_dimension=0,
            tiled=True,
        ),
        lax.psum_scatter(
            owner_blocks(output_w_grad, owners, replicas),
            ("dp", "fsdp"),
            scatter_dimension=0,
            tiled=True,
        ),
    )
    finals = (
        lax.all_gather(gain_attn_piece.astype(jnp.bfloat16), "dp", axis=0, tiled=True).astype(
            gain_attn_piece.dtype
        ),
        lax.all_gather(query_piece.astype(jnp.bfloat16), "dp", axis=0, tiled=True).astype(
            query_piece.dtype
        ),
        lax.all_gather(key_piece.astype(jnp.bfloat16), "dp", axis=0, tiled=True).astype(
            key_piece.dtype
        ),
        lax.all_gather(value_piece.astype(jnp.bfloat16), "dp", axis=0, tiled=True).astype(
            value_piece.dtype
        ),
        lax.all_gather(output_piece.astype(jnp.bfloat16), "dp", axis=0, tiled=True).astype(
            output_piece.dtype
        ),
        lax.all_gather(gain_mlp_piece.astype(jnp.bfloat16), "dp", axis=0, tiled=True).astype(
            gain_mlp_piece.dtype
        ),
        lax.all_gather(gate_piece.astype(jnp.bfloat16), "dp", axis=0, tiled=True).astype(
            gate_piece.dtype
        ),
        lax.all_gather(up_piece.astype(jnp.bfloat16), "dp", axis=0, tiled=True).astype(
            up_piece.dtype
        ),
        lax.all_gather(down_piece.astype(jnp.bfloat16), "dp", axis=0, tiled=True).astype(
            down_piece.dtype
        ),
    )
    return (
        result.astype(jnp.bfloat16)[None],
        input_grad[None],
        finals[0],
        finals[1],
        finals[2],
        finals[3],
        finals[4],
        finals[5],
        finals[6],
        finals[7],
        finals[8],
        statistics,
    )


def shards(
    hidden_in,
    segment_ids,
    valid_mask,
    cotangent,
    norm_attn,
    w_query,
    w_key,
    w_value,
    w_output,
    norm_mlp,
    w_gate,
    w_up,
    w_down,
):
    return plan_gather(
        hidden_in,
        segment_ids,
        valid_mask,
        cotangent,
        norm_attn,
        w_query,
        w_key,
        w_value,
        w_output,
        norm_mlp,
        w_gate,
        w_up,
        w_down,
    )


def solution(mesh):
    return jax.shard_map(
        shards,
        mesh=mesh,
        in_specs=(
            P(("dp", "fsdp"), None, None),
            P(("dp", "fsdp"), None),
            P(("dp", "fsdp"), None),
            P(("dp", "fsdp"), None, None),
            P("fsdp"),
            P("fsdp", None),
            P("fsdp", None),
            P("fsdp", None),
            P("fsdp", None),
            P("fsdp"),
            P("fsdp", None),
            P("fsdp", None),
            P("fsdp", None),
        ),
        out_specs=(
            P(("dp", "fsdp"), None, None),
            P(("dp", "fsdp"), None, None),
            P("fsdp"),
            P("fsdp", None),
            P("fsdp", None),
            P("fsdp", None),
            P("fsdp", None),
            P("fsdp"),
            P("fsdp", None),
            P("fsdp", None),
            P("fsdp", None),
            P(),
        ),
        check_vma=False,
    )
```

profile of v0, /device:TPU:0, one launch (start us, length us, event | category | flops | bytes accessed | tf_op | source)
XLA Modules:
  0.0 6811.6 jit_solution(12372464982121008071)
XLA Ops:
  51.1 34.0 all-gather.17.cloned.1.call-done
  91.6 83.1 %all-gather.19.cloned.1.call-done = bf16[2048,2048]{1,0:T(8,128)(2,1)} async-done(((bf16[512,2048]{1,0:T(8,128)(2,1)}), bf16[2048,2048]{1,0:T(8,128)(2,1)}) %all-gather.19.cloned.1.call-update) | async-done | bytes 8388624 | tf_op jit(solution)/shard_map/all_gather | solution.py:150
  212.5 51.5 all-gather.21.cloned.1.call-done
  271.7 291.2 %all-gather.23.cloned.1.call-done = bf16[2048,8192]{1,0:T(8,128)(2,1)} async-done(((bf16[512,8192]{1,0:T(8,128)(2,1)}), bf16[2048,8192]{1,0:T(8,128)(2,1)}) %all-gather.23.cloned.1.call-update) | async-done | bytes 33554448 | tf_op jit(solution)/shard_map/all_gather | solution.py:176
  584.3 277.5 %all-gather.25.cloned.1.call-done = bf16[2048,8192]{1,0:T(8,128)(2,1)} async-done(((bf16[512,8192]{1,0:T(8,128)(2,1)}), bf16[2048,8192]{1,0:T(8,128)(2,1)}) %all-gather.25.cloned.1.call-update) | async-done | bytes 33554448 | tf_op jit(solution)/shard_map/all_gather | solution.py:177
  861.8 27.2 fusion.54
  889.0 271.9 %all-gather.27.cloned.1.call-done = bf16[8192,2048]{1,0:T(8,128)(2,1)} async-done(((bf16[2048,2048]{1,0:T(8,128)(2,1)}), bf16[8192,2048]{1,0:T(8,128)(2,1)}) %all-gather.27.cloned.1.call-update) | async-done | bytes 33554448 | tf_op jit(solution)/shard_map/all_gather | solution.py:178
  1218.1 26.6 multiply_reduce_fusion.1
  1265.2 52.6 while.31
  1340.7 25.9 fusion.113
  1366.6 44.6 copy.103
  1437.0 44.5 copy.102
  1513.7 45.4 copy.105
  1568.0 46.2 reduce-scatter.14.cloned.1.call-done
  1616.1 360.1 %reduce-scatter.8.cloned.1.call-done = f32[64,2048]{1,0:T(8,128)} async-done(((f32[2048,2048]{1,0:T(8,128)}), f32[64,2048]{1,0:T(8,128)}) %reduce-scatter.8.cloned.1.call-update) | async-done | bytes 524304 | tf_op jit(solution)/shard_map/reduce_scatter | solution.py:283
  1978.0 1406.1 %reduce-scatter.18.cloned.1.call-done = f32[64,8192]{1,0:T(8,128)} async-done(((f32[2048,8192]{1,0:T(8,128)}), f32[64,8192]{1,0:T(8,128)}) %reduce-scatter.18.cloned.1.call-update) | async-done | bytes 2097168 | tf_op jit(solution)/shard_map/reduce_scatter | solution.py:224
  3386.9 1404.2 %reduce-scatter.16.cloned.1.call-done = f32[64,8192]{1,0:T(8,128)} async-done(((f32[2048,8192]{1,0:T(8,128)}), f32[64,8192]{1,0:T(8,128)}) %reduce-scatter.16.cloned.1.call-update) | async-done | bytes 2097168 | tf_op jit(solution)/shard_map/reduce_scatter | solution.py:218
  4793.9 1403.9 %reduce-scatter.20.cloned.1.call-done = f32[256,2048]{1,0:T(8,128)} async-done(((f32[8192,2048]{1,0:T(8,128)}), f32[256,2048]{1,0:T(8,128)}) %reduce-scatter.20.cloned.1.call-update) | async-done | bytes 2097168 | tf_op jit(solution)/shard_map/reduce_scatter | solution.py:200
  6206.1 41.3 all-reduce.4
  6269.3 73.8 %reduce-scatter.12.cloned.1.call-done = f32[64,512]{1,0:T(8,128)} async-done(((f32[2048,512]{1,0:T(8,128)}), f32[64,512]{1,0:T(8,128)}) %reduce-scatter.12.cloned.1.call-update) | async-done | bytes 131088 | tf_op jit(solution)/shard_map/reduce_scatter | solution.py:295
  6360.2 124.9 %reduce-scatter.10.cloned.1.call-done = f32[64,512]{1,0:T(8,128)} async-done(((f32[2048,512]{1,0:T(8,128)}), f32[64,512]{1,0:T(8,128)}) %reduce-scatter.10.cloned.1.call-update) | async-done | bytes 131088 | tf_op jit(solution)/shard_map/reduce_scatter | solution.py:289
  6548.6 79.5 %all-gather.35.cloned.1.call-done = bf16[512,8192]{1,0:T(8,128)(2,1)} async-done(((bf16[64,8192]{1,0:T(8,128)(2,1)}), bf16[512,8192]{1,0:T(8,128)(2,1)}) %all-gather.35.cloned.1.call-update) | async-done | bytes 8388624 | tf_op jit(solution)/shard_map/all_gather | solution.py:330
  6640.6 70.1 %all-gather.33.cloned.1.call-done = bf16[512,8192]{1,0:T(8,128)(2,1)} async-done(((bf16[64,8192]{1,0:T(8,128)(2,1)}), bf16[512,8192]{1,0:T(8,128)(2,1)}) %all-gather.33.cloned.1.call-update) | async-done | bytes 8388624 | tf_op jit(solution)/shard_map/all_gather | solution.py:327
  6723.3 69.7 %all-gather.37.cloned.1.call-done = bf16[2048,2048]{1,0:T(8,128)(2,1)} async-done(((bf16[256,2048]{1,0:T(8,128)(2,1)}), bf16[2048,2048]{1,0:T(8,128)(2,1)}) %all-gather.37.cloned.1.call-update) | async-done | bytes 8388624 | tf_op jit(solution)/shard_map/all_gather | solution.py:333
  (331 shorter events, 510.1 us)
Async XLA Ops:
  7.2 40.8 all-gather.15.cloned.1.call-start
  7.9 77.2 %all-gather.17.cloned.1.call-start = ((), (), s32[]{:S(2)}) async-start(), calls=%async_computation.8 | async-start | bytes 2621440 | tf_op jit(solution)/shard_map/all_gather | solution.py:151
  8.7 166.0 %all-gather.19.cloned.1.call-start = ((), (), s32[]{:S(2)}) async-start(), calls=%async_computation.9 | async-start | bytes 10485760 | tf_op jit(solution)/shard_map/all_gather | solution.py:150
  9.4 254.6 %all-gather.21.cloned.1.call-start = ((), (), s32[]{:S(2)}) async-start(), calls=%async_computation.10 | async-start | bytes 10485760 | tf_op jit(solution)/shard_map/all_gather | solution.py:153
  10.0 552.9 %all-gather.23.cloned.1.call-start = ((), (), s32[]{:S(2)}) async-start(), calls=%async_computation.11 | async-start | bytes 41943040 | tf_op jit(solution)/shard_map/all_gather | solution.py:176
  10.6 851.3 %all-gather.25.cloned.1.call-start = ((), (), s32[]{:S(2)}) async-start(), calls=%async_computation.12 | async-start | bytes 41943040 | tf_op jit(solution)/shard_map/all_gather | solution.py:177
  11.2 1149.7 %all-gather.27.cloned.1.call-start = ((), (), s32[]{:S(2)}) async-start(), calls=%async_computation.13 | async-start | bytes 41943040 | tf_op jit(solution)/shard_map/all_gather | solution.py:178
  11.9 1602.3 %reduce-scatter.14.cloned.1.call-start = ((), (), s32[]{:S(2)}) async-start(), calls=%async_computation.18 | async-start | bytes 17301504 | tf_op jit(solution)/shard_map/reduce_scatter | solution.py:301
  1256.5 719.7 %reduce-scatter.8.cloned.1.call-start = ((), (), s32[]{:S(2)}) async-start(), calls=%async_computation.14 | async-start | bytes 17301504 | tf_op jit(solution)/shard_map/reduce_scatter | solution.py:283
  1339.5 2044.7 %reduce-scatter.18.cloned.1.call-start = ((), (), s32[]{:S(2)}) async-start(), calls=%async_computation.22 | async-start | bytes 69206016 | tf_op jit(solution)/shard_map/reduce_scatter | solution.py:224
  1411.2 3379.9 %reduce-scatter.16.cloned.1.call-start = ((), (), s32[]{:S(2)}) async-start(), calls=%async_computation.20 | async-start | bytes 69206016 | tf_op jit(solution)/shard_map/reduce_scatter | solution.py:218
  1481.6 4716.3 %reduce-scatter.20.cloned.1.call-start = ((), (), s32[]{:S(2)}) async-start(), calls=%async_computation.24 | async-start | bytes 69206016 | tf_op jit(solution)/shard_map/reduce_scatter | solution.py:200
  1559.1 4784.0 %reduce-scatter.12.cloned.1.call-start = ((), (), s32[]{:S(2)}) async-start(), calls=%async_computation.17 | async-start | bytes 4325376 | tf_op jit(solution)/shard_map/reduce_scatter | solution.py:295
  1563.7 4921.4 %reduce-scatter.10.cloned.1.call-start = ((), (), s32[]{:S(2)}) async-start(), calls=%async_computation.16 | async-start | bytes 4325376 | tf_op jit(solution)/shard_map/reduce_scatter | solution.py:289
  1568.0 4946.6 %all-gather.31.cloned.1.call-start = ((), (), s32[]{:S(2)}) async-start(), calls=%async_computation.19 | async-start | bytes 2359296 | tf_op jit(solution)/shard_map/all_gather | solution.py:321
  1616.0 4928.5 %all-gather.29.cloned.1.call-start = ((), (), s32[]{:S(2)}) async-start(), calls=%async_computation.15 | async-start | bytes 2359296 | tf_op jit(solution)/shard_map/all_gather | solution.py:312
  1978.0 4650.1 %all-gather.35.cloned.1.call-start = ((), (), s32[]{:S(2)}) async-start(), calls=%async_computation.23 | async-start | bytes 9437184 | tf_op jit(solution)/shard_map/all_gather | solution.py:330
  3386.8 3323.9 %all-gather.33.cloned.1.call-start = ((), (), s32[]{:S(2)}) async-start(), calls=%async_computation.21 | async-start | bytes 9437184 | tf_op jit(solution)/shard_map/all_gather | solution.py:327
  4793.8 1472.3 %copy-start.39 = (f32[256]{0:T(256)S(1)}, f32[256]{0:T(256)}, u32[]{:S(2)}) copy-start(f32[256]{0:T(256)} %get-tuple-element.158) | copy-start | bytes 3076
  4793.8 1472.3 %copy-start.3 = (f32[256,2048]{1,0:T(8,128)S(1)}, f32[256,2048]{1,0:T(8,128)}, u32[]{:S(2)}) copy-start(f32[256,2048]{1,0:T(8,128)} %copy-done.2) | copy-start | bytes 6291460
  4793.9 1472.3 %copy-start.8 = (bf16[1,256,2048]{2,1,0:T(8,128)(2,1)S(1)}, bf16[1,256,2048]{2,1,0:T(8,128)(2,1)}, u32[]{:S(2)}) copy-start(bf16[1,256,2048]{2,1,0:T(8,128)(2,1)} %param.17) | copy-start | bytes 3145732
  4793.9 1472.2 %copy-start.31 = (f32[4,1,512]{2,1,0:T(1,128)S(1)}, f32[4,1,512]{2,1,0:T(1,128)}, u32[]{:S(2)}) copy-start(f32[4,1,512]{2,1,0:T(1,128)} %copy-done.29) | copy-start | bytes 24580
  4793.9 1472.2 %copy-start.37 = (f32[256]{0:T(256)S(1)}, f32[256]{0:T(256)}, u32[]{:S(2)}) copy-start(f32[256]{0:T(256)} %copy-done.35) | copy-start | bytes 3076
  4793.9 1999.1 %all-gather.37.cloned.1.call-start = ((), (), s32[]{:S(2)}) async-start(), calls=%async_computation.25 | async-start | bytes 9437184 | tf_op jit(solution)/shard_map/all_gather | solution.py:333
  (40 other events, 8079.4 us)
Sparse Core Ops, SparseCore 0:
  9.9 38.0 all-gather.14
  49.8 35.2 all-gather.16
  87.0 87.5 all-gather.18
  176.3 87.5 all-gather.20
  265.7 297.2 all-gather.22
  564.6 297.2 all-gather.24
  863.7 297.2 all-gather.26
  1256.6 357.5 reduce-scatter.13
  1617.1 359.0 reduce-scatter.7
  1978.4 1405.6 reduce-scatter.17
  3386.5 1404.5 reduce-scatter.15
  4793.3 1404.5 reduce-scatter.19
  6200.7 142.3 reduce-scatter.11
  6345.8 139.2 reduce-scatter.9
  6486.5 28.0 all-gather.30
  6516.6 27.8 all-gather.28
  6546.5 81.5 all-gather.34
  6630.1 80.5 all-gather.32
  6712.3 80.5 all-gather.36
where the time goes:
time: 6820 us; the launch traced here: 6810 us
  waiting for transfers between devices  6110 us (90%)
  matrix products  304 us (4%)
  local copies, waits for them, and re-layouts  193 us (3%)
  blocking collectives  106 us (2%)
  other arithmetic  84 us (1%)
    reduce_scatter x1, waiting for transfers between devices, plan_gather(): lax.psum_scatter(owner_blocks(up_w_grad, owners, replicas), ('dp', 'fsdp'...  1410 us
    reduce_scatter x1, waiting for transfers between devices, plan_gather(): lax.psum_scatter(owner_blocks(gate_w_grad, owners, replicas), ('dp', 'fsd...  1400 us
    reduce_scatter x1, waiting for transfers between devices, plan_gather(): lax.psum_scatter(owner_blocks(down_w_grad, owners, replicas), ('dp', 'fsd...  1400 us
    reduce_scatter x1, waiting for transfers between devices, plan_gather(): lax.psum_scatter(owner_blocks(query_w_grad, owners, replicas), ('dp', 'fs...  360 us
    all_gather x1, waiting for transfers between devices, plan_gather(): lax.all_gather(w_gate, 'fsdp', axis=0, tiled=True)  291 us
    all_gather x1, waiting for transfers between devices, plan_gather(): lax.all_gather(w_up, 'fsdp', axis=0, tiled=True)  278 us
    all_gather x1, waiting for transfers between devices, plan_gather(): lax.all_gather(w_down, 'fsdp', axis=0, tiled=True)  272 us
    transpose x9, local copies, waits for them, and re-layouts, owner_blocks(): return jnp.swapaxes(blocked, 0, 1).reshape(term.shape)  153 us
  transfers between devices with their start and end apart: 19, of which 19 were waited for; matrix products, arithmetic and copies ran while one was open for 7% of the time, Pallas kernels for 0%

commit v1 on v0

v1 whole, which is shorter than its diff:
```python
import jax
import jax.numpy as jnp
from jax import lax
from jax.sharding import Mesh
from jax.sharding import PartitionSpec as P

H = 32
KV = 8
HD = 64
GROUPS = H // KV

EPSILON = 1e-05
RESIDUAL_SCALE = 0.22
SCORE_SCALE = 1.0 / 64.0
MASKED_SCORE = -1e30
ROPE_BASE = 10000000.0

BF16 = jnp.bfloat16
F32 = jnp.float32


def rope_tables(length, head_size):
    half_size = head_size // 2
    frequency = ROPE_BASE ** (-(jnp.arange(half_size, dtype=F32) * 2.0 / head_size))
    angles = jnp.arange(length, dtype=F32)[:, None] * frequency[None, :]
    return (jnp.cos(angles), jnp.sin(angles))


def rotate(tensor, cos_table, sin_table):
    half_size = tensor.shape[-1] // 2
    front_half = tensor[..., :half_size]
    back_half = tensor[..., half_size:]
    return jnp.concatenate(
        [
            front_half * cos_table - back_half * sin_table,
            back_half * cos_table + front_half * sin_table,
        ],
        axis=-1,
    )


def dot_f32(left, right):
    return jnp.dot(left, right, preferred_element_type=F32)


def contract_rows(left, right):
    return jnp.einsum("sa,sb->ab", left, right, preferred_element_type=F32)


def contract_cols(left, right):
    return jnp.einsum("sb,ab->sa", left, right, preferred_element_type=F32)


def row_scale(source):
    return lax.rsqrt(jnp.mean(source * source, axis=-1, keepdims=True) + EPSILON)


def norm_backward(grad_norm, scale_row, unit_rows, gain):
    gain_grad = jnp.sum(grad_norm * unit_rows, axis=0)
    scaled = grad_norm * gain
    source_grad = scale_row * (
        scaled - unit_rows * jnp.mean(scaled * unit_rows, axis=-1, keepdims=True)
    )
    return (gain_grad, source_grad)


def gather_tokens(block):
    return lax.all_gather(block, ("sub", "fsdp"), axis=0, tiled=True)


def scatter_tokens(partial):
    return lax.psum_scatter(partial, ("sub", "fsdp"), scatter_dimension=0, tiled=True)


def column_blocks(weight, owners, subs):
    rows, columns = weight.shape
    blocked = weight.reshape(rows, owners, subs, columns // (owners * subs))
    mine = lax.dynamic_index_in_dim(blocked, lax.axis_index("sub"), axis=2, keepdims=False)
    return jnp.swapaxes(mine, 0, 1)


def regroup_columns(weights, owners, subs):
    blocks = jnp.concatenate([column_blocks(w, owners, subs) for w in weights], axis=-1)
    moved = lax.all_to_all(blocks, "fsdp", split_axis=0, concat_axis=0, tiled=True)
    return moved.reshape(-1, moved.shape[-1])


def row_block(weight, subs):
    rows = weight.shape[0] // subs
    return lax.dynamic_slice_in_dim(weight, lax.axis_index("sub") * rows, rows, axis=0)


def finish_rows(term):
    piece = lax.psum_scatter(term, "rep", scatter_dimension=0, tiled=True)
    spread = lax.all_gather(piece, ("rep", "sub"), axis=0, tiled=False)
    rep, subs = lax.axis_size("rep"), lax.axis_size("sub")
    spread = spread.reshape((rep, subs) + piece.shape)
    return jnp.swapaxes(spread, 0, 1).reshape(-1, piece.shape[-1]).astype(F32)


def finish_columns(term, widths):
    owners, rep, subs = lax.axis_size("fsdp"), lax.axis_size("rep"), lax.axis_size("sub")
    rows, columns = term.shape
    blocked = jnp.swapaxes(term.reshape(owners, rep, rows // (owners * rep), columns), 0, 1)
    blocked = blocked.reshape(rows, columns)
    piece = lax.psum_scatter(blocked, "rep", scatter_dimension=0, tiled=True)
    piece = piece.reshape(owners, -1, columns)
    moved = lax.all_to_all(piece, "fsdp", split_axis=0, concat_axis=0, tiled=True)
    spread = lax.all_gather(moved, ("rep", "sub"), axis=0, tiled=False)
    spread = spread.reshape((rep, subs) + moved.shape)
    outs = []
    at = 0
    for width in widths:
        part = lax.slice_in_dim(spread, at, at + width, axis=4)
        part = jnp.transpose(part, (0, 3, 2, 1, 4))
        outs.append(part.reshape(rep * moved.shape[1], owners * subs * width).astype(F32))
        at += width
    return outs


def shards(
    hidden_in,
    segment_ids,
    valid_mask,
    cotangent,
    norm_attn,
    w_query,
    w_key,
    w_value,
    w_output,
    norm_mlp,
    w_gate,
    w_up,
    w_down,
):
    owners, subs = lax.axis_size("fsdp"), lax.axis_size("sub")
    members = owners * subs
    length, width = hidden_in.shape[1:]
    tokens = members * length

    gains = lax.all_gather(jnp.stack([norm_attn, norm_mlp]), "fsdp", axis=1, tiled=True)
    gain_attn = gains[0].astype(F32)
    gain_mlp = gains[1].astype(F32)
    codes = gather_tokens(segment_ids * 2 + valid_mask)
    hidden_low = gather_tokens(hidden_in).reshape(tokens, width)
    qkv = regroup_columns((w_query, w_key, w_value), owners, subs)
    out_rows = row_block(w_output, subs)
    gate_up = regroup_columns((w_gate, w_up), owners, subs)
    down_rows = row_block(w_down, subs)
    ff = down_rows.shape[0]

    hidden_all = hidden_low.astype(F32)
    normed_one = (hidden_all * row_scale(hidden_all) * gain_attn).astype(BF16)
    projected = dot_f32(normed_one, qkv)
    q_width, k_width = GROUPS * HD, HD
    cos_table, sin_table = rope_tables(length, HD)
    cos_heads = cos_table[None, :, None, :]
    sin_heads = sin_table[None, :, None, :]
    per_seq = projected.reshape(members, length, GROUPS + 2, HD)
    queries = rotate(per_seq[:, :, :GROUPS], cos_heads, sin_heads).astype(BF16)
    keys = rotate(per_seq[:, :, GROUPS : GROUPS + 1], cos_heads, sin_heads).astype(BF16)[:, :, 0]
    values = per_seq[:, :, GROUPS + 1].astype(BF16)

    segments, validity = codes // 2, codes % 2
    row_index = jnp.arange(length, dtype=jnp.int32)[:, None]
    col_index = jnp.arange(length, dtype=jnp.int32)[None, :]
    allowed = (
        (segments[:, :, None] == segments[:, None, :])
        & (col_index <= row_index)
        & ((validity[:, None, :] == 1) | (col_index == row_index))
    )[:, None]
    scores = jnp.einsum("stgd,sud->sgtu", queries, keys, preferred_element_type=F32) * SCORE_SCALE
    scores = jnp.where(allowed, scores, MASKED_SCORE)
    shifted = jnp.exp(scores - jnp.max(scores, axis=-1, keepdims=True))
    probs = shifted / jnp.sum(shifted, axis=-1, keepdims=True)
    probs_low = probs.astype(BF16)
    attended = jnp.einsum("sgtu,sud->stgd", probs_low, values, preferred_element_type=F32)
    attended = attended.reshape(tokens, q_width).astype(BF16)
    attn_branch = scatter_tokens(dot_f32(attended, out_rows).astype(BF16)).astype(F32)

    hidden = hidden_in[0].astype(F32)
    scale_one = row_scale(hidden)
    unit_one = hidden * scale_one
    middle = hidden + RESIDUAL_SCALE * attn_branch
    scale_two = row_scale(middle)
    unit_two = middle * scale_two
    normed_two = gather_tokens((unit_two * gain_mlp).astype(BF16))
    gate_up_proj = dot_f32(normed_two, gate_up)
    gate_proj, up_proj = gate_up_proj[:, :ff], gate_up_proj[:, ff:]
    sigma = jax.nn.sigmoid(gate_proj)
    silu_gate = gate_proj * sigma
    mixed_act = (silu_gate * up_proj).astype(BF16)
    mlp_branch = scatter_tokens(dot_f32(mixed_act, down_rows).astype(BF16)).astype(F32)
    result = middle + RESIDUAL_SCALE * mlp_branch

    result_grad = cotangent[0].astype(F32)
    mlp_out_grad = gather_tokens((RESIDUAL_SCALE * result_grad).astype(BF16))
    mixed_grad = contract_cols(mlp_out_grad, down_rows)
    down_w_grad = contract_rows(mixed_act, mlp_out_grad).astype(BF16)
    slope = sigma * (1.0 + gate_proj * (1.0 - sigma))
    gate_grad = (mixed_grad * up_proj * slope).astype(BF16)
    up_grad = (mixed_grad * silu_gate).astype(BF16)
    gate_up_grad = jnp.concatenate([gate_grad, up_grad], axis=1)
    normed_two_grad = scatter_tokens(contract_cols(gate_up_grad, gate_up).astype(BF16)).astype(F32)
    gate_up_w_grad = contract_rows(normed_two, gate_up_grad).astype(BF16)
    gain_mlp_grad, middle_part = norm_backward(normed_two_grad, scale_two, unit_two, gain_mlp)
    middle_grad = result_grad + middle_part

    attn_out_grad = gather_tokens((RESIDUAL_SCALE * middle_grad).astype(BF16))
    attended_grad = contract_cols(attn_out_grad, out_rows).astype(BF16)
    output_w_grad = contract_rows(attended, attn_out_grad).astype(BF16)
    heads_grad = attended_grad.reshape(members, length, GROUPS, HD)
    prob_grad = jnp.einsum("stgd,sud->sgtu", heads_grad, values, preferred_element_type=F32)
    row_dot = jnp.sum(probs * prob_grad, axis=-1, keepdims=True)
    score_grad = (probs * (prob_grad - row_dot)).astype(BF16)
    query_grad = (
        jnp.einsum("sgtu,sud->stgd", score_grad, keys, preferred_element_type=F32) * SCORE_SCALE
    )
    key_grad = (
        jnp.einsum("sgtu,stgd->sud", score_grad, queries, preferred_element_type=F32) * SCORE_SCALE
    )
    value_grad = jnp.einsum("sgtu,stgd->sud", probs_low, heads_grad, preferred_element_type=F32)
    qkv_grad = jnp.concatenate(
        [
            rotate(query_grad, cos_heads, -sin_heads),
            rotate(key_grad[:, :, None], cos_heads, -sin_heads),
            value_grad[:, :, None],
        ],
        axis=2,
    )
    qkv_grad = qkv_grad.reshape(tokens, q_width + 2 * k_width).astype(BF16)
    normed_one_grad = scatter_tokens(contract_cols(qkv_grad, qkv).astype(BF16)).astype(F32)
    qkv_w_grad = contract_rows(normed_one, qkv_grad).astype(BF16)
    gain_attn_grad, hidden_part = norm_backward(normed_one_grad, scale_one, unit_one, gain_attn)
    input_grad = (middle_grad + hidden_part).astype(BF16)

    validity_own = valid_mask[0].astype(F32)[:, None]
    squares = [
        jnp.sum(tensor * tensor * validity_own)
        for tensor in (hidden, middle, result, attn_branch, mlp_branch)
    ]
    tally = jnp.concatenate(
        [gain_attn_grad, gain_mlp_grad, jnp.stack(squares + [jnp.sum(validity_own)])]
    )
    tally = lax.psum(tally, ("rep", "sub", "fsdp"))
    part = width // owners
    start = lax.axis_index("fsdp") * part
    gain_attn_out = lax.dynamic_slice_in_dim(tally, start, part)
    gain_mlp_out = lax.dynamic_slice_in_dim(tally, width + start, part)
    statistics = jnp.sqrt(tally[2 * width : 2 * width + 5] / (tally[2 * width + 5] * width))

    down_out = finish_rows(down_w_grad)
    gate_out, up_out = finish_columns(gate_up_w_grad, (ff, ff))
    output_out = finish_rows(output_w_grad)
    query_out, key_out, value_out = finish_columns(qkv_w_grad, (q_width, k_width, k_width))
    return (
        result.astype(BF16)[None],
        input_grad[None],
        gain_attn_out,
        query_out,
        key_out,
        value_out,
        output_out,
        gain_mlp_out,
        gate_out,
        up_out,
        down_out,
        statistics,
    )


def solution(mesh):
    fsdp = mesh.shape["fsdp"]
    subs = max(1, KV // fsdp)
    rep = mesh.shape["dp"] // subs
    plane_mesh = Mesh(mesh.devices.reshape(rep, subs, fsdp), ("rep", "sub", "fsdp"))
    batch = ("rep", "sub", "fsdp")
    return jax.shard_map(
        shards,
        mesh=plane_mesh,
        in_specs=(
            P(batch, None, None),
            P(batch, None),
            P(batch, None),
            P(batch, None, None),
            P("fsdp"),
            P("fsdp", None),
            P("fsdp", None),
            P("fsdp", None),
            P("fsdp", None),
            P("fsdp"),
            P("fsdp", None),
            P("fsdp", None),
            P("fsdp", None),
        ),
        out_specs=(
            P(batch, None, None),
            P(batch, None, None),
            P("fsdp"),
            P("fsdp", None),
            P("fsdp", None),
            P("fsdp", None),
            P("fsdp", None),
            P("fsdp"),
            P("fsdp", None),
            P("fsdp", None),
            P("fsdp", None),
            P(),
        ),
        check_vma=False,
    )
```

time: 6820 us -> 1450 us (0.21)
  waiting for transfers between devices: 6110 us -> 802 us
  matrix products: 304 us -> 183 us
    reduce_scatter x7 -> x8, waiting for transfers between devices: 4820 us -> 442 us  [the longest x4 243 us: scatter_tokens(): lax.psum_scatter(partial, ('sub', 'fsdp'), scatter_dimension=0, tiled=True)]
    all_gather x12 -> x8, waiting for transfers between devices: 1280 us -> 233 us  [the longest x2 130 us: finish_columns(): spread = lax.all_gather(moved, ('rep', 'sub'), axis=0, tiled=False)]
    transpose x9 -> x0, local copies, waits for them, and re-layouts: 153 us -> none  [owner_blocks(): return jnp.swapaxes(blocked, 0, 1).reshape(term.shape)]
    dot_general x77 -> x17, matrix products: 304 us -> 177 us  [the longest x4 60.1 us: contract_cols(): return jnp.einsum('sb,ab->sa', left, right, preferred_element_type=F32)]
    all_to_all x0 -> x2, waiting for transfers between devices: none -> 126 us  [regroup_columns(): lax.all_to_all(blocks, 'fsdp', split_axis=0, concat_axis=0, tiled=True)]
    convert_element_type x2 -> x9, local copies, waits for them, and re-layouts: 2.6 us -> 119 us  [the longest x6 104 us: finish_columns(): part.reshape(rep * moved.shape[1], owners * subs * width).astype(F32)]
  transfers between devices with their start and end apart: 19 -> 18, of which waited for: 19 -> 15; matrix products, arithmetic and copies ran while one was open for 7% -> 20% of each run, Pallas kernels for 0% -> 0%
where the time goes in v1:
time: 1450 us
  waiting for transfers between devices  802 us (55%)
  local copies, waits for them, and re-layouts  220 us (15%)
  matrix products  183 us (13%)
  blocking collectives  125 us (9%)
  other arithmetic  87.6 us (6%)
  between operations  15.6 us (1%)
    reduce_scatter x4, waiting for transfers between devices, scatter_tokens(): lax.psum_scatter(partial, ('sub', 'fsdp'), scatter_dimension=0, tiled=True)  243 us
    reduce_scatter x2, waiting for transfers between devices, finish_columns(): piece = lax.psum_scatter(blocked, 'rep', scatter_dimension=0, tiled=True)  163 us
    all_gather x2, waiting for transfers between devices, finish_columns(): spread = lax.all_gather(moved, ('rep', 'sub'), axis=0, tiled=False)  130 us
    all_to_all x2, waiting for transfers between devices, regroup_columns(): lax.all_to_all(blocks, 'fsdp', split_axis=0, concat_axis=0, tiled=True)  126 us
    convert_element_type x6, local copies, waits for them, and re-layouts, finish_columns(): part.reshape(rep * moved.shape[1], owners * subs * width).astype(F32)  104 us
    dot_general x4, matrix products, contract_cols(): return jnp.einsum('sb,ab->sa', left, right, preferred_element_type=F32)  60.1 us
    all_gather x2, waiting for transfers between devices, finish_rows(): spread = lax.all_gather(piece, ('rep', 'sub'), axis=0, tiled=False)  59.4 us
    unnamed x101, local copies, waits for them, and re-layouts  51.2 us
  transfers between devices with their start and end apart: 18, of which 15 were waited for; matrix products, arithmetic and copies ran while one was open for 20% of the time, Pallas kernels for 0%

profile of v1, /device:TPU:0, one launch (start us, length us, event | category | flops | bytes accessed | tf_op | source)
XLA Modules:
  0.0 1445.7 jit_solution(5286320953307588363)
XLA Ops:
  30.6 29.1 %all-gather.4 = s32[8,1,256]{2,1,0:T(1,128)S(1)} all-gather(s32[1,1,256]{2,1,0:T(1,128)S(1)} %get-tuple-element.79), channel_id=1, replica_groups=mesh['rep'=4,'sub'=2,'fsdp'=4] {'sub','fsdp'}, dimensions={0}, use_global_device_ids=true | all-gather | bytes 9216 | tf_op jit(solution)/shard_map/all_gather | solution.py:68
  117.2 71.0 %reduce-scatter.9.cloned.1.call-done = bf16[256,2048]{1,0:T(8,128)(2,1)} async-done(((bf16[2048,2048]{1,0:T(8,128)(2,1)}), bf16[256,2048]{1,0:T(8,128)(2,1)}) %reduce-scatter.9.cloned.1.call-update) | async-done | bytes 1048592 | tf_op jit(solution)/shard_map/reduce_scatter | solution.py:72
  254.3 126.4 %all-to-all-done.1 = bf16[4,512,2048]{2,1,0:T(8,128)(2,1)} async-done(((bf16[4,512,2048]{2,1,0:T(8,128)(2,1)}), bf16[4,512,2048]{2,1,0:T(8,128)(2,1)}, u32[]{:S(2)}, u32[]{:S(2)}) %all-to-all-start.1) | async-done | bytes 8388640 | tf_op jit(solution)/shard_map/all_to_all | solution.py:84
  380.7 24.4 %fusion.103 = f32[2048,2048]{0,1:T(8,128)} fusion(bf16[2048,2048]{1,0:T(8,128)(2,1)} %all-gather.16.cloned.1.call-done, bf16[2048,2048]{1,0:T(8,128)(2,1)} %bitcast.37), kind=kOutput, calls=%fused_computation.179 | convolution fusion | flops 17179869184 | bytes 33554432 | tf_op jit(solution)/shard_map/dot_general | solution.py:43
  405.1 22.2 %multiply_convert_fusion.1 = (bf16[2048,1024]{0,1:T(8,128)(2,1)}, bf16[2048,1024]{0,1:T(8,128)(2,1)}, bf16[2048,1024]{0,1:T(8,128)(2,1)}) fusion(f32[2048,2048]{0,1:T(8,128)} %fusion.103, bf16[2048,2048]{1,0:T(8,128)(2,1)} %all-gather.18.cloned.1.call-done, bf16[2048,2048]{1,0:T(8,128)(2,1)} %param.25, s32[]{:T(128)S(6)} %select_n.43), kind=kOutput, calls=%fused_computation.20 | convolution fusion | flops 8621391872 | bytes 41943044 | tf_op jit(solution)/shard_map/sb,ab->sa/dot_general | solution.py:51
  427.3 23.9 %convolution_convert_fusion.2 = bf16[2048,2048]{1,0:T(8,128)(2,1)} fusion(bf16[2048,2048]{1,0:T(8,128)(2,1)} %bitcast.37, bf16[2048,1024]{0,1:T(8,128)(2,1)} %get-tuple-element.61, bf16[2048,1024]{0,1:T(8,128)(2,1)} %get-tuple-element.60), kind=kOutput, calls=%fused_computation.27 | convolution fusion | flops 17200840704 | bytes 25165824 | tf_op jit(solution)/shard_map/sb,ab->sa/dot_general | solution.py:51
  451.3 14.3 convolution_convert_fusion.3
  465.7 56.7 %reduce-scatter.13.cloned.1.call-done = bf16[256,2048]{1,0:T(8,128)(2,1)} async-done(((bf16[2048,2048]{1,0:T(8,128)(2,1)}), bf16[256,2048]{1,0:T(8,128)(2,1)}) %reduce-scatter.13.cloned.1.call-update) | async-done | bytes 1048592 | tf_op jit(solution)/shard_map/reduce_scatter | solution.py:72
  522.3 75.2 %reduce-scatter.11.cloned.1.call-done = bf16[256,2048]{1,0:T(8,128)(2,1)} async-done(((bf16[2048,2048]{1,0:T(8,128)(2,1)}), bf16[256,2048]{1,0:T(8,128)(2,1)}) %reduce-scatter.11.cloned.1.call-update) | async-done | bytes 1048592 | tf_op jit(solution)/shard_map/reduce_scatter | solution.py:72
  619.4 40.4 %all-gather.20.cloned.1.call-done = bf16[2048,2048]{1,0:T(8,128)(2,1)} async-done(((bf16[256,2048]{1,0:T(8,128)(2,1)}), bf16[2048,2048]{1,0:T(8,128)(2,1)}) %all-gather.20.cloned.1.call-update) | async-done | bytes 8388624 | tf_op jit(solution)/shard_map/all_gather | solution.py:68
  701.6 23.8 %convolution_convert_fusion = bf16[2048,2048]{1,0:T(8,128)(2,1)} fusion(bf16[2048,2048]{1,0:T(8,128)(2,1)} %all-gather.16.cloned.1.call-done, bf16[2048,1024]{0,1:T(8,128)(2,1)} %get-tuple-element.61, bf16[2048,1024]{0,1:T(8,128)(2,1)} %get-tuple-element.60), kind=kOutput, calls=%fused_computation.25 | convolution fusion | flops 17200840704 | bytes 25165824 | tf_op jit(solution)/shard_map/sa,sb->ab/dot_general | solution.py:47
  739.0 30.5 %reduce-scatter.19.cloned.1.call-done = bf16[64,2048]{1,0:T(8,128)(2,1)} async-done(((bf16[256,2048]{1,0:T(8,128)(2,1)}), bf16[64,2048]{1,0:T(8,128)(2,1)}) %reduce-scatter.19.cloned.1.call-update) | async-done | bytes 262160 | tf_op jit(solution)/shard_map/reduce_scatter | solution.py:94
  769.6 36.7 %reduce-scatter.17.cloned.1.call-done = bf16[512,384]{1,0:T(8,128)(2,1)} async-done(((bf16[2048,384]{1,0:T(8,128)(2,1)}), bf16[512,384]{1,0:T(8,128)(2,1)}) %reduce-scatter.17.cloned.1.call-update) | async-done | bytes 393232 | tf_op jit(solution)/shard_map/reduce_scatter | solution.py:106
  826.2 126.7 %reduce-scatter.21.cloned.1.call-done = bf16[512,2048]{1,0:T(8,128)(2,1)} async-done(((bf16[2048,2048]{1,0:T(8,128)(2,1)}), bf16[512,2048]{1,0:T(8,128)(2,1)}) %reduce-scatter.21.cloned.1.call-update) | async-done | bytes 2097168 | tf_op jit(solution)/shard_map/reduce_scatter | solution.py:106
  952.9 30.1 %all_to_all.21 = bf16[4,128,2048]{2,1,0:T(8,128)(2,1)} all-to-all(bf16[4,128,2048]{2,1,0:T(8,128)(2,1)} %bitcast.297), channel_id=1, replica_groups=mesh['rep'=4,'sub'=2,'fsdp'=4] {'fsdp'}, dimensions={0} | all-to-all | bytes 4194304 | tf_op jit(solution)/shard_map/all_to_all | solution.py:108
  983.7 53.6 %all-gather.28.cloned.1.call-done = bf16[2048,2048]{1,0:T(8,128)(2,1)} async-done(((bf16[256,2048]{1,0:T(8,128)(2,1)}), bf16[2048,2048]{1,0:T(8,128)(2,1)}) %all-gather.28.cloned.1.call-update) | async-done | bytes 8388624 | tf_op jit(solution)/shard_map/all_gather | solution.py:95
  1071.0 35.0 %all-gather.22.cloned.1.call-done = bf16[32,128,384]{2,1,0:T(8,128)(2,1)} async-done(((bf16[4,128,384]{2,1,0:T(8,128)(2,1)}), bf16[32,128,384]{2,1,0:T(8,128)(2,1)}) %all-gather.22.cloned.1.call-update) | async-done | bytes 3145744 | tf_op jit(solution)/shard_map/all_gather | solution.py:109
  1140.2 40.3 %reduce-scatter.15.cloned.1.call-done = bf16[256,2048]{1,0:T(8,128)(2,1)} async-done(((bf16[2048,2048]{1,0:T(8,128)(2,1)}), bf16[256,2048]{1,0:T(8,128)(2,1)}) %reduce-scatter.15.cloned.1.call-update) | async-done | bytes 1048592 | tf_op jit(solution)/shard_map/reduce_scatter | solution.py:72
  1186.4 45.6 %psum.7 = f32[4102]{0:T(1024)S(1)} all-reduce(f32[4102]{0:T(1024)S(1)} %concatenate.49), channel_id=1, replica_groups=mesh['rep'=4,'sub'=2,'fsdp'=4] {'rep','sub','fsdp'}, use_global_device_ids=true, to_apply=%region_20.21 | all-reduce | flops 4102 | bytes 32816 | tf_op jit(solution)/shard_map/psum | solution.py:245
  1238.6 95.4 %all-gather.26.cloned.1.call-done = bf16[32,128,2048]{2,1,0:T(8,128)(2,1)} async-done(((bf16[4,128,2048]{2,1,0:T(8,128)(2,1)}), bf16[32,128,2048]{2,1,0:T(8,128)(2,1)}) %all-gather.26.cloned.1.call-update) | async-done | bytes 16777232 | tf_op jit(solution)/shard_map/all_gather | solution.py:109
  1346.7 19.2 %copy.133 = f32[4,128,4,2,1024]{4,3,2,1,0:T(2,128)} copy(f32[4,128,4,2,1024]{4,1,2,3,0:T(8,128)S(1)} %get-tuple-element.62) | data formatting | bytes 33554432 | tf_op jit(solution)/shard_map/convert_element_type | solution.py:116
  1365.9 22.1 %reshape.322 = f32[512,8192]{1,0:T(8,128)} reshape(f32[4,128,4,2,1024]{4,3,2,1,0:T(2,128)} %copy.133) | data formatting | bytes 33554432 | tf_op jit(solution)/shard_map/convert_element_type | solution.py:116
  1388.0 28.7 %copy.132 = f32[4,128,4,2,1024]{4,3,2,1,0:T(2,128)} copy(f32[4,128,4,2,1024]{4,1,2,3,0:T(8,128)} %get-tuple-element.63) | data formatting | bytes 33554432 | tf_op jit(solution)/shard_map/convert_element_type | solution.py:116
  1416.7 22.3 %reshape.321 = f32[512,8192]{1,0:T(8,128)} reshape(f32[4,128,4,2,1024]{4,3,2,1,0:T(2,128)} %copy.132) | data formatting | bytes 33554432 | tf_op jit(solution)/shard_map/convert_element_type | solution.py:116
  (220 shorter events, 336.7 us)
Async XLA Ops:
  7.2 103.8 %copy-start = (bf16[512,2048]{1,0:T(8,128)(2,1)S(1)}, bf16[512,2048]{1,0:T(8,128)(2,1)}, u32[]{:S(2)}) copy-start(bf16[512,2048]{1,0:T(8,128)(2,1)} %param.21) | copy-start | bytes 6291460
  7.2 69.2 %all-gather.14.cloned.1.call-start = ((), (), s32[]{:S(2)}) async-start(), calls=%async_computation.12 | async-start | bytes 9437184 | tf_op jit(solution)/shard_map/all_gather | solution.py:68
  24.7 46.3 %all-to-all-start = ((bf16[4,512,384]{2,1,0:T(8,128)(2,1)}), bf16[4,512,384]{2,1,0:T(8,128)(2,1)}, u32[]{:S(2)}, u32[]{:S(2)}) async-start(bf16[4,512,384]{2,1,0:T(8,128)(2,1)} %pad_maximum_fusion.4), calls=%async_computation | async-start | bytes 3145728 | tf_op jit(solution)/shard_map/all_to_all | solution.py:84
  30.0 158.2 %reduce-scatter.9.cloned.1.call-start = ((), (), s32[]{:S(2)}) async-start(), calls=%async_computation.13 | async-start | bytes 9437184 | tf_op jit(solution)/shard_map/reduce_scatter | solution.py:72
  71.1 532.0 %copy-start.26 = (f32[1,2048]{1,0:T(1,128)}, f32[1,2048]{1,0:T(1,128)S(1)}, u32[]{:S(2)}) copy-start(f32[1,2048]{1,0:T(1,128)S(1)} %get-tuple-element.77) | copy-start | bytes 24580
  116.8 264.0 %all-gather.16.cloned.1.call-start = ((), (), s32[]{:S(2)}) async-start(), calls=%async_computation.14 | async-start | bytes 9437184 | tf_op jit(solution)/shard_map/all_gather | solution.py:68
  189.9 413.2 %copy-start.33 = (f32[256]{0:T(256)}, f32[256]{0:T(256)S(1)}, u32[]{:S(2)}) copy-start(f32[256]{0:T(256)S(1)} %add_rsqrt_fusion.2) | copy-start | bytes 3076
  192.6 212.5 %all-gather.18.cloned.1.call-start = ((), (), s32[]{:S(2)}) async-start(), calls=%async_computation.16 | async-start | bytes 9437184 | tf_op jit(solution)/shard_map/all_gather | solution.py:68
  248.6 132.1 %all-to-all-start.1 = ((bf16[4,512,2048]{2,1,0:T(8,128)(2,1)}), bf16[4,512,2048]{2,1,0:T(8,128)(2,1)}, u32[]{:S(2)}, u32[]{:S(2)}) async-start(bf16[4,512,2048]{2,1,0:T(8,128)(2,1)} %pad_maximum_fusion), calls=%async_computation.2 | async-start | bytes 16777216 | tf_op jit(solution)/shard_map/all_to_all | solution.py:84
  254.3 268.0 %reduce-scatter.13.cloned.1.call-start = ((), (), s32[]{:S(2)}) async-start(), calls=%async_computation.17 | async-start | bytes 9437184 | tf_op jit(solution)/shard_map/reduce_scatter | solution.py:72
  451.2 146.3 %reduce-scatter.11.cloned.1.call-start = ((), (), s32[]{:S(2)}) async-start(), calls=%async_computation.15 | async-start | bytes 9437184 | tf_op jit(solution)/shard_map/reduce_scatter | solution.py:72
  465.6 131.9 %copy-start.37 = (f32[1,256]{1,0:T(1,128)S(1)}, f32[1,256]{1,0:T(1,128)}, u32[]{:S(2)}) copy-start(f32[1,256]{1,0:T(1,128)} %get-tuple-element.78) | copy-start | bytes 3076
  465.6 194.2 %all-gather.20.cloned.1.call-start = ((), (), s32[]{:S(2)}) async-start(), calls=%async_computation.18 | async-start | bytes 9437184 | tf_op jit(solution)/shard_map/all_gather | solution.py:68
  605.3 133.7 %reduce-scatter.23.cloned.1.call-start = ((), (), s32[]{:S(2)}) async-start(), calls=%async_computation.23 | async-start | bytes 5242880 | tf_op jit(solution)/shard_map/reduce_scatter | solution.py:94
  619.4 150.2 %reduce-scatter.19.cloned.1.call-start = ((), (), s32[]{:S(2)}) async-start(), calls=%async_computation.21 | async-start | bytes 1310720 | tf_op jit(solution)/shard_map/reduce_scatter | solution.py:94
  685.2 121.1 %reduce-scatter.17.cloned.1.call-start = ((), (), s32[]{:S(2)}) async-start(), calls=%async_computation.20 | async-start | bytes 1966080 | tf_op jit(solution)/shard_map/reduce_scatter | solution.py:106
  701.4 251.5 %reduce-scatter.21.cloned.1.call-start = ((), (), s32[]{:S(2)}) async-start(), calls=%async_computation.22 | async-start | bytes 10485760 | tf_op jit(solution)/shard_map/reduce_scatter | solution.py:106
  733.9 303.3 %all-gather.28.cloned.1.call-start = ((), (), s32[]{:S(2)}) async-start(), calls=%async_computation.27 | async-start | bytes 9437184 | tf_op jit(solution)/shard_map/all_gather | solution.py:95
  739.0 327.6 %all-gather.24.cloned.1.call-start = ((), (), s32[]{:S(2)}) async-start(), calls=%async_computation.25 | async-start | bytes 2359296 | tf_op jit(solution)/shard_map/all_gather | solution.py:95
  769.6 336.4 %all-gather.22.cloned.1.call-start = ((), (), s32[]{:S(2)}) async-start(), calls=%async_computation.24 | async-start | bytes 3538944 | tf_op jit(solution)/shard_map/all_gather | solution.py:109
  817.8 362.7 %reduce-scatter.15.cloned.1.call-start = ((), (), s32[]{:S(2)}) async-start(), calls=%async_computation.19 | async-start | bytes 9437184 | tf_op jit(solution)/shard_map/reduce_scatter | solution.py:72
  826.1 156.9 %copy-start.42 = (s32[1,256]{1,0:T(1,128)S(1)}, s32[1,256]{1,0:T(1,128)}, u32[]{:S(2)}) copy-start(s32[1,256]{1,0:T(1,128)} %param.15) | copy-start | bytes 3076
  826.1 507.9 %all-gather.26.cloned.1.call-start = ((), (), s32[]{:S(2)}) async-start(), calls=%async_computation.26 | async-start | bytes 18874368 | tf_op jit(solution)/shard_map/all_gather | solution.py:109
  1131.4 103.1 %copy-start.5 = (bf16[256,2048]{1,0:T(8,128)(2,1)S(1)}, bf16[256,2048]{1,0:T(8,128)(2,1)}, u32[]{:S(2)}) copy-start(bf16[256,2048]{1,0:T(8,128)(2,1)} %reduce-scatter.9.cloned.1.call-done) | copy-start | bytes 3145732
  (39 other events, 840.2 us)
Sparse Core Ops, SparseCore 0:
  9.9 66.4 all-gather.13
  116.9 71.2 reduce-scatter.8
  192.7 54.3 all-gather.15
  249.6 129.3 all-gather.17
  451.4 70.9 reduce-scatter.12
  526.2 71.2 reduce-scatter.10
  605.4 54.3 all-gather.19
  662.2 76.7 reduce-scatter.22
  741.8 27.6 reduce-scatter.18
  772.4 33.9 reduce-scatter.16
  809.4 143.4 reduce-scatter.20
  954.4 82.7 all-gather.27
  1038.9 27.6 all-gather.23
  1068.2 37.7 all-gather.21
  1110.3 70.1 reduce-scatter.14
  1181.9 152.1 all-gather.25

commit v2 on v1

--- a/solution.py
+++ b/solution.py
@@ -1,6 +1,10 @@
+import functools
+
 import jax
 import jax.numpy as jnp
 from jax import lax
+from jax.experimental import pallas as pl
+from jax.experimental.pallas import tpu as pltpu
 from jax.sharding import Mesh
 from jax.sharding import PartitionSpec as P
 
@@ -17,6 +21,10 @@
 
 BF16 = jnp.bfloat16
 F32 = jnp.float32
+MESH = pl.DeviceIdType.MESH
+SCALE = 3_300_000
+HBM = pl.BlockSpec(memory_space=pltpu.HBM)
+VM = pl.BlockSpec(memory_space=pltpu.VMEM)
 
 
 def rope_tables(length, head_size):
@@ -64,12 +72,448 @@
     return (gain_grad, source_grad)
 
 
-def gather_tokens(block):
-    return lax.all_gather(block, ("sub", "fsdp"), axis=0, tiled=True)
-
-
-def scatter_tokens(partial):
-    return lax.psum_scatter(partial, ("sub", "fsdp"), scatter_dimension=0, tiled=True)
+def after(value, *others):
+    return lax.optimization_barrier((value,) + others)[0]
+
+
+def plane_position():
+    rep, core, own = lax.axis_index("rep"), lax.axis_index("sub"), lax.axis_index("fsdp")
+    row, col = own // 2, own % 2
+    across = row * 2 + (1 - col)
+    down = (1 - row) * 2 + col
+    corner = (1 - row) * 2 + (1 - col)
+    return rep, core, own, across, down, corner
+
+
+def meet(devices):
+    barrier = pltpu.get_barrier_semaphore()
+    for device in devices:
+        pl.semaphore_signal(barrier, inc=1, device_id=device, device_id_type=MESH)
+    pl.semaphore_wait(barrier, len(devices))
+
+
+def params(collective_id, megabytes=16):
+    return pltpu.CompilerParams(
+        collective_id=collective_id, has_side_effects=True, vmem_limit_bytes=megabytes << 20
+    )
+
+
+def link_cost(microseconds, flops=0):
+    return pl.CostEstimate(
+        flops=0, bytes_accessed=int(microseconds * SCALE), transcendentals=0
+    )
+
+
+class Sender:
+    def __init__(self, send_sems, recv_sems):
+        self.send_sems, self.recv_sems, self.copies = send_sems, recv_sems, []
+
+    def send(self, src, dst, device):
+        index = len(self.copies)
+        copy = pltpu.make_async_remote_copy(
+            src_ref=src,
+            dst_ref=dst,
+            send_sem=self.send_sems.at[index],
+            recv_sem=self.recv_sems.at[index],
+            device_id=device,
+            device_id_type=MESH,
+        )
+        copy.start()
+        self.copies.append(copy)
+        return copy
+
+    def finish(self):
+        for copy in self.copies:
+            copy.wait_send()
+
+
+class Gather:
+    def __init__(self, sender, x_ref, out_ref, local_sem, place):
+        self.sender, self.x_ref, self.out_ref, self.place = sender, x_ref, out_ref, place
+        rep, core, own, across, down, _ = place
+        self.to_across, self.to_down = (rep, core, across), (rep, core, down)
+        self.to_core = (rep, 1 - core, own)
+        half = x_ref.shape[0] // 2
+        self.low, self.high, self.whole = pl.ds(0, half), pl.ds(half, half), pl.ds(0, 2 * half)
+        self.base = core * 4
+        self.mine = pltpu.make_async_copy(x_ref, out_ref.at[self.base + own], local_sem)
+
+    def first(self, rows, device):
+        own = self.place[2]
+        return self.sender.send(
+            self.x_ref.at[rows], self.out_ref.at[self.base + own, rows], device
+        )
+
+    def forward(self, block, rows, device):
+        ref = self.out_ref.at[self.base + block, rows]
+        return self.sender.send(ref, ref, device)
+
+    def begin(self):
+        self.across_low = self.first(self.low, self.to_across)
+        self.down_high = self.first(self.high, self.to_down)
+        self.across_high = self.first(self.high, self.to_across)
+        self.down_low = self.first(self.low, self.to_down)
+        self.swaps = [self.first(self.whole, self.to_core)]
+        self.mine.start()
+
+    def relay(self):
+        _, _, _, across, down, _ = self.place
+        low, high, to_core = self.low, self.high, self.to_core
+        self.across_low.wait_recv()
+        self.corner_low = self.forward(across, low, self.to_down)
+        self.swaps.append(self.forward(across, low, to_core))
+        self.down_high.wait_recv()
+        self.corner_high = self.forward(down, high, self.to_across)
+        self.swaps.append(self.forward(down, high, to_core))
+        self.across_high.wait_recv()
+        self.swaps.append(self.forward(across, high, to_core))
+        self.down_low.wait_recv()
+        self.swaps.append(self.forward(down, low, to_core))
+
+    def finish(self):
+        corner = self.place[5]
+        self.corner_low.wait_recv()
+        self.swaps.append(self.forward(corner, self.low, self.to_core))
+        self.corner_high.wait_recv()
+        self.swaps.append(self.forward(corner, self.high, self.to_core))
+        for swap in self.swaps:
+            swap.wait_recv()
+        self.mine.wait()
+
+
+def gather_kernel(count, *refs):
+    xs, outs = refs[:count], refs[count : 2 * count]
+    local_sems, send_sems, recv_sems = refs[2 * count :]
+    place = plane_position()
+    rep, core, own, across, down, _ = place
+    meet([(rep, core, across), (rep, core, down), (rep, 1 - core, own)])
+    sender = Sender(send_sems, recv_sems)
+    moves = [
+        Gather(sender, x, out, local_sems.at[i], place) for i, (x, out) in enumerate(zip(xs, outs))
+    ]
+    for move in moves:
+        move.begin()
+    for move in moves:
+        move.relay()
+    for move in moves:
+        move.finish()
+    sender.finish()
+
+
+def gather_plane(blocks, collective_id):
+    count = len(blocks)
+    return pl.pallas_call(
+        functools.partial(gather_kernel, count),
+        out_shape=[jax.ShapeDtypeStruct((8,) + x.shape, x.dtype) for x in blocks],
+        in_specs=[HBM] * count,
+        out_specs=[HBM] * count,
+        scratch_shapes=[
+            pltpu.SemaphoreType.DMA((count,)),
+            pltpu.SemaphoreType.DMA((13 * count,)),
+            pltpu.SemaphoreType.DMA((13 * count,)),
+        ],
+        compiler_params=params(collective_id),
+        cost_estimate=link_cost(40 * count),
+    )(*blocks)
+
+
+def quarter_kernel(gate_ref, up_ref, out_ref, local_sems, send_sems, recv_sems):
+    rep, core, own, across, down, corner = plane_position()
+    peers = (corner, across, down)
+    meet([(rep, core, peer) for peer in peers])
+    rows = out_ref.shape[1]
+    width = out_ref.shape[2] // 2
+    mine = pl.ds(pl.multiple_of(rep * rows, rows), rows)
+
+    def source(ref, block):
+        columns = pl.ds(pl.multiple_of((block * 2 + core) * width, width), width)
+        return ref.at[mine, columns]
+
+    sender = Sender(send_sems, recv_sems)
+    for peer in peers:
+        for k, ref in enumerate((gate_ref, up_ref)):
+            target = out_ref.at[own, :, pl.ds(k * width, width)]
+            sender.send(source(ref, peer), target, (rep, core, peer))
+    local = []
+    for k, ref in enumerate((gate_ref, up_ref)):
+        copy = pltpu.make_async_copy(
+            source(ref, own), out_ref.at[own, :, pl.ds(k * width, width)], local_sems.at[k]
+        )
+        copy.start()
+        local.append(copy)
+    for copy in sender.copies:
+        copy.wait_recv()
+    sender.finish()
+    for copy in local:
+        copy.wait()
+
+
+def quarter_columns(w_gate, w_up, reps, collective_id):
+    rows, columns = w_gate.shape
+    return pl.pallas_call(
+        quarter_kernel,
+        out_shape=jax.ShapeDtypeStruct((4, rows // reps, columns // 4), BF16),
+        in_specs=[HBM, HBM],
+        out_specs=HBM,
+        scratch_shapes=[
+            pltpu.SemaphoreType.DMA((2,)),
+            pltpu.SemaphoreType.DMA((6,)),
+            pltpu.SemaphoreType.DMA((6,)),
+        ],
+        compiler_params=params(collective_id),
+        cost_estimate=link_cost(25),
+    )(w_gate, w_up)
+
+
+def start_kernel(
+    x_ref, code_ref, gain_ref, q_ref, k_ref, v_ref,
+    x_out, code_out, gain_out, q_out, k_out, v_out,
+    local_sems, send_sems, recv_sems,
+):
+    place = plane_position()
+    rep, core, own, across, down, corner = place
+    peers = (corner, across, down)
+    meet([(rep, core, peer) for peer in peers] + [(rep, 1 - core, peer) for peer in peers]
+         + [(rep, 1 - core, own)])
+    sender = Sender(send_sems, recv_sems)
+    direct, local = [], []
+
+    def keep(src, dst):
+        copy = pltpu.make_async_copy(src, dst, local_sems.at[1 + len(local)])
+        copy.start()
+        local.append(copy)
+
+    def columns(ref, block, width):
+        return ref.at[:, pl.ds(pl.multiple_of(block * width, width), width)]
+
+    def weights():
+        for peer in peers:
+            there = (rep, core, peer)
+            direct.append(sender.send(gain_ref, gain_out.at[own], there))
+            direct.append(sender.send(columns(q_ref, peer * 2 + core, 256), q_out.at[own], there))
+            direct.append(sender.send(columns(k_ref, peer, 128), k_out.at[own], there))
+            direct.append(sender.send(columns(v_ref, peer, 128), v_out.at[own], there))
+            direct.append(sender.send(code_ref, code_out.at[core * 4 + own], there))
+            other = (rep, 1 - core, peer)
+            direct.append(sender.send(code_ref, code_out.at[core * 4 + own], other))
+        direct.append(sender.send(code_ref, code_out.at[core * 4 + own], (rep, 1 - core, own)))
+        keep(gain_ref, gain_out.at[own])
+        keep(columns(q_ref, own * 2 + core, 256), q_out.at[own])
+        keep(columns(k_ref, own, 128), k_out.at[own])
+        keep(columns(v_ref, own, 128), v_out.at[own])
+        keep(code_ref, code_out.at[core * 4 + own])
+
+    move = Gather(sender, x_ref, x_out, local_sems.at[0], place)
+    move.begin()
+    weights()
+    move.relay()
+    move.finish()
+    for copy in direct:
+        copy.wait_recv()
+    sender.finish()
+    for copy in local:
+        copy.wait()
+
+
+def start_plane(hidden, codes, gains, w_query, w_key, w_value, collective_id):
+    rows = w_query.shape[0]
+    shapes = [
+        ((8,) + hidden.shape, BF16),
+        ((8,) + codes.shape, jnp.int32),
+        ((4,) + gains.shape, BF16),
+        ((4, rows, GROUPS * HD), BF16),
+        ((4, rows, 2 * HD), BF16),
+        ((4, rows, 2 * HD), BF16),
+    ]
+    return pl.pallas_call(
+        start_kernel,
+        out_shape=[jax.ShapeDtypeStruct(s, d) for s, d in shapes],
+        in_specs=[HBM] * 6,
+        out_specs=[HBM] * 6,
+        scratch_shapes=[
+            pltpu.SemaphoreType.DMA((6,)),
+            pltpu.SemaphoreType.DMA((32,)),
+            pltpu.SemaphoreType.DMA((32,)),
+        ],
+        compiler_params=params(collective_id),
+        cost_estimate=link_cost(60),
+    )(hidden, codes, gains, w_query, w_key, w_value)
+
+
+def product_scatter_kernel(turned, count, *refs):
+    x_hbm, w_hbm, out_ref = refs[:count], refs[count], refs[count + 1]
+    x_refs, w_ref = refs[count + 2 : 2 * count + 2], refs[2 * count + 2]
+    (
+        swap, held, from_core, from_across, from_down, last_across, last_down,
+        x_sems, w_sems, core_send, core_recv, send_sems, recv_sems,
+    ) = refs[2 * count + 3 :]
+    rep, core, own, across, down, corner = plane_position()
+    to_across, to_down, to_core = (rep, core, across), (rep, core, down), (rep, 1 - core, own)
+    _, rows, wide = held.shape
+    depth = x_refs[0].shape[1]
+    tile = 512
+    tiles = wide // tile
+    half = rows // 2
+    low, high = pl.ds(0, half), pl.ds(half, half)
+    order = []
+    for block in (corner, across, down, own):
+        order += [(1 - core) * 4 + block, core * 4 + block]
+
+    def rows_of(block):
+        return pl.ds(pl.multiple_of(block * rows, rows), rows)
+
+    x_loads = [
+        [
+            pltpu.make_async_copy(
+                x_hbm[i].at[rows_of(block)], x_refs[i].at[rows_of(block)], x_sems.at[i, n]
+            )
+            for i in range(count)
+        ]
+        for n, block in enumerate(order)
+    ]
+    w_loads = []
+    for t in range(tiles):
+        columns = pl.ds(t * tile, tile)
+        if turned:
+            src, dst = w_hbm.at[columns], w_ref.at[columns]
+        else:
+            kept = pl.ds(pl.multiple_of(core * depth, depth), depth)
+            src, dst = w_hbm.at[kept, columns], w_ref.at[:, columns]
+        w_loads.append(pltpu.make_async_copy(src, dst, w_sems.at[t]))
+    for load in x_loads[0]:
+        load.start()
+    for load in w_loads:
+        load.start()
+    for loads in x_loads[1:]:
+        for load in loads:
+            load.start()
+    meet([to_across, to_down, to_core])
+
+    def product(dst, mine, columns):
+        total = None
+        for i in range(count):
+            x = x_refs[i][mine, :]
+            if turned:
+                w = w_ref[columns, pl.ds(i * depth, depth)]
+                part = lax.dot_general(
+                    x, w, (((1,), (1,)), ((), ())), preferred_element_type=F32
+                )
+            else:
+                part = dot_f32(x, w_ref[:, columns])
+            total = part if total is None else total + part
+        dst[:, columns] = total.astype(BF16)
+
+    def fill(dst, n):
+        for load in x_loads[n]:
+            load.wait()
+        mine = rows_of(order[n])
+        if n == 0:
+            for t in range(tiles):
+                w_loads[t].wait()
+                product(dst, mine, pl.ds(t * tile, tile))
+        else:
+
+            @pl.loop(0, tiles)
+            def _(t):
+                product(dst, mine, pl.ds(pl.multiple_of(t * tile, tile), tile))
+
+    swaps = Sender(core_send, core_recv)
+    sender = Sender(send_sems, recv_sems)
+    sent = {}
+    for k in range(4):
+        fill(swap.at[k], 2 * k)
+        swaps.send(swap.at[k], from_core.at[k], to_core)
+        fill(held.at[k], 2 * k + 1)
+        swaps.copies[k].wait_recv()
+        held[k] = held[k] + from_core[k]
+        if k == 0:
+            sent[0] = sender.send(held.at[0, low], from_across.at[0], to_across)
+            sent[1] = sender.send(held.at[0, high], from_down.at[0], to_down)
+        if k == 1:
+            sent[2] = sender.send(held.at[1, low], from_across.at[1], to_across)
+        if k == 2:
+            sent[3] = sender.send(held.at[2, high], from_down.at[1], to_down)
+    sent[0].wait_recv()
+    held[2, low] = held[2, low] + from_across[0]
+    to_last = sender.send(held.at[2, low], last_down, to_down)
+    sent[1].wait_recv()
+    held[1, high] = held[1, high] + from_down[0]
+    across_last = sender.send(held.at[1, high], last_across, to_across)
+    sent[2].wait_recv()
+    sent[3].wait_recv()
+    to_last.wait_recv()
+    out_ref[low] = (
+        held[3, low].astype(F32) + from_across[1].astype(F32) + last_down[...].astype(F32)
+    )
+    across_last.wait_recv()
+    out_ref[high] = (
+        held[3, high].astype(F32) + from_down[1].astype(F32) + last_across[...].astype(F32)
+    )
+    swaps.finish()
+    sender.finish()
+
+
+def product_scatter(xs, w, turned, collective_id):
+    count = len(xs)
+    tokens, depth = xs[0].shape
+    rows = tokens // 8
+    wide = w.shape[0] if turned else w.shape[1]
+    half = rows // 2
+    return pl.pallas_call(
+        functools.partial(product_scatter_kernel, turned, count),
+        out_shape=jax.ShapeDtypeStruct((rows, wide), F32),
+        in_specs=[HBM] * (count + 1),
+        out_specs=VM,
+        scratch_shapes=[pltpu.VMEM((tokens, depth), BF16)] * count
+        + [
+            pltpu.VMEM((wide, depth * count) if turned else (depth, wide), BF16),
+            pltpu.VMEM((4, rows, wide), BF16),
+            pltpu.VMEM((4, rows, wide), BF16),
+            pltpu.VMEM((4, rows, wide), BF16),
+            pltpu.VMEM((2, half, wide), BF16),
+            pltpu.VMEM((2, half, wide), BF16),
+            pltpu.VMEM((half, wide), BF16),
+            pltpu.VMEM((half, wide), BF16),
+            pltpu.SemaphoreType.DMA((count, 8)),
+            pltpu.SemaphoreType.DMA((wide // 512,)),
+            pltpu.SemaphoreType.DMA((4,)),
+            pltpu.SemaphoreType.DMA((4,)),
+            pltpu.SemaphoreType.DMA((6,)),
+            pltpu.SemaphoreType.DMA((6,)),
+        ],
+        compiler_params=params(collective_id, 56),
+        cost_estimate=link_cost(44, 2 * tokens * depth * count * wide),
+    )(*xs, w)
+
+
+def cast_kernel(x_ref, out_ref):
+    out_ref[...] = x_ref[...].reshape(out_ref.shape).astype(F32)
+
+
+def cast_rows(spread):
+    reps, subs, rows, columns = spread.shape
+    return pl.pallas_call(
+        cast_kernel,
+        grid=(subs, reps),
+        out_shape=jax.ShapeDtypeStruct((reps * subs * rows, columns), F32),
+        in_specs=[pl.BlockSpec((1, 1, rows, columns), lambda s, r: (r, s, 0, 0))],
+        out_specs=pl.BlockSpec((rows, columns), lambda s, r: (s * reps + r, 0)),
+        cost_estimate=link_cost(8),
+    )(spread)
+
+
+def cast_columns(spread):
+    reps, subs, owners, rows, columns = spread.shape
+    return pl.pallas_call(
+        cast_kernel,
+        grid=(reps, owners, subs),
+        out_shape=jax.ShapeDtypeStruct((reps * rows, owners * subs * columns), F32),
+        in_specs=[
+            pl.BlockSpec((1, 1, 1, rows, columns), lambda r, j, s: (r, s, j, 0, 0)),
+        ],
+        out_specs=pl.BlockSpec((rows, columns), lambda r, j, s: (r, j * subs + s)),
+        cost_estimate=link_cost(8),
+    )(spread)
 
 
 def column_blocks(weight, owners, subs):
@@ -90,35 +534,44 @@
     return lax.dynamic_slice_in_dim(weight, lax.axis_index("sub") * rows, rows, axis=0)
 
 
-def finish_rows(term):
-    piece = lax.psum_scatter(term, "rep", scatter_dimension=0, tiled=True)
+def gather_tokens(block):
+    return lax.all_gather(block, ("sub", "fsdp"), axis=0, tiled=True)
+
+
+def scatter_tokens(partial):
+    return lax.psum_scatter(partial, ("sub", "fsdp"), scatter_dimension=0, tiled=True)
+
+
+def sum_planes(term):
+    return lax.psum_scatter(term, "rep", scatter_dimension=0, tiled=True)
+
+
+def spread_planes(piece):
+    rep, subs = lax.axis_size("rep"), lax.axis_size("sub")
     spread = lax.all_gather(piece, ("rep", "sub"), axis=0, tiled=False)
-    rep, subs = lax.axis_size("rep"), lax.axis_size("sub")
-    spread = spread.reshape((rep, subs) + piece.shape)
-    return jnp.swapaxes(spread, 0, 1).reshape(-1, piece.shape[-1]).astype(F32)
-
-
-def finish_columns(term, widths):
-    owners, rep, subs = lax.axis_size("fsdp"), lax.axis_size("rep"), lax.axis_size("sub")
+    return spread.reshape((rep, subs) + piece.shape)
+
+
+def owner_major(term):
+    owners, rep = lax.axis_size("fsdp"), lax.axis_size("rep")
     rows, columns = term.shape
     blocked = jnp.swapaxes(term.reshape(owners, rep, rows // (owners * rep), columns), 0, 1)
-    blocked = blocked.reshape(rows, columns)
-    piece = lax.psum_scatter(blocked, "rep", scatter_dimension=0, tiled=True)
-    piece = piece.reshape(owners, -1, columns)
-    moved = lax.all_to_all(piece, "fsdp", split_axis=0, concat_axis=0, tiled=True)
-    spread = lax.all_gather(moved, ("rep", "sub"), axis=0, tiled=False)
-    spread = spread.reshape((rep, subs) + moved.shape)
-    outs = []
-    at = 0
-    for width in widths:
-        part = lax.slice_in_dim(spread, at, at + width, axis=4)
-        part = jnp.transpose(part, (0, 3, 2, 1, 4))
-        outs.append(part.reshape(rep * moved.shape[1], owners * subs * width).astype(F32))
-        at += width
-    return outs
+    return blocked.reshape(rows, columns)
+
+
+def to_owners(piece):
+    blocked = piece.reshape(lax.axis_size("fsdp"), -1, piece.shape[1])
+    return lax.all_to_all(blocked, "fsdp", split_axis=0, concat_axis=0, tiled=True)
+
+
+def place_columns(spread):
+    reps, subs, owners, rows, columns = spread.shape
+    part = jnp.transpose(spread, (0, 3, 2, 1, 4))
+    return part.reshape(reps * rows, owners * subs * columns).astype(F32)
 
 
 def shards(
+    kernels,
     hidden_in,
     segment_ids,
     valid_mask,
@@ -133,26 +586,63 @@
     w_up,
     w_down,
 ):
-    owners, subs = lax.axis_size("fsdp"), lax.axis_size("sub")
+    owners, subs, reps = lax.axis_size("fsdp"), lax.axis_size("sub"), lax.axis_size("rep")
     members = owners * subs
     length, width = hidden_in.shape[1:]
     tokens = members * length
-
-    gains = lax.all_gather(jnp.stack([norm_attn, norm_mlp]), "fsdp", axis=1, tiled=True)
+    q_width, k_width = GROUPS * HD, HD
+
+    def gathered(blocks, collective_id):
+        if kernels:
+            outs = gather_plane(blocks, collective_id)
+        else:
+            outs = [gather_tokens(block) for block in blocks]
+        return [out.reshape(tokens, -1) for out in outs]
+
+    def scattered(xs, w, turned, collective_id):
+        if kernels:
+            return product_scatter(xs, w, turned, collective_id)
+        x = jnp.concatenate(xs, axis=1)
+        if turned:
+            return scatter_tokens(contract_cols(x, w).astype(BF16)).astype(F32)
+        return scatter_tokens(dot_f32(x, row_block(w, subs)).astype(BF16)).astype(F32)
+
+    codes = segment_ids * 2 + valid_mask
+    gains = jnp.stack([norm_attn, norm_mlp])
+    result_grad = cotangent[0].astype(F32)
+    mlp_out_low = (RESIDUAL_SCALE * result_grad).astype(BF16)
+    if kernels:
+        quarter = quarter_columns(w_gate, w_up, reps, 0)
+        hidden_tied = after(hidden_in[0], quarter)
+        hidden_low, codes, gains, q_cols, k_cols, v_cols = start_plane(
+            hidden_tied, codes, gains, w_query, w_key, w_value, 1
+        )
+        hidden_low = hidden_low.reshape(tokens, width)
+        codes = codes.reshape(members, length)
+        gains = jnp.swapaxes(gains, 0, 1).reshape(2, width)
+        core_at = lax.axis_index("sub") * HD
+        qkv = jnp.concatenate(
+            [
+                q_cols,
+                lax.dynamic_slice_in_dim(k_cols, core_at, HD, axis=2),
+                lax.dynamic_slice_in_dim(v_cols, core_at, HD, axis=2),
+            ],
+            axis=2,
+        ).reshape(width, q_width + 2 * k_width)
+        gate_up = lax.all_gather(quarter, "rep", axis=1, tiled=True).reshape(width, -1)
+    else:
+        gains = lax.all_gather(gains, "fsdp", axis=1, tiled=True)
+        codes = gather_tokens(codes)
+        hidden_low = gather_tokens(hidden_in[0])
+        qkv = regroup_columns((w_query, w_key, w_value), owners, subs)
+        gate_up = regroup_columns((w_gate, w_up), owners, subs)
     gain_attn = gains[0].astype(F32)
     gain_mlp = gains[1].astype(F32)
-    codes = gather_tokens(segment_ids * 2 + valid_mask)
-    hidden_low = gather_tokens(hidden_in).reshape(tokens, width)
-    qkv = regroup_columns((w_query, w_key, w_value), owners, subs)
-    out_rows = row_block(w_output, subs)
-    gate_up = regroup_columns((w_gate, w_up), owners, subs)
-    down_rows = row_block(w_down, subs)
-    ff = down_rows.shape[0]
+    ff = gate_up.shape[1] // 2
 
     hidden_all = hidden_low.astype(F32)
     normed_one = (hidden_all * row_scale(hidden_all) * gain_attn).astype(BF16)
     projected = dot_f32(normed_one, qkv)
-    q_width, k_width = GROUPS * HD, HD
     cos_table, sin_table = rope_tables(length, HD)
     cos_heads = cos_table[None, :, None, :]
     sin_heads = sin_table[None, :, None, :]
@@ -176,7 +666,7 @@
     probs_low = probs.astype(BF16)
     attended = jnp.einsum("sgtu,sud->stgd", probs_low, values, preferred_element_type=F32)
     attended = attended.reshape(tokens, q_width).astype(BF16)
-    attn_branch = scatter_tokens(dot_f32(attended, out_rows).astype(BF16)).astype(F32)
+    attn_branch = scattered([attended], w_output, False, 2)
 
     hidden = hidden_in[0].astype(F32)
     scale_one = row_scale(hidden)
@@ -184,31 +674,34 @@
     middle = hidden + RESIDUAL_SCALE * attn_branch
     scale_two = row_scale(middle)
     unit_two = middle * scale_two
-    normed_two = gather_tokens((unit_two * gain_mlp).astype(BF16))
+    normed_two, mlp_out_grad = gathered([(unit_two * gain_mlp).astype(BF16), mlp_out_low], 3)
     gate_up_proj = dot_f32(normed_two, gate_up)
     gate_proj, up_proj = gate_up_proj[:, :ff], gate_up_proj[:, ff:]
     sigma = jax.nn.sigmoid(gate_proj)
     silu_gate = gate_proj * sigma
     mixed_act = (silu_gate * up_proj).astype(BF16)
-    mlp_branch = scatter_tokens(dot_f32(mixed_act, down_rows).astype(BF16)).astype(F32)
-    result = middle + RESIDUAL_SCALE * mlp_branch
-
-    result_grad = cotangent[0].astype(F32)
-    mlp_out_grad = gather_tokens((RESIDUAL_SCALE * result_grad).astype(BF16))
-    mixed_grad = contract_cols(mlp_out_grad, down_rows)
+
     down_w_grad = contract_rows(mixed_act, mlp_out_grad).astype(BF16)
+    down_w_piece = sum_planes(down_w_grad)
+    mixed_grad = contract_cols(after(mlp_out_grad, down_w_grad), row_block(w_down, subs))
     slope = sigma * (1.0 + gate_proj * (1.0 - sigma))
     gate_grad = (mixed_grad * up_proj * slope).astype(BF16)
     up_grad = (mixed_grad * silu_gate).astype(BF16)
-    gate_up_grad = jnp.concatenate([gate_grad, up_grad], axis=1)
-    normed_two_grad = scatter_tokens(contract_cols(gate_up_grad, gate_up).astype(BF16)).astype(F32)
-    gate_up_w_grad = contract_rows(normed_two, gate_up_grad).astype(BF16)
+    gate_w_grad = owner_major(contract_rows(normed_two, gate_grad).astype(BF16))
+    up_w_grad = owner_major(contract_rows(normed_two, up_grad).astype(BF16))
+    gate_sum = sum_planes(gate_w_grad)
+    up_sum = sum_planes(up_w_grad)
+    gate_up_grad = [after(gate_grad, gate_w_grad, up_w_grad), up_grad]
+    normed_two_grad = scattered(gate_up_grad, gate_up, True, 4)
     gain_mlp_grad, middle_part = norm_backward(normed_two_grad, scale_two, unit_two, gain_mlp)
     middle_grad = result_grad + middle_part
 
-    attn_out_grad = gather_tokens((RESIDUAL_SCALE * middle_grad).astype(BF16))
-    attended_grad = contract_cols(attn_out_grad, out_rows).astype(BF16)
+    attn_out_low = after((RESIDUAL_SCALE * middle_grad).astype(BF16), down_w_piece)
+    (attn_out_grad,) = gathered([attn_out_low], 5)
+    attn_out_grad = after(attn_out_grad, gate_sum)
+    attended_grad = contract_cols(attn_out_grad, row_block(w_output, subs)).astype(BF16)
     output_w_grad = contract_rows(attended, attn_out_grad).astype(BF16)
+    output_w_piece = sum_planes(output_w_grad)
     heads_grad = attended_grad.reshape(members, length, GROUPS, HD)
     prob_grad = jnp.einsum("stgd,sud->sgtu", heads_grad, values, preferred_element_type=F32)
     row_dot = jnp.sum(probs * prob_grad, axis=-1, keepdims=True)
@@ -229,10 +722,17 @@
         axis=2,
     )
     qkv_grad = qkv_grad.reshape(tokens, q_width + 2 * k_width).astype(BF16)
-    normed_one_grad = scatter_tokens(contract_cols(qkv_grad, qkv).astype(BF16)).astype(F32)
-    qkv_w_grad = contract_rows(normed_one, qkv_grad).astype(BF16)
+    qkv_tied = after(qkv_grad, output_w_grad)
+    normed_one_grad = scattered([qkv_tied], qkv, True, 6)
+    qkv_w_grad = owner_major(contract_rows(normed_one, after(qkv_grad, normed_one_grad, up_sum)).astype(BF16))
+    qkv_sum = sum_planes(qkv_w_grad)
+    gate_piece, up_piece, qkv_piece = (to_owners(t) for t in (gate_sum, up_sum, qkv_sum))
     gain_attn_grad, hidden_part = norm_backward(normed_one_grad, scale_one, unit_one, gain_attn)
     input_grad = (middle_grad + hidden_part).astype(BF16)
+
+    mixed_tied = after(mixed_act, normed_one_grad, qkv_w_grad)
+    mlp_branch = scattered([mixed_tied], w_down, False, 7)
+    result = middle + RESIDUAL_SCALE * mlp_branch
 
     validity_own = valid_mask[0].astype(F32)[:, None]
     squares = [
@@ -249,10 +749,23 @@
     gain_mlp_out = lax.dynamic_slice_in_dim(tally, width + start, part)
     statistics = jnp.sqrt(tally[2 * width : 2 * width + 5] / (tally[2 * width + 5] * width))
 
-    down_out = finish_rows(down_w_grad)
-    gate_out, up_out = finish_columns(gate_up_w_grad, (ff, ff))
-    output_out = finish_rows(output_w_grad)
-    query_out, key_out, value_out = finish_columns(qkv_w_grad, (q_width, k_width, k_width))
+    down_spread = spread_planes(down_w_piece)
+    gate_spread = spread_planes(gate_piece)
+    up_spread = spread_planes(up_piece)
+    output_spread = spread_planes(output_w_piece)
+    qkv_spread = spread_planes(qkv_piece)
+    query_out = place_columns(qkv_spread[..., :q_width])
+    key_out = place_columns(qkv_spread[..., q_width : q_width + k_width])
+    value_out = place_columns(qkv_spread[..., q_width + k_width :])
+    if kernels:
+        down_out, output_out = cast_rows(down_spread), cast_rows(output_spread)
+        gate_out, up_out = cast_columns(gate_spread), cast_columns(up_spread)
+    else:
+        down_out, output_out = (
+            jnp.swapaxes(s, 0, 1).reshape(-1, width).astype(F32)
+            for s in (down_spread, output_spread)
+        )
+        gate_out, up_out = place_columns(gate_spread), place_columns(up_spread)
     return (
         result.astype(BF16)[None],
         input_grad[None],
@@ -273,10 +786,11 @@
     fsdp = mesh.shape["fsdp"]
     subs = max(1, KV // fsdp)
     rep = mesh.shape["dp"] // subs
+    kernels = fsdp == 4 and subs == 2
     plane_mesh = Mesh(mesh.devices.reshape(rep, subs, fsdp), ("rep", "sub", "fsdp"))
     batch = ("rep", "sub", "fsdp")
     return jax.shard_map(
-        shards,
+        functools.partial(shards, kernels),
         mesh=plane_mesh,
         in_specs=(
             P(batch, None, None),

time: 1450 us -> 972 us (0.67)
  waiting for transfers between devices: 802 us -> 154 us
  Pallas kernels: 0 us -> 438 us
  local copies, waits for them, and re-layouts: 220 us -> 89.1 us
  matrix products: 183 us -> 127 us
  other arithmetic: 87.6 us -> 48 us
  blocking collectives: 125 us -> 88.9 us
    pallas_call x0 -> x12, Pallas kernels: none -> 438 us  [the longest x4 178 us: product_scatter(): pl.pallas_call(functools.partial(product_scatter_kernel, turned, count),...]
    reduce_scatter x8 -> x5, waiting for transfers between devices: 442 us -> 54.4 us  [sum_planes(): return lax.psum_scatter(term, 'rep', scatter_dimension=0, tiled=True)]
    all_gather x8 -> x6, waiting for transfers between devices: 233 us -> 98.8 us  [the longest x5 98.8 us: spread_planes(): spread = lax.all_gather(piece, ('rep', 'sub'), axis=0, tiled=False)]
    all_to_all x2 -> x0, waiting for transfers between devices: 126 us -> none  [regroup_columns(): lax.all_to_all(blocks, 'fsdp', split_axis=0, concat_axis=0, tiled=True)]
    convert_element_type x8 -> x2, local copies, waits for them, and re-layouts: 118 us -> 11.7 us  [place_columns(): return part.reshape(reps * rows, owners * subs * columns).astype(F32)]
    all_gather x2 -> x0, blocking collectives: 37.9 us -> none  [the longest x1 29.1 us: gather_tokens(): return lax.all_gather(block, ('sub', 'fsdp'), axis=0, tiled=True)]
    dot_general x4 -> x2, matrix products: 60.1 us -> 28.3 us  [contract_cols(): return jnp.einsum('sb,ab->sa', left, right, preferred_element_type=F32)]
    convert_element_type x8 -> x7, other arithmetic: 39.6 us -> 8.4 us  [the longest x2 4.34 us: place_columns(): return part.reshape(reps * rows, owners * subs * columns).astype(F32)]
  transfers between devices with their start and end apart: 18 -> 11, of which waited for: 15 -> 4; matrix products, arithmetic and copies ran while one was open for 20% -> 20% of each run, Pallas kernels for 0% -> 41%
where the time goes in v2:
time: 972 us; the launch traced here: 961 us
  Pallas kernels  438 us (45%)
  waiting for transfers between devices  154 us (16%)
  matrix products  127 us (13%)
  local copies, waits for them, and re-layouts  89.1 us (9%)
  blocking collectives  88.9 us (9%)
  other arithmetic  48 us (5%)
  between operations  15.7 us (2%)
    pallas_call x4, Pallas kernels, product_scatter(): pl.pallas_call(functools.partial(product_scatter_kernel, turned, count),...  178 us
    pallas_call x2, Pallas kernels, gather_plane(): pl.pallas_call(functools.partial(gather_kernel, count), out_shape=[jax.Sh...  112 us
    all_gather x5, waiting for transfers between devices, spread_planes(): spread = lax.all_gather(piece, ('rep', 'sub'), axis=0, tiled=False)  98.8 us
    pallas_call x1, Pallas kernels, start_plane(): pl.pallas_call(start_kernel, out_shape=[jax.ShapeDtypeStruct(s, d) for s,...  63.2 us
    reduce_scatter x5, waiting for transfers between devices, sum_planes(): return lax.psum_scatter(term, 'rep', scatter_dimension=0, tiled=True)  54.4 us
    unnamed x117, local copies, waits for them, and re-layouts  52.5 us
    dot_general x5, matrix products, contract_rows(): return jnp.einsum('sa,sb->ab', left, right, preferred_element_type=F32)  48.9 us
    psum x1, blocking collectives, shards(): tally = lax.psum(tally, ('rep', 'sub', 'fsdp'))  45.2 us
  transfers between devices with their start and end apart: 11, of which 4 were waited for; matrix products, arithmetic and copies ran while one was open for 20% of the time, Pallas kernels for 41%

profile of v2, /device:TPU:0, one launch (start us, length us, event | category | flops | bytes accessed | tf_op | source)
XLA Modules:
  0.0 961.0 jit_solution(14819807446840447333)
XLA Ops:
  14.1 27.7 %shard_map.220 = bf16[4,128,2048]{2,1,0:T(8,128)(2,1)} custom-call(bf16[512,8192]{1,0:T(8,128)(2,1)S(1)} %copy-done.4, bf16[512,8192]{1,0:T(8,128)(2,1)S(1)} %copy-done.5), custom_call_target="tpu_custom_call" | custom-call | bytes 82500000 | tf_op jit(solution)/shard_map/pallas_call | solution.py:253
  45.5 63.2 %shard_map.221 = (bf16[8,256,2048]{2,1,0:T(8,128)(2,1)S(1)}, s32[8,1,256]{2,1,0:T(1,128)S(1)}, bf16[4,2,512]{2,1,0:T(2,128)(2,1)S(1)}, bf16[4,512,256]{2,1,0:T(8...) custom-call(bf16[256,2048]{1,0:T(8,128)(2,1)S(1)} %bitcast.232, ...), custom_call_target="tpu_custom_call" | custom-call | bytes 198000000 | tf_op jit(solution)/shard_map/pallas_call | solution.py:328
  146.3 42.2 %shard_map.222 = f32[256,2048]{1,0:T(8,128)} custom-call(bf16[2048,256]{1,0:T(8,128)(2,1)} %copy.96.refs_0_, bf16[512,2048]{1,0:T(8,128)(2,1)} %refs_1_.2), custom_call_target="tpu_custom_call" | custom-call | bytes 145200000 | tf_op jit(solution)/shard_map/pallas_call | solution.py:462
  191.1 72.8 %shard_map.223 = (bf16[8,256,2048]{2,1,0:T(8,128)(2,1)S(1)}, bf16[8,256,2048]{2,1,0:T(8,128)(2,1)S(1)}) custom-call(bf16[256,2048]{1,0:T(8,128)(2,1)S(1)} %multiply_convert_fusion.5.refs_0_, bf16[256,2048]{1,0:T(8,128)(2,1)S(1)} %fusion.22.refs_1_), custom_call_target="tpu_custom_call" | custom-call | bytes 264000000 | tf_op jit(solution)/shard_map/pallas_call | solution.py:205
  270.4 21.5 %fusion.86 = f32[2048,2048]{1,0:T(8,128)S(1)} fusion(bf16[2048,2048]{1,0:T(8,128)(2,1)} %bitcast.238, bf16[2048,2048]{1,0:T(8,128)(2,1)} %bitcast.250), kind=kOutput, calls=%fused_computation.155 | convolution fusion | flops 17179869184 | bytes 33554432 | tf_op jit(solution)/shard_map/dot_general | solution.py:51
  302.4 11.0 %convolution_convert_fusion = bf16[1024,2048]{1,0:T(8,128)(2,1)} fusion(bf16[2048,1024]{1,0:T(8,128)(2,1)S(1)} %multiply_convert_fusion.3.refs_0_, bf16[2048,2048]{1,0:T(8,128)(2,1)S(1)} %bitcast.242), kind=kOutput, calls=%fused_computation.28 | convolution fusion | flops 8592031744 | bytes 16777216 | tf_op jit(solution)/shard_map/sa,sb->ab/dot_general | solution.py:55
  313.5 22.3 %multiply_convert_fusion.1 = (bf16[2048,1024]{1,0:T(8,128)(2,1)}, bf16[2048,1024]{1,0:T(8,128)(2,1)S(1)}) fusion(f32[2048,2048]{1,0:T(8,128)} %copy-done.19, bf16[2048,2048]{1,0:T(8,128)(2,1)} %bitcast.241, bf16[2048,2048]{1,0:T(8,128)(2,1)} %refs_1_.3, s32[]{:T(128)S(6)} %select_n.45), kind=kOutput, calls=%fused_computation.13 | convolution fusion | flops 8617197568 | bytes 37748740 | tf_op jit(solution)/shard_map/sb,ab->sa/dot_general | solution.py:59
  335.8 13.0 %convolution_convert_fusion.2 = bf16[2048,1024]{1,0:T(8,128)(2,1)S(1)} fusion(bf16[2048,2048]{1,0:T(8,128)(2,1)} %bitcast.239, bf16[2048,1024]{1,0:T(8,128)(2,1)S(1)} %get-tuple-element.38.refs_0_), kind=kOutput, calls=%fused_computation.30 | convolution fusion | flops 8592031744 | bytes 16777216 | tf_op jit(solution)/shard_map/sa,sb->ab/dot_general | solution.py:55
  351.4 13.1 %convolution_convert_fusion.1 = bf16[2048,1024]{1,0:T(8,128)(2,1)S(1)} fusion(bf16[2048,2048]{1,0:T(8,128)(2,1)} %bitcast.240, bf16[2048,1024]{1,0:T(8,128)(2,1)} %get-tuple-element.96.refs_1_), kind=kOutput, calls=%fused_computation.29 | convolution fusion | flops 8592031744 | bytes 16777216 | tf_op jit(solution)/shard_map/sa,sb->ab/dot_general | solution.py:55
  376.3 48.7 %shard_map.224 = f32[256,2048]{1,0:T(8,128)} custom-call(bf16[2048,1024]{1,0:T(8,128)(2,1)} %copy-done.25, bf16[2048,1024]{1,0:T(8,128)(2,1)} %get-tuple-element.96.refs_1_, bf16[2048,2048]{1,0:T(8,128)(2,1)} %bitcast.251), custom_call_target="tpu_custom_call" | custom-call | bytes 145200000 | tf_op jit(solution)/shard_map/pallas_call | solution.py:462
  428.2 39.0 %shard_map.225 = bf16[8,256,2048]{2,1,0:T(8,128)(2,1)S(1)} custom-call(bf16[256,2048]{1,0:T(8,128)(2,1)S(1)} %multiply_convert_fusion.4.refs_0_), custom_call_target="tpu_custom_call" | custom-call | bytes 132000000 | tf_op jit(solution)/shard_map/pallas_call | solution.py:205
  509.4 43.3 %shard_map.226 = f32[256,2048]{1,0:T(8,128)} custom-call(bf16[2048,384]{1,0:T(8,128)(2,1)} %copy.106.refs_0_, bf16[2048,384]{1,0:T(8,128)(2,1)} %bitcast.246), custom_call_target="tpu_custom_call" | custom-call | bytes 145200000 | tf_op jit(solution)/shard_map/pallas_call | solution.py:462
  562.5 17.8 %reduce-scatter.14.cloned.1.call-done = bf16[64,2048]{1,0:T(8,128)(2,1)} async-done(((bf16[256,2048]{1,0:T(8,128)(2,1)}), bf16[64,2048]{1,0:T(8,128)(2,1)}) %reduce-scatter.14.cloned.1.call-update) | async-done | bytes 262160 | tf_op jit(solution)/shard_map/reduce_scatter | solution.py:546
  580.3 36.6 %reduce-scatter.12.cloned.1.call-done = bf16[512,384]{1,0:T(8,128)(2,1)} async-done(((bf16[2048,384]{1,0:T(8,128)(2,1)}), bf16[512,384]{1,0:T(8,128)(2,1)}) %reduce-scatter.12.cloned.1.call-update) | async-done | bytes 393232 | tf_op jit(solution)/shard_map/reduce_scatter | solution.py:546
  617.0 11.4 %all_to_all.15 = bf16[4,128,384]{2,1,0:T(8,128)(2,1)} all-to-all(bf16[4,128,384]{2,1,0:T(8,128)(2,1)} %bitcast.268), channel_id=1, replica_groups=mesh['rep'=4,'sub'=2,'fsdp'=4] {'fsdp'}, dimensions={0} | all-to-all | bytes 786432 | tf_op jit(solution)/shard_map/all_to_all | solution.py:564
  629.2 17.2 %all_to_all.16 = bf16[4,128,1024]{2,1,0:T(8,128)(2,1)} all-to-all(bf16[4,128,1024]{2,1,0:T(8,128)(2,1)} %bitcast.267), channel_id=1, replica_groups=mesh['rep'=4,'sub'=2,'fsdp'=4] {'fsdp'}, dimensions={0} | all-to-all | bytes 2097152 | tf_op jit(solution)/shard_map/all_to_all | solution.py:564
  646.5 15.1 %all_to_all.17 = bf16[4,128,1024]{2,1,0:T(8,128)(2,1)} all-to-all(bf16[4,128,1024]{2,1,0:T(8,128)(2,1)S(1)} %bitcast.266), channel_id=1, replica_groups=mesh['rep'=4,'sub'=2,'fsdp'=4] {'fsdp'}, dimensions={0} | all-to-all | bytes 2097152 | tf_op jit(solution)/shard_map/all_to_all | solution.py:564
  662.3 43.8 %shard_map.227 = f32[256,2048]{1,0:T(8,128)} custom-call(bf16[2048,1024]{1,0:T(8,128)(2,1)} %copy-done.18, bf16[2048,2048]{1,0:T(8,128)(2,1)} %refs_1_.3), custom_call_target="tpu_custom_call" | custom-call | bytes 145200000 | tf_op jit(solution)/shard_map/pallas_call | solution.py:462
  715.4 45.2 %psum.7 = f32[4102]{0:T(1024)S(1)} all-reduce(f32[4102]{0:T(1024)S(1)} %concatenate.41), channel_id=1, replica_groups=mesh['rep'=4,'sub'=2,'fsdp'=4] {'rep','sub','fsdp'}, use_global_device_ids=true, to_apply=%region_19.20 | all-reduce | flops 4102 | bytes 32816 | tf_op jit(solution)/shard_map/psum | solution.py:745
  804.1 10.4 %shard_map.231 = f32[2048,2048]{1,0:T(8,128)} custom-call(bf16[4,2,256,2048]{3,2,1,0:T(8,128)(2,1)} %bitcast.247), custom_call_target="tpu_custom_call" | custom-call | bytes 26400000 | tf_op jit(solution)/shard_map/pallas_call | solution.py:495
  814.4 37.2 %all-gather.20.cloned.1.call-done = bf16[32,128,1024]{2,1,0:T(8,128)(2,1)} async-done(((bf16[4,128,1024]{2,1,0:T(8,128)(2,1)}), bf16[32,128,1024]{2,1,0:T(8,128)(2,1)}) %all-gather.20.cloned.1.call-update) | async-done | bytes 8388624 | tf_op jit(solution)/shard_map/all_gather | solution.py:551
  851.7 20.6 %shard_map.230 = f32[512,8192]{1,0:T(8,128)} custom-call(bf16[4,2,4,128,1024]{4,3,2,1,0:T(8,128)(2,1)} %bitcast.248), custom_call_target="tpu_custom_call" | custom-call | bytes 26400000 | tf_op jit(solution)/shard_map/pallas_call | solution.py:507
  872.3 61.6 %all-gather.18.cloned.1.call-done = bf16[32,128,1024]{2,1,0:T(8,128)(2,1)} async-done(((bf16[4,128,1024]{2,1,0:T(8,128)(2,1)}), bf16[32,128,1024]{2,1,0:T(8,128)(2,1)}) %all-gather.18.cloned.1.call-update) | async-done | bytes 8388624 | tf_op jit(solution)/shard_map/all_gather | solution.py:551
  933.9 20.4 %shard_map.229 = f32[512,8192]{1,0:T(8,128)} custom-call(bf16[4,2,4,128,1024]{4,3,2,1,0:T(8,128)(2,1)} %bitcast.249), custom_call_target="tpu_custom_call" | custom-call | bytes 26400000 | tf_op jit(solution)/shard_map/pallas_call | solution.py:507
  (214 shorter events, 190.3 us)
Async XLA Ops:
  7.2 35.3 %copy-start.1 = (bf16[1,256,2048]{2,1,0:T(8,128)(2,1)S(1)}, bf16[1,256,2048]{2,1,0:T(8,128)(2,1)}, u32[]{:S(2)}) copy-start(bf16[1,256,2048]{2,1,0:T(8,128)(2,1)} %param.13) | copy-start | bytes 3145732
  7.2 263.2 %all-gather.12.cloned.1.call-start = ((), (), s32[]{:S(2)}) async-start(), calls=%async_computation.8 | async-start | bytes 10485760 | tf_op jit(solution)/shard_map/all_gather | solution.py:632
  14.1 27.8 %copy-start.47 = (bf16[512]{0:T(512)(128)(2,1)S(1)}, bf16[512]{0:T(512)(128)(2,1)}, u32[]{:S(2)}) copy-start(bf16[512]{0:T(512)(128)(2,1)} %param.17) | copy-start | bytes 3076
  14.1 27.8 %copy-start.48 = (bf16[512]{0:T(512)(128)(2,1)S(1)}, bf16[512]{0:T(512)(128)(2,1)}, u32[]{:S(2)}) copy-start(bf16[512]{0:T(512)(128)(2,1)} %param.22) | copy-start | bytes 3076
  14.1 27.9 %copy-start.49 = (s32[1,256]{1,0:T(1,128)S(1)}, s32[1,256]{1,0:T(1,128)}, u32[]{:S(2)}) copy-start(s32[1,256]{1,0:T(1,128)} %param.14) | copy-start | bytes 3076
  14.1 27.9 %copy-start.50 = (s32[1,256]{1,0:T(1,128)S(1)}, s32[1,256]{1,0:T(1,128)}, u32[]{:S(2)}) copy-start(s32[1,256]{1,0:T(1,128)} %param.15) | copy-start | bytes 3076
  41.8 386.4 %reduce-scatter.6.cloned.1.call-start = ((), (), s32[]{:S(2)}) async-start(), calls=%async_computation.9 | async-start | bytes 5242880 | tf_op jit(solution)/shard_map/reduce_scatter | solution.py:546
  291.9 8.4 copy-start.19
  291.9 10.5 %copy-start.14 = (bf16[8,256,2048]{2,1,0:T(8,128)(2,1)S(1)}, bf16[8,256,2048]{2,1,0:T(8,128)(2,1)}, u32[]{:S(2)}) copy-start(bf16[8,256,2048]{2,1,0:T(8,128)(2,1)} %copy-done.13) | copy-start | bytes 25165828
  313.4 157.2 %reduce-scatter.8.cloned.1.call-start = ((), (), s32[]{:S(2)}) async-start(), calls=%async_computation.10 | async-start | bytes 5242880 | tf_op jit(solution)/shard_map/reduce_scatter | solution.py:546
  335.8 13.1 %copy-start.25 = (bf16[2048,1024]{1,0:T(8,128)(2,1)}, bf16[2048,1024]{1,0:T(8,128)(2,1)S(1)}, u32[]{:S(2)}) copy-start(bf16[2048,1024]{1,0:T(8,128)(2,1)S(1)} %get-tuple-element.38.refs_0_) | copy-start | bytes 12582916
  351.3 201.4 %reduce-scatter.10.cloned.1.call-start = ((), (), s32[]{:S(2)}) async-start(), calls=%async_computation.11 | async-start | bytes 5242880 | tf_op jit(solution)/shard_map/reduce_scatter | solution.py:546
  367.0 213.3 %reduce-scatter.14.cloned.1.call-start = ((), (), s32[]{:S(2)}) async-start(), calls=%async_computation.13 | async-start | bytes 1310720 | tf_op jit(solution)/shard_map/reduce_scatter | solution.py:546
  499.1 117.9 %reduce-scatter.12.cloned.1.call-start = ((), (), s32[]{:S(2)}) async-start(), calls=%async_computation.12 | async-start | bytes 1966080 | tf_op jit(solution)/shard_map/reduce_scatter | solution.py:546
  562.4 84.0 %copy-start.31 = (bf16[512,1024]{1,0:T(8,128)(2,1)S(1)}, bf16[512,1024]{1,0:T(8,128)(2,1)}, u32[]{:S(2)}) copy-start(bf16[512,1024]{1,0:T(8,128)(2,1)} %reduce-scatter.8.cloned.1.call-done) | copy-start | bytes 3145732
  562.5 205.3 %all-gather.16.cloned.1.call-start = ((), (), s32[]{:S(2)}) async-start(), calls=%async_computation.15 | async-start | bytes 2359296 | tf_op jit(solution)/shard_map/all_gather | solution.py:551
  580.3 193.5 %all-gather.14.cloned.1.call-start = ((), (), s32[]{:S(2)}) async-start(), calls=%async_computation.14 | async-start | bytes 3538944 | tf_op jit(solution)/shard_map/all_gather | solution.py:551
  628.4 175.7 %all-gather.22.cloned.1.call-start = ((), (), s32[]{:S(2)}) async-start(), calls=%async_computation.18 | async-start | bytes 9437184 | tf_op jit(solution)/shard_map/all_gather | solution.py:551
  629.1 222.6 %all-gather.20.cloned.1.call-start = ((), (), s32[]{:S(2)}) async-start(), calls=%async_computation.17 | async-start | bytes 9437184 | tf_op jit(solution)/shard_map/all_gather | solution.py:551
  629.2 32.5 %copy-start.51 = (s32[1,256]{1,0:T(1,128)S(1)}, s32[1,256]{1,0:T(1,128)}, u32[]{:S(2)}) copy-start(s32[1,256]{1,0:T(1,128)} %param.15) | copy-start | bytes 3076
  646.4 287.5 %all-gather.18.cloned.1.call-start = ((), (), s32[]{:S(2)}) async-start(), calls=%async_computation.16 | async-start | bytes 9437184 | tf_op jit(solution)/shard_map/all_gather | solution.py:551
  662.3 43.8 %copy-start.2 = (bf16[1,256,2048]{2,1,0:T(8,128)(2,1)S(1)}, bf16[1,256,2048]{2,1,0:T(8,128)(2,1)}, u32[]{:S(2)}) copy-start(bf16[1,256,2048]{2,1,0:T(8,128)(2,1)} %param.13) | copy-start | bytes 3145732
  662.3 43.8 %copy-start.16 = (f32[256,2048]{1,0:T(8,128)S(1)}, f32[256,2048]{1,0:T(8,128)}, u32[]{:S(2)}) copy-start(f32[256,2048]{1,0:T(8,128)} %shard_map.222) | copy-start | bytes 6291460
  662.3 43.8 %copy-start.46 = (f32[1,256]{1,0:T(1,128)S(1)}, f32[1,256]{1,0:T(1,128)}, u32[]{:S(2)}) copy-start(f32[1,256]{1,0:T(1,128)} %get-tuple-element.113) | copy-start | bytes 3076
  (41 other events, 133.1 us)
Sparse Core Ops, SparseCore 0:
  41.9 149.8 all-gather.11
  313.5 77.0 reduce-scatter.5
  393.0 77.2 reduce-scatter.7
  472.5 77.2 reduce-scatter.9
  552.6 27.6 reduce-scatter.13
  583.0 33.9 reduce-scatter.11
  618.6 28.0 all-gather.15
  648.3 37.7 all-gather.13
  687.7 81.9 all-gather.21
  771.2 80.4 all-gather.19
  853.3 80.5 all-gather.17

commit v3 on v2

--- a/solution.py
+++ b/solution.py
@@ -181,40 +181,359 @@
         self.mine.wait()
 
 
-def gather_kernel(count, *refs):
-    xs, outs = refs[:count], refs[count : 2 * count]
-    local_sems, send_sems, recv_sems = refs[2 * count :]
+class ExchangeJob:
+    def __init__(self, source):
+        self.rows = source.shape[0] // 4
+        self.arrays = [source]
+        self.corner = True
+        self.outs = [jax.ShapeDtypeStruct((4, self.rows, source.shape[1]), BF16)]
+        self.scratch = [pltpu.SemaphoreType.DMA((3,))] * 2 + [pltpu.SemaphoreType.DMA]
+
+    def open(self, arrays, outs, scratch, place):
+        self.source, self.out = arrays[0], outs[0]
+        self.sems, self.keep_sem, self.place = scratch[:2], scratch[2], place
+
+    def part(self, block):
+        return self.source.at[pl.ds(pl.multiple_of(block * self.rows, 16), self.rows)]
+
+    def stage(self, n):
+        rep, core, own, across, down, corner = self.place
+        if n == 0:
+            self.sender = Sender(*self.sems)
+            for peer in (corner, across, down):
+                self.sender.send(self.part(peer), self.out.at[own], (rep, core, peer))
+            self.keep = pltpu.make_async_copy(self.part(own), self.out.at[own], self.keep_sem)
+            self.keep.start()
+        if n == 6:
+            for copy in self.sender.copies:
+                copy.wait()
+            self.keep.wait()
+
+
+def column_place(place, reps):
+    rep, core, own = place[:3]
+    up = (rep == 0, rep == reps - 1, (rep + 1, core, own), (rep - 1, core, own))
+    down = (rep == reps - 1, rep == 0, (rep - 1, core, own), (rep + 1, core, own))
+    return (up, down)
+
+
+def skewed(rep, reps, count, act, i):
+    for low in (True, False):
+        near = 0 if low else 1
+
+        @pl.when((rep * 2 < reps) == low)
+        def _(near=near):
+            if i < count:
+                act(near, i)
+            if i >= 1:
+                act(1 - near, i - 1)
+
+
+class SumJob:
+    def __init__(self, sources, blocks, cuts, reps, steps):
+        self.blocks, self.cuts, self.reps, self.steps = blocks, cuts, reps, steps
+        self.arrays = sources
+        self.corner = blocks > 1
+        rows = sources[0].shape[0]
+        self.span = rows // blocks
+        self.half = self.span // 2
+        self.size = self.half // cuts
+        self.widths = [source.shape[1] for source in sources]
+        wide = sum(self.widths)
+        self.outs = [jax.ShapeDtypeStruct((2, blocks, self.half, wide), BF16)]
+        self.count = blocks * cuts
+        sems = pltpu.SemaphoreType.DMA((2, self.count))
+        self.scratch = [
+            pltpu.VMEM((2, blocks, self.half, wide), BF16),
+            pltpu.VMEM((2, blocks, self.half, wide), BF16),
+            pltpu.SemaphoreType.DMA((2, blocks, len(sources))),
+        ] + [sems] * 5
+
+    def open(self, arrays, outs, scratch, place):
+        self.sources, self.fin = arrays, outs[0]
+        self.held, self.landed, self.load_sems = scratch[:3]
+        self.chain_sems, self.give_sems, self.keep_sems = scratch[3:5], scratch[5:7], scratch[7]
+        self.rep, self.core, self.own = place[:3]
+        self.ways = column_place(place, self.reps)
+        for k in range(self.blocks):
+            for way in range(2):
+                for load in self.loads(way, k):
+                    load.start()
+
+    def block(self, k):
+        return (self.own + k) % self.blocks
+
+    def loads(self, way, k):
+        copies = []
+        at = 0
+        for n, (source, width) in enumerate(zip(self.sources, self.widths)):
+            start = pl.multiple_of(self.block(k) * self.span + way * self.half, 16)
+            src = source.at[pl.ds(start, self.half)]
+            dst = self.held.at[way, k, :, pl.ds(at, width)]
+            copies.append(pltpu.make_async_copy(src, dst, self.load_sems.at[way, k, n]))
+            at += width
+        return copies
+
+    def rows(self, i):
+        return i // self.cuts, pl.ds(i % self.cuts * self.size, self.size)
+
+    def chain(self, way, i):
+        k, rows = self.rows(i)
+        return pltpu.make_async_remote_copy(
+            src_ref=self.held.at[way, k, rows],
+            dst_ref=self.landed.at[way, k, rows],
+            send_sem=self.chain_sems[0].at[way, i],
+            recv_sem=self.chain_sems[1].at[way, i],
+            device_id=self.ways[way][2],
+            device_id_type=MESH,
+        )
+
+    def give(self, way, i):
+        k, rows = self.rows(i)
+        return pltpu.make_async_remote_copy(
+            src_ref=self.held.at[way, k, rows],
+            dst_ref=self.fin.at[way, self.own, rows],
+            send_sem=self.give_sems[0].at[way, i],
+            recv_sem=self.give_sems[1].at[way, i],
+            device_id=(self.rep, self.core, self.block(k)),
+            device_id_type=MESH,
+        )
+
+    def keep(self, way, i):
+        k, rows = self.rows(i)
+        own = self.own if self.blocks > 1 else 0
+        src, dst = self.held.at[way, k, rows], self.fin.at[way, own, rows]
+        return pltpu.make_async_copy(src, dst, self.keep_sems.at[way, i])
+
+    def loaded(self, way, i):
+        if i % self.cuts == 0:
+            for load in self.loads(way, i // self.cuts):
+                load.wait()
+
+    def prime(self):
+        for way in range(2):
+
+            @pl.when(self.ways[way][0])
+            def _(way=way):
+                for i in range(self.count):
+                    self.loaded(way, i)
+                    self.chain(way, i).start()
+
+    def add(self, way, i):
+        first, last = self.ways[way][:2]
+        k, rows = self.rows(i)
+
+        @pl.when(jnp.logical_not(first))
+        def _():
+            self.loaded(way, i)
+            self.chain(way, i).wait_recv()
+            self.held[way, k, rows] = self.held[way, k, rows] + self.landed[way, k, rows]
+
+            @pl.when(jnp.logical_not(last))
+            def _():
+                self.chain(way, i).start()
+
+            @pl.when(last)
+            def _():
+                if k == 0:
+                    self.keep(way, i).start()
+                else:
+                    self.give(way, i).start()
+
+    def step(self, i):
+        skewed(self.rep, self.reps, self.count, self.add, i)
+
+    def stage(self, n):
+        if n == 1:
+            self.prime()
+        if n in self.steps:
+            for i in self.steps[n]:
+                self.step(i)
+        if n == 7:
+            for way in range(2):
+                last = self.ways[way][1]
+                for i in range(self.count):
+
+                    @pl.when(jnp.logical_not(last))
+                    def _(way=way, i=i):
+                        self.chain(way, i).wait_send()
+
+                    @pl.when(last)
+                    def _(way=way, i=i):
+                        if i // self.cuts == 0:
+                            self.keep(way, i).wait()
+                        else:
+                            self.give(way, i).wait()
+
+
+class HandJob:
+    def __init__(self, source, reps):
+        self.inner = isinstance(source, SumJob)
+        self.sums = source if self.inner else None
+        shape = source.outs[0].shape if self.inner else source.shape
+        self.arrays = [] if self.inner else [source]
+        self.reps, self.blocks = reps, shape[1]
+        self.corner = False
+        self.outs = [jax.ShapeDtypeStruct((2, 2) + shape[1:], BF16)]
+        self.scratch = [pltpu.SemaphoreType.DMA((2, self.blocks))] * 5
+
+    def open(self, arrays, outs, scratch, place):
+        self.fin = None if self.inner else arrays[0]
+        self.out = outs[0]
+        self.hand_sems, self.side_sems, self.keep_sems = scratch[:2], scratch[2:4], scratch[4]
+        self.rep, self.core, self.own = place[:3]
+        self.ways = column_place(place, self.reps)
+
+    def remote(self, src, way, j, sems, device):
+        return pltpu.make_async_remote_copy(
+            src_ref=src,
+            dst_ref=self.out.at[way, self.core, j],
+            send_sem=sems[0].at[way, j],
+            recv_sem=sems[1].at[way, j],
+            device_id=device,
+            device_id_type=MESH,
+        )
+
+    def beside(self):
+        return (self.rep, 1 - self.core, self.own)
+
+    def begin(self):
+        fin = self.sums.fin if self.inner else self.fin
+        for j in range(self.blocks):
+            for way in range(2):
+
+                @pl.when(self.ways[way][1])
+                def _(way=way, j=j):
+                    src = fin.at[way, j]
+                    self.remote(src, way, j, self.hand_sems, self.ways[way][3]).start()
+                    self.remote(src, way, j, self.side_sems, self.beside()).start()
+                    dst = self.out.at[way, self.core, j]
+                    pltpu.make_async_copy(src, dst, self.keep_sems.at[way, j]).start()
+
+    def hand(self, way, j):
+        first, last = self.ways[way][:2]
+
+        @pl.when(jnp.logical_not(last))
+        def _():
+            ref = self.out.at[way, self.core, j]
+            hand = self.remote(ref, way, j, self.hand_sems, self.ways[way][3])
+            hand.wait_recv()
+
+            @pl.when(jnp.logical_not(first))
+            def _():
+                hand.start()
+
+            self.remote(ref, way, j, self.side_sems, self.beside()).start()
+
+    def pass_on(self):
+        for j in range(self.blocks + 1):
+            skewed(self.rep, self.reps, self.blocks, lambda w, i: self.hand(1 - w, i), j)
+
+    def close(self):
+        for j in range(self.blocks):
+            for way in range(2):
+                first, last = self.ways[way][:2]
+                ref = self.out.at[way, self.core, j]
+                self.remote(ref, way, j, self.side_sems, self.beside()).wait()
+
+                @pl.when(jnp.logical_not(first))
+                def _(way=way, j=j, ref=ref):
+                    self.remote(ref, way, j, self.hand_sems, self.ways[way][3]).wait_send()
+
+                @pl.when(last)
+                def _(way=way, j=j, ref=ref):
+                    pltpu.make_async_copy(ref, ref, self.keep_sems.at[way, j]).wait()
+
+    def stage(self, n):
+        if n == (7 if self.inner else 0):
+            self.begin()
+        if n == (8 if self.inner else 6):
+            self.pass_on()
+        if n == 9:
+            self.close()
+
+
+class Jobs:
+    def __init__(self, jobs, reps):
+        self.jobs, self.reps = jobs, reps
+        self.arrays = [a for job in jobs for a in job.arrays]
+        self.out_shapes = [o for job in jobs for o in job.outs]
+        self.scratch = [x for job in jobs for x in job.scratch]
+
+    def greet(self, place):
+        rep, core, own, across, down, corner = place
+        devices = [(rep, core, across), (rep, core, down), (rep, 1 - core, own)]
+        if self.jobs:
+            devices += [((rep + 1) % self.reps, core, own)]
+            devices += [((rep + self.reps - 1) % self.reps, core, own)]
+        if any(job.corner for job in self.jobs):
+            devices.append((rep, core, corner))
+        meet(devices)
+
+    def open(self, arrays, outs, scratch, place):
+        arrays, outs, scratch = list(arrays), list(outs), list(scratch)
+
+        def take(refs, count):
+            taken = refs[:count]
+            del refs[:count]
+            return taken
+
+        for job in self.jobs:
+            mine = [take(arrays, len(job.arrays)), take(outs, len(job.outs))]
+            job.open(*mine, take(scratch, len(job.scratch)), place)
+
+    def stage(self, n):
+        for job in self.jobs:
+            job.stage(n)
+
+
+def gather_kernel(count, jobs, *refs):
+    arrays, outs = len(jobs.arrays), len(jobs.out_shapes)
+    xs, job_arrays = refs[:count], refs[count : count + arrays]
+    refs = refs[count + arrays :]
+    x_outs, job_outs = refs[:count], refs[count : count + outs]
+    refs = refs[count + outs :]
+    local_sems, send_sems, recv_sems = refs[:3]
     place = plane_position()
-    rep, core, own, across, down, _ = place
-    meet([(rep, core, across), (rep, core, down), (rep, 1 - core, own)])
+    jobs.greet(place)
     sender = Sender(send_sems, recv_sems)
     moves = [
-        Gather(sender, x, out, local_sems.at[i], place) for i, (x, out) in enumerate(zip(xs, outs))
+        Gather(sender, x, out, local_sems.at[i], place)
+        for i, (x, out) in enumerate(zip(xs, x_outs))
     ]
     for move in moves:
         move.begin()
+    jobs.open(job_arrays, job_outs, refs[3:], place)
+    jobs.stage(0)
+    jobs.stage(1)
     for move in moves:
         move.relay()
+    jobs.stage(5)
     for move in moves:
         move.finish()
     sender.finish()
-
-
-def gather_plane(blocks, collective_id):
+    for n in (6, 7, 8, 9):
+        jobs.stage(n)
+
+
+def gather_plane(blocks, collective_id, jobs=(), reps=1):
     count = len(blocks)
+    jobs = Jobs(jobs, reps)
     return pl.pallas_call(
-        functools.partial(gather_kernel, count),
-        out_shape=[jax.ShapeDtypeStruct((8,) + x.shape, x.dtype) for x in blocks],
-        in_specs=[HBM] * count,
-        out_specs=[HBM] * count,
+        functools.partial(gather_kernel, count, jobs),
+        out_shape=[jax.ShapeDtypeStruct((8,) + x.shape, x.dtype) for x in blocks]
+        + jobs.out_shapes,
+        in_specs=[HBM] * (count + len(jobs.arrays)),
+        out_specs=[HBM] * (count + len(jobs.out_shapes)),
         scratch_shapes=[
             pltpu.SemaphoreType.DMA((count,)),
             pltpu.SemaphoreType.DMA((13 * count,)),
             pltpu.SemaphoreType.DMA((13 * count,)),
-        ],
-        compiler_params=params(collective_id),
+        ]
+        + jobs.scratch,
+        compiler_params=params(collective_id, 60),
         cost_estimate=link_cost(40 * count),
-    )(*blocks)
+    )(*blocks, *jobs.arrays)
 
 
 def quarter_kernel(gate_ref, up_ref, out_ref, local_sems, send_sems, recv_sems):
@@ -260,7 +579,7 @@
             pltpu.SemaphoreType.DMA((6,)),
             pltpu.SemaphoreType.DMA((6,)),
         ],
-        compiler_params=params(collective_id),
+        compiler_params=params(collective_id, 60),
         cost_estimate=link_cost(25),
     )(w_gate, w_up)
 
@@ -335,19 +654,24 @@
             pltpu.SemaphoreType.DMA((32,)),
             pltpu.SemaphoreType.DMA((32,)),
         ],
-        compiler_params=params(collective_id),
+        compiler_params=params(collective_id, 60),
         cost_estimate=link_cost(60),
     )(hidden, codes, gains, w_query, w_key, w_value)
 
 
-def product_scatter_kernel(turned, count, *refs):
-    x_hbm, w_hbm, out_ref = refs[:count], refs[count], refs[count + 1]
-    x_refs, w_ref = refs[count + 2 : 2 * count + 2], refs[2 * count + 2]
+def product_scatter_kernel(turned, count, jobs, *refs):
+    arrays, outs = len(jobs.arrays), len(jobs.out_shapes)
+    x_hbm, w_hbm, job_arrays = refs[:count], refs[count], refs[count + 1 : count + 1 + arrays]
+    refs = refs[count + 1 + arrays :]
+    out_ref, job_outs = refs[0], refs[1 : 1 + outs]
+    refs = refs[1 + outs :]
+    x_refs, w_ref = refs[:count], refs[count]
     (
         swap, held, from_core, from_across, from_down, last_across, last_down,
         x_sems, w_sems, core_send, core_recv, send_sems, recv_sems,
-    ) = refs[2 * count + 3 :]
-    rep, core, own, across, down, corner = plane_position()
+    ) = refs[count + 1 : count + 14]
+    place = plane_position()
+    rep, core, own, across, down, corner = place
     to_across, to_down, to_core = (rep, core, across), (rep, core, down), (rep, 1 - core, own)
     _, rows, wide = held.shape
     depth = x_refs[0].shape[1]
@@ -387,7 +711,9 @@
     for loads in x_loads[1:]:
         for load in loads:
             load.start()
-    meet([to_across, to_down, to_core])
+    jobs.open(job_arrays, job_outs, refs[count + 14 :], place)
+    jobs.greet(place)
+    jobs.stage(0)
 
     def product(dst, mine, columns):
         total = None
@@ -433,12 +759,14 @@
             sent[2] = sender.send(held.at[1, low], from_across.at[1], to_across)
         if k == 2:
             sent[3] = sender.send(held.at[2, high], from_down.at[1], to_down)
+        jobs.stage(1 + k)
     sent[0].wait_recv()
     held[2, low] = held[2, low] + from_across[0]
     to_last = sender.send(held.at[2, low], last_down, to_down)
     sent[1].wait_recv()
     held[1, high] = held[1, high] + from_down[0]
     across_last = sender.send(held.at[1, high], last_across, to_across)
+    jobs.stage(5)
     sent[2].wait_recv()
     sent[3].wait_recv()
     to_last.wait_recv()
@@ -451,19 +779,22 @@
     )
     swaps.finish()
     sender.finish()
-
-
-def product_scatter(xs, w, turned, collective_id):
+    for n in (6, 7, 8, 9):
+        jobs.stage(n)
+
+
+def product_scatter(xs, w, turned, collective_id, jobs=(), reps=1):
     count = len(xs)
+    jobs = Jobs(jobs, reps)
     tokens, depth = xs[0].shape
     rows = tokens // 8
     wide = w.shape[0] if turned else w.shape[1]
     half = rows // 2
     return pl.pallas_call(
-        functools.partial(product_scatter_kernel, turned, count),
-        out_shape=jax.ShapeDtypeStruct((rows, wide), F32),
-        in_specs=[HBM] * (count + 1),
-        out_specs=VM,
+        functools.partial(product_scatter_kernel, turned, count, jobs),
+        out_shape=[jax.ShapeDtypeStruct((rows, wide), F32)] + jobs.out_shapes,
+        in_specs=[HBM] * (count + 1 + len(jobs.arrays)),
+        out_specs=[VM] + [HBM] * len(jobs.out_shapes),
         scratch_shapes=[pltpu.VMEM((tokens, depth), BF16)] * count
         + [
             pltpu.VMEM((wide, depth * count) if turned else (depth, wide), BF16),
@@ -480,20 +811,21 @@
             pltpu.SemaphoreType.DMA((4,)),
             pltpu.SemaphoreType.DMA((6,)),
             pltpu.SemaphoreType.DMA((6,)),
-        ],
-        compiler_params=params(collective_id, 56),
+        ]
+        + jobs.scratch,
+        compiler_params=params(collective_id, 60),
         cost_estimate=link_cost(44, 2 * tokens * depth * count * wide),
-    )(*xs, w)
-
-
-def cast_kernel(x_ref, out_ref):
-    out_ref[...] = x_ref[...].reshape(out_ref.shape).astype(F32)
+    )(*xs, w, *jobs.arrays)
+
+
+def cast_rows_kernel(x_ref, out_ref):
+    out_ref[...] = x_ref[0, 0].astype(F32)
 
 
 def cast_rows(spread):
     reps, subs, rows, columns = spread.shape
     return pl.pallas_call(
-        cast_kernel,
+        cast_rows_kernel,
         grid=(subs, reps),
         out_shape=jax.ShapeDtypeStruct((reps * subs * rows, columns), F32),
         in_specs=[pl.BlockSpec((1, 1, rows, columns), lambda s, r: (r, s, 0, 0))],
@@ -502,18 +834,117 @@
     )(spread)
 
 
-def cast_columns(spread):
-    reps, subs, owners, rows, columns = spread.shape
+def cast_columns_kernel(x_ref, out_ref):
+    _, subs, owners, _, columns = x_ref.shape
+    for j in range(owners):
+        for s in range(subs):
+            at = (j * subs + s) * columns
+            out_ref[:, at : at + columns] = x_ref[0, s, j].astype(F32)
+
+
+def cast_columns(handed, columns):
+    parts, subs, owners, rows, _ = handed.shape
+    wide = owners * subs * columns
+    cuts = 4
+    block = (1, subs, owners, rows // cuts, columns)
     return pl.pallas_call(
-        cast_kernel,
-        grid=(reps, owners, subs),
-        out_shape=jax.ShapeDtypeStruct((reps * rows, owners * subs * columns), F32),
-        in_specs=[
-            pl.BlockSpec((1, 1, 1, rows, columns), lambda r, j, s: (r, s, j, 0, 0)),
+        cast_columns_kernel,
+        grid=(parts, cuts),
+        out_shape=jax.ShapeDtypeStruct((parts * rows, wide), F32),
+        in_specs=[pl.BlockSpec(block, lambda r, h: (r, 0, 0, h, 0))],
+        out_specs=pl.BlockSpec((rows // cuts, wide), lambda r, h: (r * cuts + h, 0)),
+        cost_estimate=link_cost(8),
+    )(handed)
+
+
+def cast_heads_kernel(q_ref, kv_ref, q_out, k_out, v_out):
+    _, subs, owners, _, columns = q_ref.shape
+    for j in range(owners):
+        for s in range(subs):
+            at = (j * subs + s) * columns
+            q_out[:, at : at + columns] = q_ref[0, s, j].astype(F32)
+        pair = [kv_ref[0, s, j].astype(F32) for s in range(subs)]
+        wide = HD * subs
+        at = j * wide
+        k_out[:, at : at + wide] = jnp.concatenate([p[:, :HD] for p in pair], axis=1)
+        v_out[:, at : at + wide] = jnp.concatenate([p[:, HD:] for p in pair], axis=1)
+
+
+def cast_heads(handed, skip):
+    parts, subs, owners, rows, _ = handed.shape
+    q_wide, k_wide = GROUPS * HD, 2 * HD
+    members = owners * subs
+
+    def source(wide, at):
+        return pl.BlockSpec((1, subs, owners, rows, wide), lambda r: (r, 0, 0, 0, at // wide))
+
+    def shape(wide):
+        return jax.ShapeDtypeStruct((parts * rows, wide), F32)
+
+    widths = (members * q_wide, members * HD, members * HD)
+    return pl.pallas_call(
+        cast_heads_kernel,
+        grid=(parts,),
+        out_shape=[shape(w) for w in widths],
+        in_specs=[source(q_wide, skip), source(k_wide, skip + q_wide)],
+        out_specs=[pl.BlockSpec((rows, w), lambda r: (r, 0)) for w in widths],
+        compiler_params=pltpu.CompilerParams(vmem_limit_bytes=48 << 20),
+        cost_estimate=link_cost(5),
+    )(handed, handed)
+
+
+def tally_kernel(x_ref, out_ref, plane, planes, total, sems, plane_sems):
+    rep, core, own, _, _, _ = plane_position()
+    reps = planes.shape[0]
+    mates = [(c, j) for c in range(2) for j in range(4)][1:]
+    others = [(rep, (core + c) % 2, (own + j) % 4) for c, j in mates]
+    above = [((rep + r) % reps, core, own) for r in range(1, reps)]
+    meet(others + above)
+    sender = Sender(sems.at[0], sems.at[1])
+    for device in others:
+        sender.send(x_ref, plane.at[core * 4 + own], device)
+    plane[core * 4 + own] = x_ref[...]
+    for copy in sender.copies:
+        copy.wait_recv()
+    mine = plane[0]
+    for k in range(1, 8):
+        mine = mine + plane[k]
+    total[...] = mine
+    climber = Sender(plane_sems.at[0], plane_sems.at[1])
+    for device in above:
+        climber.send(total, planes.at[rep], device)
+    planes[rep] = mine
+    for copy in climber.copies:
+        copy.wait_recv()
+    whole = planes[0]
+    for k in range(1, reps):
+        whole = whole + planes[k]
+    out_ref[...] = whole
+    sender.finish()
+    climber.finish()
+
+
+def tally_all(values, reps, collective_id):
+    size = values.shape[0]
+    rows = -(-size // 1024) * 8
+    padded = jnp.pad(values, (0, rows * 128 - size)).reshape(rows, 128)
+    block = pltpu.VMEM((rows, 128), F32)
+    summed = pl.pallas_call(
+        tally_kernel,
+        out_shape=jax.ShapeDtypeStruct((rows, 128), F32),
+        in_specs=[VM],
+        out_specs=VM,
+        scratch_shapes=[
+            pltpu.VMEM((8, rows, 128), F32),
+            pltpu.VMEM((reps, rows, 128), F32),
+            block,
+            pltpu.SemaphoreType.DMA((2, 7)),
+            pltpu.SemaphoreType.DMA((2, reps - 1)),
         ],
-        out_specs=pl.BlockSpec((rows, columns), lambda r, j, s: (r, j * subs + s)),
-        cost_estimate=link_cost(8),
-    )(spread)
+        compiler_params=params(collective_id),
+        cost_estimate=link_cost(10),
+    )(padded)
+    return summed.reshape(-1)[:size]
 
 
 def column_blocks(weight, owners, subs):
@@ -592,20 +1023,19 @@
     tokens = members * length
     q_width, k_width = GROUPS * HD, HD
 
-    def gathered(blocks, collective_id):
+    def gathered(blocks, collective_id, jobs=()):
         if kernels:
-            outs = gather_plane(blocks, collective_id)
+            outs = list(gather_plane(blocks, collective_id, jobs, reps))
         else:
             outs = [gather_tokens(block) for block in blocks]
-        return [out.reshape(tokens, -1) for out in outs]
-
-    def scattered(xs, w, turned, collective_id):
+        return [o.reshape(tokens, -1) for o in outs[: len(blocks)]] + outs[len(blocks) :]
+
+    def scattered(xs, w, turned, collective_id, jobs=()):
         if kernels:
-            return product_scatter(xs, w, turned, collective_id)
+            return product_scatter(xs, w, turned, collective_id, jobs, reps)
         x = jnp.concatenate(xs, axis=1)
-        if turned:
-            return scatter_tokens(contract_cols(x, w).astype(BF16)).astype(F32)
-        return scatter_tokens(dot_f32(x, row_block(w, subs)).astype(BF16)).astype(F32)
+        product = contract_cols(x, w) if turned else dot_f32(x, row_block(w, subs))
+        return [scatter_tokens(product.astype(BF16)).astype(F32)]
 
     codes = segment_ids * 2 + valid_mask
     gains = jnp.stack([norm_attn, norm_mlp])
@@ -666,7 +1096,7 @@
     probs_low = probs.astype(BF16)
     attended = jnp.einsum("sgtu,sud->stgd", probs_low, values, preferred_element_type=F32)
     attended = attended.reshape(tokens, q_width).astype(BF16)
-    attn_branch = scattered([attended], w_output, False, 2)
+    (attn_branch,) = scattered([attended], w_output, False, 2)
 
     hidden = hidden_in[0].astype(F32)
     scale_one = row_scale(hidden)
@@ -687,21 +1117,19 @@
     slope = sigma * (1.0 + gate_proj * (1.0 - sigma))
     gate_grad = (mixed_grad * up_proj * slope).astype(BF16)
     up_grad = (mixed_grad * silu_gate).astype(BF16)
-    gate_w_grad = owner_major(contract_rows(normed_two, gate_grad).astype(BF16))
-    up_w_grad = owner_major(contract_rows(normed_two, up_grad).astype(BF16))
-    gate_sum = sum_planes(gate_w_grad)
-    up_sum = sum_planes(up_w_grad)
+    gate_w_grad = contract_rows(normed_two, gate_grad).astype(BF16)
+    up_w_grad = contract_rows(normed_two, up_grad).astype(BF16)
+    gate_sum = sum_planes(owner_major(gate_w_grad))
     gate_up_grad = [after(gate_grad, gate_w_grad, up_w_grad), up_grad]
-    normed_two_grad = scattered(gate_up_grad, gate_up, True, 4)
+    (normed_two_grad,) = scattered(gate_up_grad, gate_up, True, 4)
     gain_mlp_grad, middle_part = norm_backward(normed_two_grad, scale_two, unit_two, gain_mlp)
     middle_grad = result_grad + middle_part
 
-    attn_out_low = after((RESIDUAL_SCALE * middle_grad).astype(BF16), down_w_piece)
+    attn_out_low = (RESIDUAL_SCALE * middle_grad).astype(BF16)
+    down_spread = spread_planes(after(down_w_piece, normed_two_grad))
     (attn_out_grad,) = gathered([attn_out_low], 5)
-    attn_out_grad = after(attn_out_grad, gate_sum)
     attended_grad = contract_cols(attn_out_grad, row_block(w_output, subs)).astype(BF16)
     output_w_grad = contract_rows(attended, attn_out_grad).astype(BF16)
-    output_w_piece = sum_planes(output_w_grad)
     heads_grad = attended_grad.reshape(members, length, GROUPS, HD)
     prob_grad = jnp.einsum("stgd,sud->sgtu", heads_grad, values, preferred_element_type=F32)
     row_dot = jnp.sum(probs * prob_grad, axis=-1, keepdims=True)
@@ -722,16 +1150,23 @@
         axis=2,
     )
     qkv_grad = qkv_grad.reshape(tokens, q_width + 2 * k_width).astype(BF16)
-    qkv_tied = after(qkv_grad, output_w_grad)
-    normed_one_grad = scattered([qkv_tied], qkv, True, 6)
-    qkv_w_grad = owner_major(contract_rows(normed_one, after(qkv_grad, normed_one_grad, up_sum)).astype(BF16))
-    qkv_sum = sum_planes(qkv_w_grad)
-    gate_piece, up_piece, qkv_piece = (to_owners(t) for t in (gate_sum, up_sum, qkv_sum))
+    qkv_tied = after(qkv_grad, output_w_grad, down_spread)
+    (normed_one_grad,) = scattered([qkv_tied], qkv, True, 6)
+    qkv_grad = after(qkv_grad, normed_one_grad, gate_sum)
+    qkv_w_grad = contract_rows(normed_one, qkv_grad).astype(BF16)
     gain_attn_grad, hidden_part = norm_backward(normed_one_grad, scale_one, unit_one, gain_attn)
     input_grad = (middle_grad + hidden_part).astype(BF16)
 
     mixed_tied = after(mixed_act, normed_one_grad, qkv_w_grad)
-    mlp_branch = scattered([mixed_tied], w_down, False, 7)
+    last_jobs = []
+    if kernels:
+        up_job = SumJob(
+            [up_w_grad, qkv_w_grad], 4, 2, reps, {1: (0, 1), 2: (2, 3), 3: (4, 5), 4: (6, 7, 8)}
+        )
+        output_job = SumJob([output_w_grad], 1, 1, reps, {4: (0, 1)})
+        last_jobs = [ExchangeJob(gate_sum), up_job, output_job]
+        last_jobs += [HandJob(up_job, reps), HandJob(output_job, reps)]
+    mlp_branch, *last = scattered([mixed_tied], w_down, False, 7, last_jobs)
     result = middle + RESIDUAL_SCALE * mlp_branch
 
     validity_own = valid_mask[0].astype(F32)[:, None]
@@ -742,30 +1177,37 @@
     tally = jnp.concatenate(
         [gain_attn_grad, gain_mlp_grad, jnp.stack(squares + [jnp.sum(validity_own)])]
     )
-    tally = lax.psum(tally, ("rep", "sub", "fsdp"))
+    tally = tally_all(tally, reps, 8) if kernels else lax.psum(tally, ("rep", "sub", "fsdp"))
     part = width // owners
     start = lax.axis_index("fsdp") * part
     gain_attn_out = lax.dynamic_slice_in_dim(tally, start, part)
     gain_mlp_out = lax.dynamic_slice_in_dim(tally, width + start, part)
     statistics = jnp.sqrt(tally[2 * width : 2 * width + 5] / (tally[2 * width + 5] * width))
 
-    down_spread = spread_planes(down_w_piece)
-    gate_spread = spread_planes(gate_piece)
-    up_spread = spread_planes(up_piece)
-    output_spread = spread_planes(output_w_piece)
-    qkv_spread = spread_planes(qkv_piece)
-    query_out = place_columns(qkv_spread[..., :q_width])
-    key_out = place_columns(qkv_spread[..., q_width : q_width + k_width])
-    value_out = place_columns(qkv_spread[..., q_width + k_width :])
     if kernels:
-        down_out, output_out = cast_rows(down_spread), cast_rows(output_spread)
-        gate_out, up_out = cast_columns(gate_spread), cast_columns(up_spread)
+        gate_piece, _, _, up_handed, output_handed = last
+        gate_spread = spread_planes(gate_piece)
+        down_out = cast_rows(down_spread)
+        output_out = cast_rows(output_handed.reshape((2, 2) + output_handed.shape[3:]))
+        gate_out, up_out = cast_columns(gate_spread, ff), cast_columns(up_handed, ff)
+        query_out, key_out, value_out = cast_heads(up_handed, ff)
     else:
         down_out, output_out = (
             jnp.swapaxes(s, 0, 1).reshape(-1, width).astype(F32)
-            for s in (down_spread, output_spread)
+            for s in (down_spread, spread_planes(sum_planes(output_w_grad)))
+        )
+        gate_spread, up_spread, qkv_spread = (
+            spread_planes(to_owners(g))
+            for g in (
+                gate_sum,
+                sum_planes(owner_major(up_w_grad)),
+                sum_planes(owner_major(qkv_w_grad)),
+            )
         )
         gate_out, up_out = place_columns(gate_spread), place_columns(up_spread)
+        query_out = place_columns(qkv_spread[..., :q_width])
+        key_out = place_columns(qkv_spread[..., q_width : q_width + k_width])
+        value_out = place_columns(qkv_spread[..., q_width + k_width :])
     return (
         result.astype(BF16)[None],
         input_grad[None],
@@ -786,7 +1228,7 @@
     fsdp = mesh.shape["fsdp"]
     subs = max(1, KV // fsdp)
     rep = mesh.shape["dp"] // subs
-    kernels = fsdp == 4 and subs == 2
+    kernels = fsdp == 4 and subs == 2 and rep >= 3
     plane_mesh = Mesh(mesh.devices.reshape(rep, subs, fsdp), ("rep", "sub", "fsdp"))
     batch = ("rep", "sub", "fsdp")
     return jax.shard_map(

time: 972 us -> 911 us (0.937)
  Pallas kernels: 438 us -> 625 us
  waiting for transfers between devices: 154 us -> 47 us
  blocking collectives: 88.9 us -> 0 us
  local copies, waits for them, and re-layouts: 89.1 us -> 36.4 us
    pallas_call x10 -> x12, Pallas kernels: 347 us -> 533 us  [the longest x4 366 us: product_scatter(): pl.pallas_call(functools.partial(product_scatter_kernel, turned, count, j...]
    all_gather x5 -> x2, waiting for transfers between devices: 98.8 us -> 22.6 us  [spread_planes(): spread = lax.all_gather(piece, ('rep', 'sub'), axis=0, tiled=False)]
    psum x1 -> x0, blocking collectives: 45.2 us -> none  [shards(): tally = lax.psum(tally, ('rep', 'sub', 'fsdp'))]
    all_to_all x3 -> x0, blocking collectives: 43.8 us -> none  [to_owners(): lax.all_to_all(blocked, 'fsdp', split_axis=0, concat_axis=0, tiled=True)]
    unnamed x117 -> x93, local copies, waits for them, and re-layouts: 52.5 us -> 13 us
    reduce_scatter x5 -> x2, waiting for transfers between devices: 54.4 us -> 24.3 us  [sum_planes(): return lax.psum_scatter(term, 'rep', scatter_dimension=0, tiled=True)]
    convert_element_type x2 -> x0, local copies, waits for them, and re-layouts: 11.7 us -> none  [place_columns(): return part.reshape(reps * rows, owners * subs * columns).astype(F32)]
  transfers between devices with their start and end apart: 11 -> 5, of which waited for: 4 -> 2; matrix products, arithmetic and copies ran while one was open for 20% -> 17% of each run, Pallas kernels for 41% -> 39%
where the time goes in v3:
time: 911 us; the launch traced here: 900 us
  Pallas kernels  625 us (69%)
  matrix products  126 us (14%)
  other arithmetic  50.1 us (5%)
  waiting for transfers between devices  47 us (5%)
  local copies, waits for them, and re-layouts  36.4 us (4%)
  between operations  15.4 us (2%)
    pallas_call x4, Pallas kernels, product_scatter(): pl.pallas_call(functools.partial(product_scatter_kernel, turned, count, j...  366 us
    pallas_call x2, Pallas kernels, gather_plane(): pl.pallas_call(functools.partial(gather_kernel, count, jobs), out_shape=[...  113 us
    pallas_call x1, Pallas kernels, start_plane(): pl.pallas_call(start_kernel, out_shape=[jax.ShapeDtypeStruct(s, d) for s,...  63.8 us
    dot_general x5, matrix products, contract_rows(): return jnp.einsum('sa,sb->ab', left, right, preferred_element_type=F32)  51.3 us
    dot_general x2, matrix products, contract_cols(): return jnp.einsum('sb,ab->sa', left, right, preferred_element_type=F32)  28.6 us
    pallas_call x1, Pallas kernels, quarter_columns(): pl.pallas_call(quarter_kernel, out_shape=jax.ShapeDtypeStruct((4, rows //...  27.9 us
    dot_general x2, matrix products, dot_f32(): return jnp.dot(left, right, preferred_element_type=F32)  27.8 us
    reduce_scatter x2, waiting for transfers between devices, sum_planes(): return lax.psum_scatter(term, 'rep', scatter_dimension=0, tiled=True)  24.3 us
  transfers between devices with their start and end apart: 5, of which 2 were waited for; matrix products, arithmetic and copies ran while one was open for 17% of the time, Pallas kernels for 39%

profile of v3, /device:TPU:0, one launch (start us, length us, event | category | flops | bytes accessed | tf_op | source)
XLA Modules:
  0.0 900.4 jit_solution(14536120028850421277)
XLA Ops:
  7.3 27.9 %shard_map.220 = bf16[4,128,2048]{2,1,0:T(8,128)(2,1)} custom-call(bf16[512,8192]{1,0:T(8,128)(2,1)} %gate_ref.1, bf16[512,8192]{1,0:T(8,128)(2,1)} %up_ref.1), custom_call_target="tpu_custom_call" | custom-call | bytes 82500000 | tf_op jit(solution)/shard_map/pallas_call | solution.py:572
  36.5 63.8 %shard_map.221 = (bf16[8,256,2048]{2,1,0:T(8,128)(2,1)}, s32[8,1,256]{2,1,0:T(1,128)}, bf16[4,2,512]{2,1,0:T(2,128)(2,1)}, bf16[4,512,256]{2,1,0:T(8,128)(2,1)},...) custom-call(bf16[256,2048]{1,0:T(8,128)(2,1)} %bitcast.220, s32[1,256]{1,0:T(1,128)} %get-tuple-element.88.code_ref, ...), custom_call_target="tpu_custom_call" | custom-call | bytes 198000000 | tf_op jit(solution)/shard_map/pallas_call | solution.py:647
  113.5 6.1 fusion.8
  133.9 42.3 %shard_map.222 = f32[256,2048]{1,0:T(8,128)} custom-call(bf16[2048,256]{1,0:T(8,128)(2,1)} %copy.66.refs_0_, bf16[512,2048]{1,0:T(8,128)(2,1)} %refs_1_.2), custom_call_target="tpu_custom_call" | custom-call | bytes 145200000 | tf_op jit(solution)/shard_map/pallas_call | solution.py:793
  180.7 73.4 %shard_map.223 = (bf16[8,256,2048]{2,1,0:T(8,128)(2,1)}, bf16[8,256,2048]{2,1,0:T(8,128)(2,1)}) custom-call(bf16[256,2048]{1,0:T(8,128)(2,1)} %multiply_convert_fusion.5.refs_0_, bf16[256,2048]{1,0:T(8,128)(2,1)} %fusion.22.refs_1_), custom_call_target="tpu_custom_call" | custom-call | bytes 264000000 | tf_op jit(solution)/shard_map/pallas_call | solution.py:522
  254.1 21.7 %fusion.86 = f32[2048,2048]{1,0:T(8,128)S(1)} fusion(bf16[2048,2048]{1,0:T(8,128)(2,1)} %bitcast.256, bf16[2048,2048]{1,0:T(8,128)(2,1)} %bitcast.230), kind=kOutput, calls=%fused_computation.153 | convolution fusion | flops 17179869184 | bytes 33554432 | tf_op jit(solution)/shard_map/dot_general | solution.py:51
  278.8 5.5 copy-done.5
  286.3 11.0 %convolution_convert_fusion = bf16[1024,2048]{1,0:T(8,128)(2,1)} fusion(bf16[2048,1024]{1,0:T(8,128)(2,1)S(1)} %multiply_convert_fusion.3.refs_0_, bf16[2048,2048]{1,0:T(8,128)(2,1)S(1)} %bitcast.260), kind=kOutput, calls=%fused_computation.27 | convolution fusion | flops 8592031744 | bytes 16777216 | tf_op jit(solution)/shard_map/sa,sb->ab/dot_general | solution.py:55
  297.4 22.5 %multiply_convert_fusion.1 = (bf16[2048,1024]{1,0:T(8,128)(2,1)S(1)}, bf16[2048,1024]{1,0:T(8,128)(2,1)}) fusion(f32[2048,2048]{1,0:T(8,128)} %copy-done.5, bf16[2048,2048]{1,0:T(8,128)(2,1)} %bitcast.259, bf16[2048,2048]{1,0:T(8,128)(2,1)} %refs_1_.3, s32[]{:T(128)S(6)} %select_n.45), kind=kOutput, calls=%fused_computation.13 | convolution fusion | flops 8617197568 | bytes 37748740 | tf_op jit(solution)/shard_map/sb,ab->sa/dot_general | solution.py:59
  319.9 14.4 %convolution_convert_fusion.1.refs_3_ = bf16[2048,1024]{1,0:T(8,128)(2,1)} fusion(bf16[2048,2048]{1,0:T(8,128)(2,1)} %bitcast.257, bf16[2048,1024]{1,0:T(8,128)(2,1)S(1)} %get-tuple-element.72.refs_1_), kind=kOutput, calls=%fused_computation.28 | convolution fusion | flops 8592031744 | bytes 16777216 | tf_op jit(solution)/shard_map/sa,sb->ab/dot_general | solution.py:55
  334.3 13.0 %convolution_convert_fusion.2 = bf16[2048,1024]{1,0:T(8,128)(2,1)} fusion(bf16[2048,2048]{1,0:T(8,128)(2,1)} %bitcast.258, bf16[2048,1024]{1,0:T(8,128)(2,1)S(1)} %copy-done.12), kind=kOutput, calls=%fused_computation.29 | convolution fusion | flops 8592031744 | bytes 16777216 | tf_op jit(solution)/shard_map/sa,sb->ab/dot_general | solution.py:55
  347.3 48.5 %shard_map.224 = f32[256,2048]{1,0:T(8,128)} custom-call(bf16[2048,1024]{1,0:T(8,128)(2,1)} %get-tuple-element.44.refs_0_, bf16[2048,1024]{1,0:T(8,128)(2,1)} %copy-done.11, bf16[2048,2048]{1,0:T(8,128)(2,1)} %bitcast.231), custom_call_target="tpu_custom_call" | custom-call | bytes 145200000 | tf_op jit(solution)/shard_map/pallas_call | solution.py:793
  401.8 9.5 %fusion.2 = bf16[2048,2048]{1,0:T(8,128)(2,1)} fusion(f32[2048]{0:T(1024)S(1)} %bitcast.248, f32[2048]{0:T(1024)S(1)} %bitcast.251, bf16[8,256,2048]{2,1,0:T(8,128)(2,1)} %get-tuple-element.35), kind=kLoop, calls=%fused_computation.3 | loop fusion | flops 16777216 | bytes 16793600 | tf_op jit(solution)/shard_map/convert_element_type | solution.py:1074
  415.7 39.4 %shard_map.225 = bf16[8,256,2048]{2,1,0:T(8,128)(2,1)} custom-call(bf16[256,2048]{1,0:T(8,128)(2,1)} %multiply_convert_fusion.4.refs_0_), custom_call_target="tpu_custom_call" | custom-call | bytes 132000000 | tf_op jit(solution)/shard_map/pallas_call | solution.py:522
  455.0 6.1 convolution_convert_fusion.5
  489.5 42.9 %shard_map.226 = f32[256,2048]{1,0:T(8,128)} custom-call(bf16[2048,384]{1,0:T(8,128)(2,1)} %copy.74.refs_0_, bf16[2048,384]{1,0:T(8,128)(2,1)} %bitcast.223), custom_call_target="tpu_custom_call" | custom-call | bytes 145200000 | tf_op jit(solution)/shard_map/pallas_call | solution.py:793
  532.3 24.3 %reduce-scatter.5.cloned.1.call-done.refs_2_ = bf16[512,1024]{1,0:T(8,128)(2,1)} async-done(((bf16[2048,1024]{1,0:T(8,128)(2,1)}), bf16[512,1024]{1,0:T(8,128)(2,1)}) %reduce-scatter.5.cloned.1.call-update) | async-done | bytes 1048592 | tf_op jit(solution)/shard_map/reduce_scatter | solution.py:977
  556.6 9.5 %convolution_convert_fusion.3.refs_4_ = bf16[2048,384]{1,0:T(8,128)(2,1)} fusion(bf16[2048,2048]{1,0:T(8,128)(2,1)} %fusion.2, bf16[2048,384]{0,1:T(8,128)(2,1)} %bitcast.235), kind=kOutput, calls=%fused_computation.36 | convolution fusion | flops 3222011904 | bytes 11534336 | tf_op jit(solution)/shard_map/sa,sb->ab/dot_general | solution.py:55
  566.1 232.2 %shard_map.227 = (f32[256,2048]{1,0:T(8,128)}, bf16[4,128,1024]{2,1,0:T(8,128)(2,1)}, bf16[2,4,256,1408]{3,2,1,0:T(8,128)(2,1)}, bf16[2,1,128,2048]{3,2,1,0:T(8,...) custom-call(bf16[2048,1024]{1,0:T(8,128)(2,1)} %copy-done.4, ...), custom_call_target="tpu_custom_call" | custom-call | bytes 145200000 | tf_op jit(solution)/shard_map/pallas_call | solution.py:793
  803.3 10.6 %shard_map.232 = f32[512,8192]{1,0:T(8,128)} custom-call(bf16[2,2,4,256,1408]{4,3,2,1,0:T(8,128)(2,1)} %get-tuple-element.50.q_ref.kv_ref.x_ref), custom_call_target="tpu_custom_call" | custom-call | bytes 26400000 | tf_op jit(solution)/shard_map/pallas_call | solution.py:850
  813.9 10.5 %shard_map.233 = f32[2048,2048]{1,0:T(8,128)} custom-call(bf16[4,2,256,2048]{3,2,1,0:T(8,128)(2,1)} %bitcast.224), custom_call_target="tpu_custom_call" | custom-call | bytes 26400000 | tf_op jit(solution)/shard_map/pallas_call | solution.py:827
  834.4 11.6 %shard_map.228 = f32[40,128]{1,0:T(8,128)S(1)} custom-call(f32[40,128]{1,0:T(8,128)S(1)} %pad_bitcast_fusion.x_ref), custom_call_target="tpu_custom_call" | custom-call | bytes 33000000 | tf_op jit(solution)/shard_map/pallas_call | solution.py:932
  857.5 22.6 %all-gather.10.cloned.1.call-done = bf16[32,128,1024]{2,1,0:T(8,128)(2,1)} async-done(((bf16[4,128,1024]{2,1,0:T(8,128)(2,1)}), bf16[32,128,1024]{2,1,0:T(8,128)(2,1)}) %all-gather.10.cloned.1.call-update) | async-done | bytes 8388624 | tf_op jit(solution)/shard_map/all_gather | solution.py:982
  880.1 13.5 %shard_map.231 = f32[512,8192]{1,0:T(8,128)} custom-call(bf16[4,2,4,128,1024]{4,3,2,1,0:T(8,128)(2,1)} %bitcast.225), custom_call_target="tpu_custom_call" | custom-call | bytes 26400000 | tf_op jit(solution)/shard_map/pallas_call | solution.py:850
  (166 shorter events, 102.1 us)
Async XLA Ops:
  7.2 28.1 %copy-start.34 = (bf16[512]{0:T(512)(128)(2,1)S(1)}, bf16[512]{0:T(512)(128)(2,1)}, u32[]{:S(2)}) copy-start(bf16[512]{0:T(512)(128)(2,1)} %param.17) | copy-start | bytes 3076
  7.2 28.1 %copy-start.35 = (bf16[512]{0:T(512)(128)(2,1)S(1)}, bf16[512]{0:T(512)(128)(2,1)}, u32[]{:S(2)}) copy-start(bf16[512]{0:T(512)(128)(2,1)} %param.22) | copy-start | bytes 3076
  7.2 28.7 %copy-start.37 = (s32[1,256]{1,0:T(1,128)S(1)}, s32[1,256]{1,0:T(1,128)}, u32[]{:S(2)}) copy-start(s32[1,256]{1,0:T(1,128)} %param.15) | copy-start | bytes 3076
  7.2 28.7 %copy-start.36 = (s32[1,256]{1,0:T(1,128)S(1)}, s32[1,256]{1,0:T(1,128)}, u32[]{:S(2)}) copy-start(s32[1,256]{1,0:T(1,128)} %param.14) | copy-start | bytes 3076
  7.2 246.9 %all-gather.6.cloned.1.call-start = ((), (), s32[]{:S(2)}) async-start(), calls=%async_computation.2 | async-start | bytes 10485760 | tf_op jit(solution)/shard_map/all_gather | solution.py:1062
  35.2 360.6 %reduce-scatter.3.cloned.1.call-start = ((), (), s32[]{:S(2)}) async-start(), calls=%async_computation.3 | async-start | bytes 5242880 | tf_op jit(solution)/shard_map/reduce_scatter | solution.py:977
  104.9 7.1 copy-start.6
  106.7 6.7 copy-start.14
  112.6 6.9 copy-start.26
  113.4 7.0 copy-start.15
  119.6 7.0 copy-start.21
  119.7 6.9 copy-start.23
  132.6 43.6 %copy-start.1 = (bf16[1,256,2048]{2,1,0:T(8,128)(2,1)S(1)}, bf16[1,256,2048]{2,1,0:T(8,128)(2,1)}, u32[]{:S(2)}) copy-start(bf16[1,256,2048]{2,1,0:T(8,128)(2,1)} %param.13) | copy-start | bytes 3145732
  275.8 8.4 copy-start.5
  275.8 10.5 %copy-start.39 = (bf16[8,256,2048]{2,1,0:T(8,128)(2,1)S(1)}, bf16[8,256,2048]{2,1,0:T(8,128)(2,1)}, u32[]{:S(2)}) copy-start(bf16[8,256,2048]{2,1,0:T(8,128)(2,1)} %get-tuple-element.42) | copy-start | bytes 25165828
  297.3 189.5 %all-gather.8.cloned.1.call-start = ((), (), s32[]{:S(2)}) async-start(), calls=%async_computation.5 | async-start | bytes 9437184 | tf_op jit(solution)/shard_map/all_gather | solution.py:982
  319.9 14.4 %copy-start.11 = (bf16[2048,1024]{1,0:T(8,128)(2,1)}, bf16[2048,1024]{1,0:T(8,128)(2,1)S(1)}, u32[]{:S(2)}) copy-start(bf16[2048,1024]{1,0:T(8,128)(2,1)S(1)} %get-tuple-element.72.refs_1_) | copy-start | bytes 12582916
  319.9 14.4 %copy-start.12 = (bf16[2048,1024]{1,0:T(8,128)(2,1)S(1)}, bf16[2048,1024]{1,0:T(8,128)(2,1)}, u32[]{:S(2)}) copy-start(bf16[2048,1024]{1,0:T(8,128)(2,1)} %get-tuple-element.44.refs_0_) | copy-start | bytes 12582916
  347.3 49.0 %copy-start.31 = (f32[1,2,8,128]{3,2,1,0:T(8,128)S(1)}, f32[1,2,8,128]{3,2,1,0:T(8,128)}, u32[]{:S(2)}) copy-start(f32[1,2,8,128]{3,2,1,0:T(8,128)} %get-tuple-element.83) | copy-start | bytes 24580
  395.9 160.7 %reduce-scatter.5.cloned.1.call-start = ((), (), s32[]{:S(2)}) async-start(), calls=%async_computation.4 | async-start | bytes 5242880 | tf_op jit(solution)/shard_map/reduce_scatter | solution.py:977
  401.2 479.0 %all-gather.10.cloned.1.call-start = ((), (), s32[]{:S(2)}) async-start(), calls=%async_computation.6 | async-start | bytes 9437184 | tf_op jit(solution)/shard_map/all_gather | solution.py:982
  566.1 232.3 %copy-start.38 = (s32[1,256]{1,0:T(1,128)S(1)}, s32[1,256]{1,0:T(1,128)}, u32[]{:S(2)}) copy-start(s32[1,256]{1,0:T(1,128)} %param.15) | copy-start | bytes 3076
  813.9 10.5 %copy-start.2 = (bf16[1,256,2048]{2,1,0:T(8,128)(2,1)S(1)}, bf16[1,256,2048]{2,1,0:T(8,128)(2,1)}, u32[]{:S(2)}) copy-start(bf16[1,256,2048]{2,1,0:T(8,128)(2,1)} %param.13) | copy-start | bytes 3145732
  813.9 10.5 %copy-start.33 = (f32[1,256]{1,0:T(1,128)S(1)}, f32[1,256]{1,0:T(1,128)}, u32[]{:S(2)}) copy-start(f32[1,256]{1,0:T(1,128)} %get-tuple-element.87) | copy-start | bytes 3076
  (25 other events, 77.0 us)
Sparse Core Ops, SparseCore 0:
  35.3 149.8 all-gather.5
  297.5 77.0 reduce-scatter.2
  396.0 82.3 all-gather.7
  481.2 75.3 reduce-scatter.4
  798.5 81.5 all-gather.9

commit v4 on v3

--- a/solution.py
+++ b/solution.py
@@ -109,6 +109,11 @@
         self.send_sems, self.recv_sems, self.copies = send_sems, recv_sems, []
 
     def send(self, src, dst, device):
+        copy = self.make(src, dst, device)
+        copy.start()
+        return copy
+
+    def make(self, src, dst, device):
         index = len(self.copies)
         copy = pltpu.make_async_remote_copy(
             src_ref=src,
@@ -118,7 +123,6 @@
             device_id=device,
             device_id_type=MESH,
         )
-        copy.start()
         self.copies.append(copy)
         return copy
 
@@ -127,71 +131,96 @@
             copy.wait_send()
 
 
+class Bounce:
+    def __init__(self, src, dst, room, sems):
+        self.fetch = pltpu.make_async_copy(src, room, sems.at[0])
+        self.store = pltpu.make_async_copy(room, dst, sems.at[1])
+
+    def start(self):
+        self.fetch.start()
+
+    def turn(self):
+        self.fetch.wait()
+        self.store.start()
+
+    def wait(self):
+        self.store.wait()
+
+
 class Gather:
     def __init__(self, sender, x_ref, out_ref, local_sem, place):
-        self.sender, self.x_ref, self.out_ref, self.place = sender, x_ref, out_ref, place
-        rep, core, own, across, down, _ = place
-        self.to_across, self.to_down = (rep, core, across), (rep, core, down)
-        self.to_core = (rep, 1 - core, own)
+        rep, core, own, across, down, corner = place
+        to_across, to_down, to_core = (rep, core, across), (rep, core, down), (rep, 1 - core, own)
         half = x_ref.shape[0] // 2
-        self.low, self.high, self.whole = pl.ds(0, half), pl.ds(half, half), pl.ds(0, 2 * half)
-        self.base = core * 4
-        self.mine = pltpu.make_async_copy(x_ref, out_ref.at[self.base + own], local_sem)
-
-    def first(self, rows, device):
-        own = self.place[2]
-        return self.sender.send(
-            self.x_ref.at[rows], self.out_ref.at[self.base + own, rows], device
-        )
-
-    def forward(self, block, rows, device):
-        ref = self.out_ref.at[self.base + block, rows]
-        return self.sender.send(ref, ref, device)
+        low, high, whole = pl.ds(0, half), pl.ds(half, half), pl.ds(0, 2 * half)
+        base = core * 4
+
+        def first(rows, device):
+            return sender.make(x_ref.at[rows], out_ref.at[base + own, rows], device)
+
+        def forward(block, rows, device):
+            ref = out_ref.at[base + block, rows]
+            return sender.make(ref, ref, device)
+
+        self.across_low, self.down_high = first(low, to_across), first(high, to_down)
+        self.across_high, self.down_low = first(high, to_across), first(low, to_down)
+        self.corner_low = forward(across, low, to_down)
+        self.corner_high = forward(down, high, to_across)
+        self.swap_own = first(whole, to_core)
+        self.swap_near = [
+            forward(across, low, to_core),
+            forward(down, high, to_core),
+            forward(across, high, to_core),
+            forward(down, low, to_core),
+        ]
+        self.swap_corner = [forward(corner, low, to_core), forward(corner, high, to_core)]
+        self.mine = pltpu.make_async_copy(x_ref, out_ref.at[base + own], local_sem)
 
     def begin(self):
-        self.across_low = self.first(self.low, self.to_across)
-        self.down_high = self.first(self.high, self.to_down)
-        self.across_high = self.first(self.high, self.to_across)
-        self.down_low = self.first(self.low, self.to_down)
-        self.swaps = [self.first(self.whole, self.to_core)]
+        for copy in (self.across_low, self.down_high, self.across_high, self.down_low):
+            copy.start()
+        self.swap_own.start()
         self.mine.start()
 
     def relay(self):
-        _, _, _, across, down, _ = self.place
-        low, high, to_core = self.low, self.high, self.to_core
         self.across_low.wait_recv()
-        self.corner_low = self.forward(across, low, self.to_down)
-        self.swaps.append(self.forward(across, low, to_core))
+        self.corner_low.start()
+        self.swap_near[0].start()
         self.down_high.wait_recv()
-        self.corner_high = self.forward(down, high, self.to_across)
-        self.swaps.append(self.forward(down, high, to_core))
+        self.corner_high.start()
+        self.swap_near[1].start()
         self.across_high.wait_recv()
-        self.swaps.append(self.forward(across, high, to_core))
+        self.swap_near[2].start()
         self.down_low.wait_recv()
-        self.swaps.append(self.forward(down, low, to_core))
+        self.swap_near[3].start()
 
     def finish(self):
-        corner = self.place[5]
         self.corner_low.wait_recv()
-        self.swaps.append(self.forward(corner, self.low, self.to_core))
+        self.swap_corner[0].start()
         self.corner_high.wait_recv()
-        self.swaps.append(self.forward(corner, self.high, self.to_core))
-        for swap in self.swaps:
+        self.swap_corner[1].start()
+        for swap in [self.swap_own] + self.swap_near + self.swap_corner:
             swap.wait_recv()
         self.mine.wait()
 
 
 class ExchangeJob:
+    climbs = False
+    corner = True
+
     def __init__(self, source):
         self.rows = source.shape[0] // 4
+        shape = (self.rows, source.shape[1])
         self.arrays = [source]
-        self.corner = True
-        self.outs = [jax.ShapeDtypeStruct((4, self.rows, source.shape[1]), BF16)]
-        self.scratch = [pltpu.SemaphoreType.DMA((3,))] * 2 + [pltpu.SemaphoreType.DMA]
+        self.outs = [jax.ShapeDtypeStruct((4,) + shape, BF16)]
+        self.scratch = [pltpu.SemaphoreType.DMA((3,))] * 2
+        self.scratch += [pltpu.VMEM(shape, BF16), pltpu.SemaphoreType.DMA((2,))]
 
     def open(self, arrays, outs, scratch, place):
-        self.source, self.out = arrays[0], outs[0]
-        self.sems, self.keep_sem, self.place = scratch[:2], scratch[2], place
+        self.source, self.out, self.place = arrays[0], outs[0], place
+        own = place[2]
+        self.sems = scratch[:2]
+        self.keep = Bounce(self.part(own), self.out.at[own], scratch[2], scratch[3])
 
     def part(self, block):
         return self.source.at[pl.ds(pl.multiple_of(block * self.rows, 16), self.rows)]
@@ -199,14 +228,36 @@
     def stage(self, n):
         rep, core, own, across, down, corner = self.place
         if n == 0:
+            self.keep.start()
             self.sender = Sender(*self.sems)
             for peer in (corner, across, down):
                 self.sender.send(self.part(peer), self.out.at[own], (rep, core, peer))
-            self.keep = pltpu.make_async_copy(self.part(own), self.out.at[own], self.keep_sem)
-            self.keep.start()
+        if n == 1:
+            self.keep.turn()
         if n == 6:
             for copy in self.sender.copies:
                 copy.wait()
+            self.keep.wait()
+
+
+class KeepJob:
+    climbs = False
+    corner = False
+
+    def __init__(self, source):
+        self.arrays = [source]
+        self.outs = [jax.ShapeDtypeStruct(source.shape, BF16)]
+        self.scratch = [pltpu.VMEM(source.shape, BF16), pltpu.SemaphoreType.DMA((2,))]
+
+    def open(self, arrays, outs, scratch, place):
+        self.keep = Bounce(arrays[0], outs[0], *scratch)
+
+    def stage(self, n):
+        if n == 0:
+            self.keep.start()
+        if n == 1:
+            self.keep.turn()
+        if n == 6:
             self.keep.wait()
 
 
@@ -230,6 +281,8 @@
 
 
 class SumJob:
+    climbs = True
+
     def __init__(self, sources, blocks, cuts, reps, steps):
         self.blocks, self.cuts, self.reps, self.steps = blocks, cuts, reps, steps
         self.arrays = sources
@@ -240,19 +293,21 @@
         self.size = self.half // cuts
         self.widths = [source.shape[1] for source in sources]
         wide = sum(self.widths)
-        self.outs = [jax.ShapeDtypeStruct((2, blocks, self.half, wide), BF16)]
+        self.shape = (2, blocks, self.half, wide)
+        self.outs = []
         self.count = blocks * cuts
         sems = pltpu.SemaphoreType.DMA((2, self.count))
         self.scratch = [
-            pltpu.VMEM((2, blocks, self.half, wide), BF16),
-            pltpu.VMEM((2, blocks, self.half, wide), BF16),
+            pltpu.VMEM(self.shape, BF16),
+            pltpu.VMEM(self.shape, BF16),
+            pltpu.VMEM(self.shape, BF16),
             pltpu.SemaphoreType.DMA((2, blocks, len(sources))),
         ] + [sems] * 5
 
     def open(self, arrays, outs, scratch, place):
-        self.sources, self.fin = arrays, outs[0]
-        self.held, self.landed, self.load_sems = scratch[:3]
-        self.chain_sems, self.give_sems, self.keep_sems = scratch[3:5], scratch[5:7], scratch[7]
+        self.sources = arrays
+        self.held, self.landed, self.fin, self.load_sems = scratch[:4]
+        self.chain_sems, self.give_sems, self.keep_sems = scratch[4:6], scratch[6:8], scratch[8]
         self.rep, self.core, self.own = place[:3]
         self.ways = column_place(place, self.reps)
         for k in range(self.blocks):
@@ -367,27 +422,34 @@
 
 
 class HandJob:
-    def __init__(self, source, reps):
-        self.inner = isinstance(source, SumJob)
-        self.sums = source if self.inner else None
-        shape = source.outs[0].shape if self.inner else source.shape
-        self.arrays = [] if self.inner else [source]
-        self.reps, self.blocks = reps, shape[1]
+    climbs = True
+
+    def __init__(self, sums, reps, cuts):
+        self.sums, self.arrays = sums, []
+        shape = sums.shape
+        self.reps, self.cuts, self.size = reps, cuts, shape[2] // cuts
+        self.count = shape[1] * cuts
         self.corner = False
         self.outs = [jax.ShapeDtypeStruct((2, 2) + shape[1:], BF16)]
-        self.scratch = [pltpu.SemaphoreType.DMA((2, self.blocks))] * 5
+        self.scratch = [pltpu.SemaphoreType.DMA((2, self.count))] * 5
 
     def open(self, arrays, outs, scratch, place):
-        self.fin = None if self.inner else arrays[0]
         self.out = outs[0]
         self.hand_sems, self.side_sems, self.keep_sems = scratch[:2], scratch[2:4], scratch[4]
         self.rep, self.core, self.own = place[:3]
         self.ways = column_place(place, self.reps)
 
+    def rows(self, j):
+        return j // self.cuts, pl.ds(j % self.cuts * self.size, self.size)
+
+    def place(self, way, j):
+        block, rows = self.rows(j)
+        return self.out.at[way, self.core, block, rows]
+
     def remote(self, src, way, j, sems, device):
         return pltpu.make_async_remote_copy(
             src_ref=src,
-            dst_ref=self.out.at[way, self.core, j],
+            dst_ref=self.place(way, j),
             send_sem=sems[0].at[way, j],
             recv_sem=sems[1].at[way, j],
             device_id=device,
@@ -398,16 +460,17 @@
         return (self.rep, 1 - self.core, self.own)
 
     def begin(self):
-        fin = self.sums.fin if self.inner else self.fin
-        for j in range(self.blocks):
+        fin = self.sums.fin
+        for j in range(self.count):
             for way in range(2):
 
                 @pl.when(self.ways[way][1])
                 def _(way=way, j=j):
-                    src = fin.at[way, j]
+                    block, rows = self.rows(j)
+                    src = fin.at[way, block, rows]
                     self.remote(src, way, j, self.hand_sems, self.ways[way][3]).start()
                     self.remote(src, way, j, self.side_sems, self.beside()).start()
-                    dst = self.out.at[way, self.core, j]
+                    dst = self.place(way, j)
                     pltpu.make_async_copy(src, dst, self.keep_sems.at[way, j]).start()
 
     def hand(self, way, j):
@@ -415,7 +478,7 @@
 
         @pl.when(jnp.logical_not(last))
         def _():
-            ref = self.out.at[way, self.core, j]
+            ref = self.place(way, j)
             hand = self.remote(ref, way, j, self.hand_sems, self.ways[way][3])
             hand.wait_recv()
 
@@ -426,14 +489,14 @@
             self.remote(ref, way, j, self.side_sems, self.beside()).start()
 
     def pass_on(self):
-        for j in range(self.blocks + 1):
-            skewed(self.rep, self.reps, self.blocks, lambda w, i: self.hand(1 - w, i), j)
+        for j in range(self.count + 1):
+            skewed(self.rep, self.reps, self.count, lambda w, i: self.hand(1 - w, i), j)
 
     def close(self):
-        for j in range(self.blocks):
+        for j in range(self.count):
             for way in range(2):
                 first, last = self.ways[way][:2]
-                ref = self.out.at[way, self.core, j]
+                ref = self.place(way, j)
                 self.remote(ref, way, j, self.side_sems, self.beside()).wait()
 
                 @pl.when(jnp.logical_not(first))
@@ -445,9 +508,9 @@
                     pltpu.make_async_copy(ref, ref, self.keep_sems.at[way, j]).wait()
 
     def stage(self, n):
-        if n == (7 if self.inner else 0):
+        if n == 7:
             self.begin()
-        if n == (8 if self.inner else 6):
+        if n == 8:
             self.pass_on()
         if n == 9:
             self.close()
@@ -463,7 +526,7 @@
     def greet(self, place):
         rep, core, own, across, down, corner = place
         devices = [(rep, core, across), (rep, core, down), (rep, 1 - core, own)]
-        if self.jobs:
+        if any(job.climbs for job in self.jobs):
             devices += [((rep + 1) % self.reps, core, own)]
             devices += [((rep + self.reps - 1) % self.reps, core, own)]
         if any(job.corner for job in self.jobs):
@@ -523,7 +586,7 @@
         functools.partial(gather_kernel, count, jobs),
         out_shape=[jax.ShapeDtypeStruct((8,) + x.shape, x.dtype) for x in blocks]
         + jobs.out_shapes,
-        in_specs=[HBM] * (count + len(jobs.arrays)),
+        in_specs=[VM] * count + [HBM] * len(jobs.arrays),
         out_specs=[HBM] * (count + len(jobs.out_shapes)),
         scratch_shapes=[
             pltpu.SemaphoreType.DMA((count,)),
@@ -536,7 +599,7 @@
     )(*blocks, *jobs.arrays)
 
 
-def quarter_kernel(gate_ref, up_ref, out_ref, local_sems, send_sems, recv_sems):
+def quarter_kernel(gate_ref, up_ref, out_ref, room, local_sems, send_sems, recv_sems):
     rep, core, own, across, down, corner = plane_position()
     peers = (corner, across, down)
     meet([(rep, core, peer) for peer in peers])
@@ -555,11 +618,12 @@
             sender.send(source(ref, peer), target, (rep, core, peer))
     local = []
     for k, ref in enumerate((gate_ref, up_ref)):
-        copy = pltpu.make_async_copy(
-            source(ref, own), out_ref.at[own, :, pl.ds(k * width, width)], local_sems.at[k]
-        )
+        target = out_ref.at[own, :, pl.ds(k * width, width)]
+        copy = Bounce(source(ref, own), target, room.at[k], local_sems.at[k])
         copy.start()
         local.append(copy)
+    for copy in local:
+        copy.turn()
     for copy in sender.copies:
         copy.wait_recv()
     sender.finish()
@@ -575,7 +639,8 @@
         in_specs=[HBM, HBM],
         out_specs=HBM,
         scratch_shapes=[
-            pltpu.SemaphoreType.DMA((2,)),
+            pltpu.VMEM((2, rows // reps, columns // 8), BF16),
+            pltpu.SemaphoreType.DMA((2, 2)),
             pltpu.SemaphoreType.DMA((6,)),
             pltpu.SemaphoreType.DMA((6,)),
         ],
@@ -587,7 +652,7 @@
 def start_kernel(
     x_ref, code_ref, gain_ref, q_ref, k_ref, v_ref,
     x_out, code_out, gain_out, q_out, k_out, v_out,
-    local_sems, send_sems, recv_sems,
+    q_room, k_room, v_room, bounce_sems, local_sems, send_sems, recv_sems,
 ):
     place = plane_position()
     rep, core, own, across, down, corner = place
@@ -595,12 +660,17 @@
     meet([(rep, core, peer) for peer in peers] + [(rep, 1 - core, peer) for peer in peers]
          + [(rep, 1 - core, own)])
     sender = Sender(send_sems, recv_sems)
-    direct, local = [], []
+    direct, local, bounced = [], [], []
 
     def keep(src, dst):
         copy = pltpu.make_async_copy(src, dst, local_sems.at[1 + len(local)])
         copy.start()
         local.append(copy)
+
+    def bounce(src, dst, room):
+        copy = Bounce(src, dst, room, bounce_sems.at[len(bounced)])
+        copy.start()
+        bounced.append(copy)
 
     def columns(ref, block, width):
         return ref.at[:, pl.ds(pl.multiple_of(block * width, width), width)]
@@ -617,20 +687,22 @@
             direct.append(sender.send(code_ref, code_out.at[core * 4 + own], other))
         direct.append(sender.send(code_ref, code_out.at[core * 4 + own], (rep, 1 - core, own)))
         keep(gain_ref, gain_out.at[own])
-        keep(columns(q_ref, own * 2 + core, 256), q_out.at[own])
-        keep(columns(k_ref, own, 128), k_out.at[own])
-        keep(columns(v_ref, own, 128), v_out.at[own])
+        bounce(columns(q_ref, own * 2 + core, 256), q_out.at[own], q_room)
+        bounce(columns(k_ref, own, 128), k_out.at[own], k_room)
+        bounce(columns(v_ref, own, 128), v_out.at[own], v_room)
         keep(code_ref, code_out.at[core * 4 + own])
 
     move = Gather(sender, x_ref, x_out, local_sems.at[0], place)
     move.begin()
     weights()
+    for copy in bounced:
+        copy.turn()
     move.relay()
     move.finish()
     for copy in direct:
         copy.wait_recv()
     sender.finish()
-    for copy in local:
+    for copy in local + bounced:
         copy.wait()
 
 
@@ -647,10 +719,14 @@
     return pl.pallas_call(
         start_kernel,
         out_shape=[jax.ShapeDtypeStruct(s, d) for s, d in shapes],
-        in_specs=[HBM] * 6,
+        in_specs=[VM] + [HBM] * 5,
         out_specs=[HBM] * 6,
         scratch_shapes=[
-            pltpu.SemaphoreType.DMA((6,)),
+            pltpu.VMEM((rows, GROUPS * HD), BF16),
+            pltpu.VMEM((rows, 2 * HD), BF16),
+            pltpu.VMEM((rows, 2 * HD), BF16),
+            pltpu.SemaphoreType.DMA((3, 2)),
+            pltpu.SemaphoreType.DMA((3,)),
             pltpu.SemaphoreType.DMA((32,)),
             pltpu.SemaphoreType.DMA((32,)),
         ],
@@ -818,6 +894,196 @@
     )(*xs, w, *jobs.arrays)
 
 
+def turn(value, cos_ref, sin_ref, back):
+    wide = value.shape[1]
+    lanes = lax.broadcasted_iota(jnp.int32, value.shape, 1)
+    front = lax.rem(lanes, HD) < HD // 2
+    ahead = pltpu.roll(value, wide - HD // 2, 1)
+    behind = pltpu.roll(value, HD // 2, 1)
+    swapped = jnp.where(front, -ahead, behind) * sin_ref[...]
+    turned = value * cos_ref[...]
+    return turned - swapped if back else turned + swapped
+
+
+def allowed_pairs(row_ref, col_ref):
+    keys, queries = row_ref[0], col_ref[0]
+    length = keys.shape[1]
+    row_index = lax.broadcasted_iota(jnp.int32, (length, length), 0)
+    col_index = lax.broadcasted_iota(jnp.int32, (length, length), 1)
+    same = lax.shift_right_logical(keys, 1) == lax.shift_right_logical(queries, 1)
+    valid = jnp.bitwise_and(keys, 1) == 1
+    return same & (col_index <= row_index) & (valid | (col_index == row_index))
+
+
+def head_probs(query, keys, allowed):
+    scores = lax.dot_general(
+        query, keys, (((1,), (1,)), ((), ())), preferred_element_type=F32
+    )
+    scores = jnp.where(allowed, scores * SCORE_SCALE, MASKED_SCORE)
+    shifted = jnp.exp(scores - jnp.max(scores, axis=-1, keepdims=True))
+    return shifted / jnp.sum(shifted, axis=-1, keepdims=True)
+
+
+def attend_kernel(
+    x_ref, gain_ref, w_ref, cos_ref, sin_ref, row_ref, col_ref, cot_ref,
+    normed_ref, heads_ref, attended_ref, cot_out,
+    local_sem, send_sems, recv_sems,
+):
+    at = pl.program_id(0)
+    place = plane_position()
+    rep, core, own, across, down, _ = place
+    sender = Sender(send_sems, recv_sems)
+    move = Gather(sender, cot_ref, cot_out, local_sem, place)
+
+    @pl.when(at == 0)
+    def _():
+        meet([(rep, core, across), (rep, core, down), (rep, 1 - core, own)])
+        move.begin()
+
+    @pl.when(at == 5)
+    def _():
+        move.relay()
+
+    @pl.when(at == 7)
+    def _():
+        move.finish()
+        sender.finish()
+
+    @pl.loop(0, x_ref.shape[1] // 32)
+    def _(t):
+        rows = pl.ds(pl.multiple_of(t * 32, 32), 32)
+        x = x_ref[0, rows].astype(F32)
+        normed_ref[0, rows] = (x * row_scale(x) * gain_ref[...]).astype(BF16)
+
+    projected = dot_f32(normed_ref[0], w_ref[...])
+    heads = turn(projected, cos_ref, sin_ref, False).astype(BF16)
+    heads_ref[0] = heads
+    allowed = allowed_pairs(row_ref, col_ref)
+    keys = heads[:, GROUPS * HD : (GROUPS + 1) * HD]
+    values = heads[:, (GROUPS + 1) * HD :]
+    parts = []
+    for h in range(GROUPS):
+        probs = head_probs(heads[:, h * HD : (h + 1) * HD], keys, allowed)
+        parts.append(dot_f32(probs.astype(BF16), values))
+    attended_ref[0] = jnp.concatenate(parts, axis=1).astype(BF16)
+
+
+def attend(hidden, gain, qkv, tables, codes, cotangent, collective_id):
+    members, length, width = hidden.shape
+    wide = qkv.shape[1]
+    q_wide = GROUPS * HD
+
+    def one(columns):
+        return pl.BlockSpec((1, length, columns), lambda i: (i, 0, 0))
+
+    def fixed(*shape):
+        return pl.BlockSpec(shape, lambda i: (0,) * len(shape))
+
+    return pl.pallas_call(
+        attend_kernel,
+        grid=(members,),
+        out_shape=[
+            jax.ShapeDtypeStruct((members, length, width), BF16),
+            jax.ShapeDtypeStruct((members, length, wide), BF16),
+            jax.ShapeDtypeStruct((members, length, q_wide), BF16),
+            jax.ShapeDtypeStruct((8,) + cotangent.shape, BF16),
+        ],
+        in_specs=[
+            one(width), fixed(1, width), fixed(width, wide), fixed(length, wide),
+            fixed(length, wide), pl.BlockSpec((1, 1, length), lambda i: (i, 0, 0)), one(1), VM,
+        ],
+        out_specs=[one(width), one(wide), one(q_wide), HBM],
+        scratch_shapes=[
+            pltpu.SemaphoreType.DMA,
+            pltpu.SemaphoreType.DMA((13,)),
+            pltpu.SemaphoreType.DMA((13,)),
+        ],
+        compiler_params=params(collective_id, 60),
+        cost_estimate=link_cost(40),
+    )(hidden, gain, qkv, *tables, codes[:, None, :], codes[:, :, None], cotangent)
+
+
+def attend_back_kernel(
+    out_grad_ref, w_ref, heads_ref, attended_ref, cos_ref, sin_ref, row_ref, col_ref,
+    grad_ref, w_grad_ref, total,
+):
+    at = pl.program_id(0)
+    out_grad = out_grad_ref[0]
+    heads = heads_ref[0]
+    attended_grad = lax.dot_general(
+        out_grad, w_ref[...], (((1,), (1,)), ((), ())), preferred_element_type=F32
+    ).astype(BF16)
+    term = lax.dot_general(
+        attended_ref[0], out_grad, (((0,), (0,)), ((), ())), preferred_element_type=F32
+    )
+
+    @pl.when(at == 0)
+    def _():
+        total[...] = term
+
+    @pl.when(at > 0)
+    def _():
+        total[...] = total[...] + term
+
+    @pl.when(at == pl.num_programs(0) - 1)
+    def _():
+        w_grad_ref[...] = total[...].astype(BF16)
+
+    allowed = allowed_pairs(row_ref, col_ref)
+    keys = heads[:, GROUPS * HD : (GROUPS + 1) * HD]
+    values = heads[:, (GROUPS + 1) * HD :]
+    grads = []
+    key_grad, value_grad = None, None
+    for h in range(GROUPS):
+        lanes = slice(h * HD, (h + 1) * HD)
+        query, head_grad = heads[:, lanes], attended_grad[:, lanes]
+        probs = head_probs(query, keys, allowed)
+        prob_grad = lax.dot_general(
+            head_grad, values, (((1,), (1,)), ((), ())), preferred_element_type=F32
+        )
+        row_dot = jnp.sum(probs * prob_grad, axis=-1, keepdims=True)
+        score_grad = (probs * (prob_grad - row_dot)).astype(BF16)
+        grads.append(dot_f32(score_grad, keys) * SCORE_SCALE)
+        key_part = lax.dot_general(
+            score_grad, query, (((0,), (0,)), ((), ())), preferred_element_type=F32
+        )
+        value_part = lax.dot_general(
+            probs.astype(BF16), head_grad, (((0,), (0,)), ((), ())), preferred_element_type=F32
+        )
+        key_grad = key_part if key_grad is None else key_grad + key_part
+        value_grad = value_part if value_grad is None else value_grad + value_part
+    grads += [key_grad * SCORE_SCALE, value_grad]
+    grad_ref[0] = turn(jnp.concatenate(grads, axis=1), cos_ref, sin_ref, True).astype(BF16)
+
+
+def attend_back(out_grad, out_rows, heads, attended, tables, codes):
+    members, length, width = out_grad.shape
+    wide, q_wide = heads.shape[2], attended.shape[2]
+
+    def one(columns):
+        return pl.BlockSpec((1, length, columns), lambda i: (i, 0, 0))
+
+    def fixed(*shape):
+        return pl.BlockSpec(shape, lambda i: (0,) * len(shape))
+
+    return pl.pallas_call(
+        attend_back_kernel,
+        grid=(members,),
+        out_shape=[
+            jax.ShapeDtypeStruct((members, length, wide), BF16),
+            jax.ShapeDtypeStruct((q_wide, width), BF16),
+        ],
+        in_specs=[
+            one(width), fixed(q_wide, width), one(wide), one(q_wide), fixed(length, wide),
+            fixed(length, wide), pl.BlockSpec((1, 1, length), lambda i: (i, 0, 0)), one(1),
+        ],
+        out_specs=[one(wide), fixed(q_wide, width)],
+        scratch_shapes=[pltpu.VMEM((q_wide, width), F32)],
+        compiler_params=pltpu.CompilerParams(vmem_limit_bytes=48 << 20),
+        cost_estimate=link_cost(25),
+    )(out_grad, out_rows, heads, attended, *tables, codes[:, None, :], codes[:, :, None])
+
+
 def cast_rows_kernel(x_ref, out_ref):
     out_ref[...] = x_ref[0, 0].astype(F32)
 
@@ -1070,32 +1336,46 @@
     gain_mlp = gains[1].astype(F32)
     ff = gate_up.shape[1] // 2
 
-    hidden_all = hidden_low.astype(F32)
-    normed_one = (hidden_all * row_scale(hidden_all) * gain_attn).astype(BF16)
-    projected = dot_f32(normed_one, qkv)
     cos_table, sin_table = rope_tables(length, HD)
-    cos_heads = cos_table[None, :, None, :]
-    sin_heads = sin_table[None, :, None, :]
-    per_seq = projected.reshape(members, length, GROUPS + 2, HD)
-    queries = rotate(per_seq[:, :, :GROUPS], cos_heads, sin_heads).astype(BF16)
-    keys = rotate(per_seq[:, :, GROUPS : GROUPS + 1], cos_heads, sin_heads).astype(BF16)[:, :, 0]
-    values = per_seq[:, :, GROUPS + 1].astype(BF16)
-
-    segments, validity = codes // 2, codes % 2
-    row_index = jnp.arange(length, dtype=jnp.int32)[:, None]
-    col_index = jnp.arange(length, dtype=jnp.int32)[None, :]
-    allowed = (
-        (segments[:, :, None] == segments[:, None, :])
-        & (col_index <= row_index)
-        & ((validity[:, None, :] == 1) | (col_index == row_index))
-    )[:, None]
-    scores = jnp.einsum("stgd,sud->sgtu", queries, keys, preferred_element_type=F32) * SCORE_SCALE
-    scores = jnp.where(allowed, scores, MASKED_SCORE)
-    shifted = jnp.exp(scores - jnp.max(scores, axis=-1, keepdims=True))
-    probs = shifted / jnp.sum(shifted, axis=-1, keepdims=True)
-    probs_low = probs.astype(BF16)
-    attended = jnp.einsum("sgtu,sud->stgd", probs_low, values, preferred_element_type=F32)
-    attended = attended.reshape(tokens, q_width).astype(BF16)
+    if kernels:
+        plain = jnp.ones((length, HD), F32)
+        tables = (
+            jnp.concatenate([cos_table] * (2 * (GROUPS + 1)) + [plain], axis=1),
+            jnp.concatenate([sin_table] * (2 * (GROUPS + 1)) + [plain * 0.0], axis=1),
+        )
+        normed_one, heads, attended, mlp_out_grad = attend(
+            hidden_low.reshape(members, length, width), gain_attn[None], qkv, tables, codes,
+            mlp_out_low, 9,
+        )
+        normed_one = normed_one.reshape(tokens, width)
+        mlp_out_grad = mlp_out_grad.reshape(tokens, width)
+        attended = attended.reshape(tokens, q_width)
+    else:
+        hidden_all = hidden_low.astype(F32)
+        normed_one = (hidden_all * row_scale(hidden_all) * gain_attn).astype(BF16)
+        projected = dot_f32(normed_one, qkv)
+        cos_heads = cos_table[None, :, None, :]
+        sin_heads = sin_table[None, :, None, :]
+        per_seq = projected.reshape(members, length, GROUPS + 2, HD)
+        queries = rotate(per_seq[:, :, :GROUPS], cos_heads, sin_heads).astype(BF16)
+        keys = rotate(per_seq[:, :, GROUPS : GROUPS + 1], cos_heads, sin_heads).astype(BF16)[:, :, 0]
+        values = per_seq[:, :, GROUPS + 1].astype(BF16)
+
+        segments, validity = codes // 2, codes % 2
+        row_index = jnp.arange(length, dtype=jnp.int32)[:, None]
+        col_index = jnp.arange(length, dtype=jnp.int32)[None, :]
+        allowed = (
+            (segments[:, :, None] == segments[:, None, :])
+            & (col_index <= row_index)
+            & ((validity[:, None, :] == 1) | (col_index == row_index))
+        )[:, None]
+        scores = jnp.einsum("stgd,sud->sgtu", queries, keys, preferred_element_type=F32) * SCORE_SCALE
+        scores = jnp.where(allowed, scores, MASKED_SCORE)
+        shifted = jnp.exp(scores - jnp.max(scores, axis=-1, keepdims=True))
+        probs = shifted / jnp.sum(shifted, axis=-1, keepdims=True)
+        probs_low = probs.astype(BF16)
+        attended = jnp.einsum("sgtu,sud->stgd", probs_low, values, preferred_element_type=F32)
+        attended = attended.reshape(tokens, q_width).astype(BF16)
     (attn_branch,) = scattered([attended], w_output, False, 2)
 
     hidden = hidden_in[0].astype(F32)
@@ -1104,7 +1384,9 @@
     middle = hidden + RESIDUAL_SCALE * attn_branch
     scale_two = row_scale(middle)
     unit_two = middle * scale_two
-    normed_two, mlp_out_grad = gathered([(unit_two * gain_mlp).astype(BF16), mlp_out_low], 3)
+    (normed_two,) = gathered([(unit_two * gain_mlp).astype(BF16)], 3)
+    if not kernels:
+        (mlp_out_grad,) = gathered([mlp_out_low], 3)
     gate_up_proj = dot_f32(normed_two, gate_up)
     gate_proj, up_proj = gate_up_proj[:, :ff], gate_up_proj[:, ff:]
     sigma = jax.nn.sigmoid(gate_proj)
@@ -1126,46 +1408,56 @@
     middle_grad = result_grad + middle_part
 
     attn_out_low = (RESIDUAL_SCALE * middle_grad).astype(BF16)
-    down_spread = spread_planes(after(down_w_piece, normed_two_grad))
-    (attn_out_grad,) = gathered([attn_out_low], 5)
-    attended_grad = contract_cols(attn_out_grad, row_block(w_output, subs)).astype(BF16)
-    output_w_grad = contract_rows(attended, attn_out_grad).astype(BF16)
-    heads_grad = attended_grad.reshape(members, length, GROUPS, HD)
-    prob_grad = jnp.einsum("stgd,sud->sgtu", heads_grad, values, preferred_element_type=F32)
-    row_dot = jnp.sum(probs * prob_grad, axis=-1, keepdims=True)
-    score_grad = (probs * (prob_grad - row_dot)).astype(BF16)
-    query_grad = (
-        jnp.einsum("sgtu,sud->stgd", score_grad, keys, preferred_element_type=F32) * SCORE_SCALE
-    )
-    key_grad = (
-        jnp.einsum("sgtu,stgd->sud", score_grad, queries, preferred_element_type=F32) * SCORE_SCALE
-    )
-    value_grad = jnp.einsum("sgtu,stgd->sud", probs_low, heads_grad, preferred_element_type=F32)
-    qkv_grad = jnp.concatenate(
-        [
-            rotate(query_grad, cos_heads, -sin_heads),
-            rotate(key_grad[:, :, None], cos_heads, -sin_heads),
-            value_grad[:, :, None],
-        ],
-        axis=2,
-    )
-    qkv_grad = qkv_grad.reshape(tokens, q_width + 2 * k_width).astype(BF16)
-    qkv_tied = after(qkv_grad, output_w_grad, down_spread)
-    (normed_one_grad,) = scattered([qkv_tied], qkv, True, 6)
-    qkv_grad = after(qkv_grad, normed_one_grad, gate_sum)
+    passed = [KeepJob(down_w_piece)] if kernels else []
+    attn_out_grad, *passed = gathered([attn_out_low], 5, passed)
+    down_spread = spread_planes(passed[0] if kernels else down_w_piece)
+    if kernels:
+        qkv_grad, output_w_grad = attend_back(
+            attn_out_grad.reshape(members, length, width), row_block(w_output, subs), heads,
+            attended.reshape(members, length, q_width), tables, codes,
+        )
+        qkv_grad = qkv_grad.reshape(tokens, q_width + 2 * k_width)
+    else:
+        attended_grad = contract_cols(attn_out_grad, row_block(w_output, subs)).astype(BF16)
+        output_w_grad = contract_rows(attended, attn_out_grad).astype(BF16)
+        heads_grad = attended_grad.reshape(members, length, GROUPS, HD)
+        prob_grad = jnp.einsum("stgd,sud->sgtu", heads_grad, values, preferred_element_type=F32)
+        row_dot = jnp.sum(probs * prob_grad, axis=-1, keepdims=True)
+        score_grad = (probs * (prob_grad - row_dot)).astype(BF16)
+        query_grad = (
+            jnp.einsum("sgtu,sud->stgd", score_grad, keys, preferred_element_type=F32) * SCORE_SCALE
+        )
+        key_grad = (
+            jnp.einsum("sgtu,stgd->sud", score_grad, queries, preferred_element_type=F32) * SCORE_SCALE
+        )
+        value_grad = jnp.einsum("sgtu,stgd->sud", probs_low, heads_grad, preferred_element_type=F32)
+        qkv_grad = jnp.concatenate(
+            [
+                rotate(query_grad, cos_heads, -sin_heads),
+                rotate(key_grad[:, :, None], cos_heads, -sin_heads),
+                value_grad[:, :, None],
+            ],
+            axis=2,
+        )
+        qkv_grad = qkv_grad.reshape(tokens, q_width + 2 * k_width).astype(BF16)
+    qkv_tied = after(qkv_grad, output_w_grad)
+    gate_job = [ExchangeJob(gate_sum)] if kernels else []
+    normed_one_grad, *gate_piece = scattered([qkv_tied], qkv, True, 6, gate_job)
+    qkv_grad = after(qkv_grad, normed_one_grad)
     qkv_w_grad = contract_rows(normed_one, qkv_grad).astype(BF16)
     gain_attn_grad, hidden_part = norm_backward(normed_one_grad, scale_one, unit_one, gain_attn)
     input_grad = (middle_grad + hidden_part).astype(BF16)
 
-    mixed_tied = after(mixed_act, normed_one_grad, qkv_w_grad)
+    mixed_tied = after(mixed_act, normed_one_grad, qkv_w_grad, down_spread)
     last_jobs = []
     if kernels:
         up_job = SumJob(
-            [up_w_grad, qkv_w_grad], 4, 2, reps, {1: (0, 1), 2: (2, 3), 3: (4, 5), 4: (6, 7, 8)}
-        )
-        output_job = SumJob([output_w_grad], 1, 1, reps, {4: (0, 1)})
-        last_jobs = [ExchangeJob(gate_sum), up_job, output_job]
-        last_jobs += [HandJob(up_job, reps), HandJob(output_job, reps)]
+            [up_w_grad, qkv_w_grad], 4, 4, reps,
+            {1: range(4), 2: range(4, 8), 3: range(8, 12), 4: range(12, 17)},
+        )
+        output_job = SumJob([output_w_grad], 1, 2, reps, {4: range(3)})
+        last_jobs = [KeepJob(gate_piece[0]), up_job, output_job]
+        last_jobs += [HandJob(up_job, reps, 2), HandJob(output_job, reps, 2)]
     mlp_branch, *last = scattered([mixed_tied], w_down, False, 7, last_jobs)
     result = middle + RESIDUAL_SCALE * mlp_branch
 
@@ -1185,7 +1477,7 @@
     statistics = jnp.sqrt(tally[2 * width : 2 * width + 5] / (tally[2 * width + 5] * width))
 
     if kernels:
-        gate_piece, _, _, up_handed, output_handed = last
+        gate_piece, up_handed, output_handed = last
         gate_spread = spread_planes(gate_piece)
         down_out = cast_rows(down_spread)
         output_out = cast_rows(output_handed.reshape((2, 2) + output_handed.shape[3:]))

time: 911 us -> 849 us (0.932)
  Pallas kernels: 625 us -> 665 us
  matrix products: 126 us -> 93.5 us
  waiting for transfers between devices: 47 us -> 22.7 us
  other arithmetic: 50.1 us -> 27.8 us
  local copies, waits for them, and re-layouts: 36.4 us -> 20.6 us
    pallas_call x0 -> x2, Pallas kernels: none -> 77.4 us  [the longest x1 45.8 us: attend(): pl.pallas_call(attend_kernel, grid=(members,), out_shape=[jax.ShapeDtypeS...]
    pallas_call x2, Pallas kernels: 113 us -> 81.1 us  [gather_plane(): pl.pallas_call(functools.partial(gather_kernel, count, jobs), out_shape=[...]
    reduce_scatter x2, waiting for transfers between devices: 24.3 us -> 0.01 us  [sum_planes(): return lax.psum_scatter(term, 'rep', scatter_dimension=0, tiled=True)]
    convert_element_type x3 -> x1, other arithmetic: 15.2 us -> 1.4 us  [shards(): normed_two, = gathered([(unit_two * gain_mlp).astype(BF16)], 3)]
    dot_general x5 -> x0, matrix products: 13.1 us -> none  [the longest x1 4.97 us: shards(): jnp.einsum('stgd,sud->sgtu', heads_grad, values, preferred_element_type=F32)]
    dot_general x2 -> x1, matrix products: 28.6 us -> 22.1 us  [contract_cols(): return jnp.einsum('sb,ab->sa', left, right, preferred_element_type=F32)]
    dot_general x2 -> x1, matrix products: 27.8 us -> 21.5 us  [dot_f32(): return jnp.dot(left, right, preferred_element_type=F32)]
    dot_general x5 -> x4, matrix products: 51.3 us -> 49.9 us  [contract_rows(): return jnp.einsum('sa,sb->ab', left, right, preferred_element_type=F32)]
  transfers between devices with their start and end apart: 5 -> 5, of which waited for: 2 -> 2; matrix products, arithmetic and copies ran while one was open for 17% -> 11% of each run, Pallas kernels for 39% -> 48%
where the time goes in v4:
time: 849 us; the launch traced here: 845 us
  Pallas kernels  665 us (78%)
  matrix products  93.5 us (11%)
  other arithmetic  27.8 us (3%)
  waiting for transfers between devices  22.7 us (3%)
  local copies, waits for them, and re-layouts  20.6 us (2%)
  between operations  15.1 us (2%)
    pallas_call x4, Pallas kernels, product_scatter(): pl.pallas_call(functools.partial(product_scatter_kernel, turned, count, j...  357 us
    pallas_call x2, Pallas kernels, gather_plane(): pl.pallas_call(functools.partial(gather_kernel, count, jobs), out_shape=[...  81.1 us
    pallas_call x1, Pallas kernels, start_plane(): pl.pallas_call(start_kernel, out_shape=[jax.ShapeDtypeStruct(s, d) for s,...  64.9 us
    dot_general x4, matrix products, contract_rows(): return jnp.einsum('sa,sb->ab', left, right, preferred_element_type=F32)  49.9 us
    pallas_call x1, Pallas kernels, attend(): pl.pallas_call(attend_kernel, grid=(members,), out_shape=[jax.ShapeDtypeS...  45.8 us
    pallas_call x1, Pallas kernels, attend_back(): pl.pallas_call(attend_back_kernel, grid=(members,), out_shape=[jax.ShapeD...  31.6 us
    pallas_call x1, Pallas kernels, quarter_columns(): pl.pallas_call(quarter_kernel, out_shape=jax.ShapeDtypeStruct((4, rows //...  27.9 us
    pallas_call x2, Pallas kernels, cast_columns(): pl.pallas_call(cast_columns_kernel, grid=(parts, cuts), out_shape=jax.Sha...  24.2 us
  transfers between devices with their start and end apart: 5, of which 2 were waited for; matrix products, arithmetic and copies ran while one was open for 11% of the time, Pallas kernels for 48%

profile of v4, /device:TPU:0, one launch (start us, length us, event | category | flops | bytes accessed | tf_op | source)
XLA Modules:
  0.0 844.7 jit_solution(12128807053800665429)
XLA Ops:
  7.2 27.9 %shard_map.220 = bf16[4,128,2048]{2,1,0:T(8,128)(2,1)} custom-call(bf16[512,8192]{1,0:T(8,128)(2,1)} %gate_ref.1, bf16[512,8192]{1,0:T(8,128)(2,1)} %up_ref.1), custom_call_target="tpu_custom_call" | custom-call | bytes 82500000 | tf_op jit(solution)/shard_map/pallas_call | solution.py:636
  37.0 64.9 %shard_map.221 = (bf16[8,256,2048]{2,1,0:T(8,128)(2,1)}, s32[8,1,256]{2,1,0:T(1,128)}, bf16[4,2,512]{2,1,0:T(2,128)(2,1)}, bf16[4,512,256]{2,1,0:T(8,128)(2,1)},...) custom-call(bf16[256,2048]{1,0:T(8,128)(2,1)} %bitcast.65, s32[1,256]{1,0:T(1,128)} %get-tuple-element.92.code_ref, ...), custom_call_target="tpu_custom_call" | custom-call | bytes 198000000 | tf_op jit(solution)/shard_map/pallas_call | solution.py:719
  110.4 45.8 %shard_map.222 = (bf16[8,256,2048]{2,1,0:T(8,128)(2,1)}, bf16[8,256,384]{2,1,0:T(8,128)(2,1)}, bf16[8,256,256]{2,1,0:T(8,128)(2,1)}, bf16[8,256,2048]{2,1,0:T(8,128)(2,1)}) custom-call(bf16[8,256,2048]{2,1,0:T(8,128)(2,1)} %get-tuple-element.42.x_ref, f32[1,2048]{1,0:T(1,128)} %bitcast.84, bf16[2048,384]{1,0:T(8,128)(2,1)} %bitcast.67, ...), custom_call_target="tpu_custom_call" | custom-call | bytes 132000000 | tf_op jit(solution)/shard_map/pallas_call | solution.py:982
  156.2 42.3 %shard_map.223 = f32[256,2048]{1,0:T(8,128)} custom-call(bf16[2048,256]{1,0:T(8,128)(2,1)} %bitcast.61, bf16[512,2048]{1,0:T(8,128)(2,1)} %refs_1_.2), custom_call_target="tpu_custom_call" | custom-call | bytes 145200000 | tf_op jit(solution)/shard_map/pallas_call | solution.py:869
  202.0 40.5 %shard_map.224 = bf16[8,256,2048]{2,1,0:T(8,128)(2,1)} custom-call(bf16[256,2048]{1,0:T(8,128)(2,1)} %multiply_convert_fusion.4.refs_0_), custom_call_target="tpu_custom_call" | custom-call | bytes 132000000 | tf_op jit(solution)/shard_map/pallas_call | solution.py:585
  242.5 21.5 %fusion.23 = f32[2048,2048]{1,0:T(8,128)S(1)} fusion(bf16[2048,2048]{1,0:T(8,128)(2,1)} %bitcast.71, bf16[2048,2048]{1,0:T(8,128)(2,1)} %bitcast.74), kind=kOutput, calls=%fused_computation.64 | convolution fusion | flops 17179869184 | bytes 33554432 | tf_op jit(solution)/shard_map/dot_general | solution.py:51
  272.2 13.6 %convolution_convert_fusion = bf16[1024,2048]{1,0:T(8,128)(2,1)} fusion(bf16[2048,1024]{1,0:T(8,128)(2,1)S(1)} %multiply_convert_fusion.2.refs_0_, bf16[2048,2048]{1,0:T(8,128)(2,1)} %bitcast.90), kind=kOutput, calls=%fused_computation.7 | convolution fusion | flops 8592031744 | bytes 16777216 | tf_op jit(solution)/shard_map/sa,sb->ab/dot_general | solution.py:55
  285.9 22.1 %multiply_convert_fusion = (bf16[2048,1024]{1,0:T(8,128)(2,1)}, bf16[2048,1024]{1,0:T(8,128)(2,1)S(1)}) fusion(f32[2048,2048]{1,0:T(8,128)} %copy-done.12, bf16[2048,2048]{1,0:T(8,128)(2,1)} %bitcast.91, bf16[2048,2048]{1,0:T(8,128)(2,1)} %refs_1_.3, s32[]{:T(128)S(6)} %select_n.17), kind=kOutput, calls=%fused_computation | convolution fusion | flops 8617197568 | bytes 37748740 | tf_op jit(solution)/shard_map/sb,ab->sa/dot_general | solution.py:59
  307.9 13.0 %convolution_convert_fusion.2 = bf16[2048,1024]{1,0:T(8,128)(2,1)S(1)} fusion(bf16[2048,2048]{1,0:T(8,128)(2,1)} %bitcast.72, bf16[2048,1024]{1,0:T(8,128)(2,1)S(1)} %get-tuple-element.51.refs_0_), kind=kOutput, calls=%fused_computation.9 | convolution fusion | flops 8592031744 | bytes 16777216 | tf_op jit(solution)/shard_map/sa,sb->ab/dot_general | solution.py:55
  323.5 14.2 %convolution_convert_fusion.1.refs_3_ = bf16[2048,1024]{1,0:T(8,128)(2,1)} fusion(bf16[2048,2048]{1,0:T(8,128)(2,1)} %bitcast.73, bf16[2048,1024]{1,0:T(8,128)(2,1)} %get-tuple-element.84.refs_1_), kind=kOutput, calls=%fused_computation.8 | convolution fusion | flops 8592031744 | bytes 16777216 | tf_op jit(solution)/shard_map/sa,sb->ab/dot_general | solution.py:55
  337.7 48.3 %shard_map.225 = f32[256,2048]{1,0:T(8,128)} custom-call(bf16[2048,1024]{1,0:T(8,128)(2,1)} %copy-done.16, bf16[2048,1024]{1,0:T(8,128)(2,1)} %get-tuple-element.84.refs_1_, bf16[2048,2048]{1,0:T(8,128)(2,1)} %bitcast.75), custom_call_target="tpu_custom_call" | custom-call | bytes 145200000 | tf_op jit(solution)/shard_map/pallas_call | solution.py:869
  390.3 40.6 %shard_map.226 = (bf16[8,256,2048]{2,1,0:T(8,128)(2,1)}, bf16[256,2048]{1,0:T(8,128)(2,1)}) custom-call(bf16[256,2048]{1,0:T(8,128)(2,1)} %multiply_convert_fusion.3.refs_0_, bf16[256,2048]{1,0:T(8,128)(2,1)} %reduce-scatter.3.cloned.1.call-done.refs_1_), custom_call_target="tpu_custom_call" | custom-call | bytes 132000000 | tf_op jit(solution)/shard_map/pallas_call | solution.py:585
  433.1 31.6 %shard_map.227 = (bf16[8,256,384]{2,1,0:T(8,128)(2,1)}, bf16[256,2048]{1,0:T(8,128)(2,1)S(1)}) custom-call(bf16[8,256,2048]{2,1,0:T(8,128)(2,1)} %get-tuple-element.52.out_grad_ref, bf16[256,2048]{1,0:T(8,128)(2,1)S(1)} %constant_dynamic-slice_fusion.w_ref, bf16[8,256,384]{2,1,0:T(8,128)(2,1)} %get-tuple-element.53.heads_ref, ...), custom_call_target="tpu_custom_call" | custom-call | bytes 82500000 | tf_op jit(solution)/shard_map/pallas_call | solution.py:1069
  465.6 50.8 %shard_map.228 = (f32[256,2048]{1,0:T(8,128)}, bf16[4,128,1024]{2,1,0:T(8,128)(2,1)}) custom-call(bf16[2048,384]{1,0:T(8,128)(2,1)} %bitcast.78, bf16[2048,384]{1,0:T(8,128)(2,1)} %bitcast.68, bf16[512,1024]{1,0:T(8,128)(2,1)} %reduce-scatter.5.cloned.1.call-done.refs_2_), custom_call_target="tpu_custom_call" | custom-call | bytes 145200000 | tf_op jit(solution)/shard_map/pallas_call | solution.py:869
  516.5 9.1 %convolution_convert_fusion.3.refs_4_ = bf16[2048,384]{1,0:T(8,128)(2,1)} fusion(bf16[2048,2048]{1,0:T(8,128)(2,1)} %bitcast.89, bf16[2048,384]{1,0:T(8,128)(2,1)S(1)} %bitcast.79), kind=kOutput, calls=%fused_computation.16 | convolution fusion | flops 3222011904 | bytes 11534336 | tf_op jit(solution)/shard_map/sa,sb->ab/dot_general | solution.py:55
  527.3 215.4 %shard_map.229 = (f32[256,2048]{1,0:T(8,128)}, bf16[4,128,1024]{2,1,0:T(8,128)(2,1)}, bf16[2,2,4,256,1408]{4,3,2,1,0:T(8,128)(2,1)}, bf16[2,2,1,128,2048]{4,3,2,1,0:T(8,128)(2,1)}) custom-call(bf16[2048,1024]{1,0:T(8,128)(2,1)} %copy-done.11, bf16[2048,2048]{1,0:T(8,128)(2,1)} %refs_1_.3, bf16[4,128,1024]{2,1,0:T(8,128)(2,1)} %get-tuple-element.62.refs_2_, ...), custom_call_target="tpu_custom_call" | custom-call | bytes 145200000 | tf_op jit(solution)/shard_map/pallas_call | solution.py:869
  743.4 10.8 %shard_map.234 = f32[512,8192]{1,0:T(8,128)} custom-call(bf16[2,2,4,256,1408]{4,3,2,1,0:T(8,128)(2,1)} %get-tuple-element.64.q_ref.kv_ref.x_ref), custom_call_target="tpu_custom_call" | custom-call | bytes 26400000 | tf_op jit(solution)/shard_map/pallas_call | solution.py:1116
  754.1 4.3 shard_map.231
  758.5 11.0 %shard_map.235 = f32[2048,2048]{1,0:T(8,128)} custom-call(bf16[4,2,256,2048]{3,2,1,0:T(8,128)(2,1)} %bitcast.70), custom_call_target="tpu_custom_call" | custom-call | bytes 26400000 | tf_op jit(solution)/shard_map/pallas_call | solution.py:1093
  769.5 5.3 multiply_reduce_fusion
  779.5 12.9 %shard_map.230 = f32[40,128]{1,0:T(8,128)S(1)} custom-call(f32[40,128]{1,0:T(8,128)S(1)} %pad_bitcast_fusion.x_ref), custom_call_target="tpu_custom_call" | custom-call | bytes 33000000 | tf_op jit(solution)/shard_map/pallas_call | solution.py:1198
  799.0 4.7 fusion.16
  803.7 20.8 %all-gather.10.cloned.1.call-done = bf16[32,128,1024]{2,1,0:T(8,128)(2,1)} async-done(((bf16[4,128,1024]{2,1,0:T(8,128)(2,1)}), bf16[32,128,1024]{2,1,0:T(8,128)(2,1)}) %all-gather.10.cloned.1.call-update) | async-done | bytes 8388624 | tf_op jit(solution)/shard_map/all_gather | solution.py:1248
  824.5 13.5 %shard_map.233 = f32[512,8192]{1,0:T(8,128)} custom-call(bf16[4,2,4,128,1024]{4,3,2,1,0:T(8,128)(2,1)} %bitcast.69), custom_call_target="tpu_custom_call" | custom-call | bytes 26400000 | tf_op jit(solution)/shard_map/pallas_call | solution.py:1116
  (107 shorter events, 44.8 us)
Async XLA Ops:
  7.2 235.3 %all-gather.6.cloned.1.call-start = ((), (), s32[]{:S(2)}) async-start(), calls=%async_computation.2 | async-start | bytes 10485760 | tf_op jit(solution)/shard_map/all_gather | solution.py:1328
  35.2 355.1 %reduce-scatter.3.cloned.1.call-start = ((), (), s32[]{:S(2)}) async-start(), calls=%async_computation.3 | async-start | bytes 5242880 | tf_op jit(solution)/shard_map/reduce_scatter | solution.py:1243
  104.0 2.7 copy-start.19
  104.0 2.7 copy-start.20
  107.1 2.1 copy-start.13
  156.2 42.3 %copy-start.9 = (bf16[1,256,2048]{2,1,0:T(8,128)(2,1)S(1)}, bf16[1,256,2048]{2,1,0:T(8,128)(2,1)}, u32[]{:S(2)}) copy-start(bf16[1,256,2048]{2,1,0:T(8,128)(2,1)} %param.13) | copy-start | bytes 3145732
  200.6 187.9 %copy-start.6 = (f32[256,2048]{1,0:T(8,128)}, f32[256,2048]{1,0:T(8,128)S(1)}, u32[]{:S(2)}) copy-start(f32[256,2048]{1,0:T(8,128)S(1)} %get-tuple-element.83) | copy-start | bytes 6291460
  264.0 6.2 copy-start.12
  270.2 2.0 copy-start.11
  285.8 179.8 %reduce-scatter.5.cloned.1.call-start = ((), (), s32[]{:S(2)}) async-start(), calls=%async_computation.4 | async-start | bytes 5242880 | tf_op jit(solution)/shard_map/reduce_scatter | solution.py:1243
  307.9 13.1 %copy-start.16 = (bf16[2048,1024]{1,0:T(8,128)(2,1)}, bf16[2048,1024]{1,0:T(8,128)(2,1)S(1)}, u32[]{:S(2)}) copy-start(bf16[2048,1024]{1,0:T(8,128)(2,1)S(1)} %get-tuple-element.51.refs_0_) | copy-start | bytes 12582916
  323.5 203.9 %all-gather.8.cloned.1.call-start = ((), (), s32[]{:S(2)}) async-start(), calls=%async_computation.5 | async-start | bytes 9437184 | tf_op jit(solution)/shard_map/all_gather | solution.py:1248
  386.0 2.4 copy-start.8
  386.1 2.6 copy-start.14
  431.0 2.1 copy-start.3
  431.0 2.1 copy-start.5
  431.0 393.5 %all-gather.10.cloned.1.call-start = ((), (), s32[]{:S(2)}) async-start(), calls=%async_computation.6 | async-start | bytes 9437184 | tf_op jit(solution)/shard_map/all_gather | solution.py:1248
  465.6 50.8 %copy-start.17 = (bf16[8,256,384]{2,1,0:T(8,128)(2,1)S(1)}, bf16[8,256,384]{2,1,0:T(8,128)(2,1)}, u32[]{:S(2)}) copy-start(bf16[8,256,384]{2,1,0:T(8,128)(2,1)} %get-tuple-element.54) | copy-start | bytes 4718596
  527.3 215.4 %copy-start.28 = (s32[1,256]{1,0:T(1,128)S(1)}, s32[1,256]{1,0:T(1,128)}, u32[]{:S(2)}) copy-start(s32[1,256]{1,0:T(1,128)} %param.15) | copy-start | bytes 3076
  758.5 11.0 %copy-start.7 = (f32[256,2048]{1,0:T(8,128)S(1)}, f32[256,2048]{1,0:T(8,128)}, u32[]{:S(2)}) copy-start(f32[256,2048]{1,0:T(8,128)} %copy-done.6) | copy-start | bytes 6291460
  758.5 11.0 %copy-start.10 = (bf16[1,256,2048]{2,1,0:T(8,128)(2,1)S(1)}, bf16[1,256,2048]{2,1,0:T(8,128)(2,1)}, u32[]{:S(2)}) copy-start(bf16[1,256,2048]{2,1,0:T(8,128)(2,1)} %param.13) | copy-start | bytes 3145732
  758.5 11.0 %copy-start.23 = (f32[1,256]{1,0:T(1,128)S(1)}, f32[1,256]{1,0:T(1,128)}, u32[]{:S(2)}) copy-start(f32[1,256]{1,0:T(1,128)} %get-tuple-element.91) | copy-start | bytes 3076
  769.5 5.3 copy-start.15
  769.5 5.3 copy-start.21
  (10 other events, 13.5 us)
Sparse Core Ops, SparseCore 0:
  35.3 149.8 all-gather.5
  285.9 77.0 reduce-scatter.2
  366.0 77.2 reduce-scatter.4
  444.7 82.5 all-gather.7
  742.9 81.5 all-gather.9

commit v5 on v4

--- a/solution.py
+++ b/solution.py
@@ -2,6 +2,7 @@
 
 import jax
 import jax.numpy as jnp
+import numpy as np
 from jax import lax
 from jax.experimental import pallas as pl
 from jax.experimental.pallas import tpu as pltpu
@@ -32,6 +33,15 @@
     frequency = ROPE_BASE ** (-(jnp.arange(half_size, dtype=F32) * 2.0 / head_size))
     angles = jnp.arange(length, dtype=F32)[:, None] * frequency[None, :]
     return (jnp.cos(angles), jnp.sin(angles))
+
+
+def turn_tables(length):
+    half = HD // 2
+    frequency = (ROPE_BASE ** (-2.0 * np.arange(half) / HD)).astype(np.float32)
+    angles = np.arange(length, dtype=np.float32)[:, None] * frequency[None, :]
+    plain = np.zeros((length, HD))
+    angles = np.concatenate([angles] * (2 * (GROUPS + 1)) + [plain], axis=1).astype(np.float64)
+    return jnp.asarray(np.cos(angles), F32), jnp.asarray(np.sin(angles), F32)
 
 
 def rotate(tensor, cos_table, sin_table):
@@ -183,22 +193,34 @@
         self.mine.start()
 
     def relay(self):
+        self.relay_first()
+        self.relay_second()
+
+    def relay_first(self):
         self.across_low.wait_recv()
         self.corner_low.start()
         self.swap_near[0].start()
         self.down_high.wait_recv()
         self.corner_high.start()
         self.swap_near[1].start()
+
+    def relay_second(self):
         self.across_high.wait_recv()
         self.swap_near[2].start()
         self.down_low.wait_recv()
         self.swap_near[3].start()
 
     def finish(self):
+        self.pass_corner()
+        self.arrive()
+
+    def pass_corner(self):
         self.corner_low.wait_recv()
         self.swap_corner[0].start()
         self.corner_high.wait_recv()
         self.swap_corner[1].start()
+
+    def arrive(self):
         for swap in [self.swap_own] + self.swap_near + self.swap_corner:
             swap.wait_recv()
         self.mine.wait()
@@ -399,7 +421,7 @@
         skewed(self.rep, self.reps, self.count, self.add, i)
 
     def stage(self, n):
-        if n == 1:
+        if n == 0:
             self.prime()
         if n in self.steps:
             for i in self.steps[n]:
@@ -599,6 +621,10 @@
     )(*blocks, *jobs.arrays)
 
 
+def column_source(ref, rows, block, width):
+    return ref.at[rows, pl.ds(pl.multiple_of(block * width, width), width)]
+
+
 def quarter_kernel(gate_ref, up_ref, out_ref, room, local_sems, send_sems, recv_sems):
     rep, core, own, across, down, corner = plane_position()
     peers = (corner, across, down)
@@ -606,22 +632,18 @@
     rows = out_ref.shape[1]
     width = out_ref.shape[2] // 2
     mine = pl.ds(pl.multiple_of(rep * rows, rows), rows)
-
-    def source(ref, block):
-        columns = pl.ds(pl.multiple_of((block * 2 + core) * width, width), width)
-        return ref.at[mine, columns]
-
     sender = Sender(send_sems, recv_sems)
-    for peer in peers:
-        for k, ref in enumerate((gate_ref, up_ref)):
-            target = out_ref.at[own, :, pl.ds(k * width, width)]
-            sender.send(source(ref, peer), target, (rep, core, peer))
     local = []
     for k, ref in enumerate((gate_ref, up_ref)):
-        target = out_ref.at[own, :, pl.ds(k * width, width)]
-        copy = Bounce(source(ref, own), target, room.at[k], local_sems.at[k])
+        columns = pl.ds(k * width, width)
+        target = out_ref.at[own, :, columns]
+        source = column_source(ref, mine, own * 2 + core, width)
+        copy = Bounce(source, target, room.at[:, columns], local_sems.at[k])
         copy.start()
         local.append(copy)
+        for peer in peers:
+            source = column_source(ref, mine, peer * 2 + core, width)
+            sender.send(source, target, (rep, core, peer))
     for copy in local:
         copy.turn()
     for copy in sender.copies:
@@ -633,13 +655,14 @@
 
 def quarter_columns(w_gate, w_up, reps, collective_id):
     rows, columns = w_gate.shape
+    shape = (rows // reps, columns // 4)
     return pl.pallas_call(
         quarter_kernel,
-        out_shape=jax.ShapeDtypeStruct((4, rows // reps, columns // 4), BF16),
-        in_specs=[HBM, HBM],
+        out_shape=jax.ShapeDtypeStruct((4,) + shape, BF16),
+        in_specs=[HBM] * 2,
         out_specs=HBM,
         scratch_shapes=[
-            pltpu.VMEM((2, rows // reps, columns // 8), BF16),
+            pltpu.VMEM(shape, BF16),
             pltpu.SemaphoreType.DMA((2, 2)),
             pltpu.SemaphoreType.DMA((6,)),
             pltpu.SemaphoreType.DMA((6,)),
@@ -650,89 +673,275 @@
 
 
 def start_kernel(
-    x_ref, code_ref, gain_ref, q_ref, k_ref, v_ref,
-    x_out, code_out, gain_out, q_out, k_out, v_out,
-    q_room, k_room, v_room, bounce_sems, local_sems, send_sems, recv_sems,
+    x_ref, code_ref, gain_ref, q_ref, k_ref, v_ref, x_out, code_out, gain_out, heads_out,
+    room, bounce_sems, local_sems, send_sems, recv_sems,
 ):
     place = plane_position()
     rep, core, own, across, down, corner = place
     peers = (corner, across, down)
-    meet([(rep, core, peer) for peer in peers] + [(rep, 1 - core, peer) for peer in peers]
-         + [(rep, 1 - core, own)])
+    others = [(rep, core, peer) for peer in peers] + [(rep, 1 - core, peer) for peer in peers]
+    others.append((rep, 1 - core, own))
+    meet(others)
     sender = Sender(send_sems, recv_sems)
-    direct, local, bounced = [], [], []
-
-    def keep(src, dst):
-        copy = pltpu.make_async_copy(src, dst, local_sems.at[1 + len(local)])
+    move = Gather(sender, x_ref, x_out, local_sems.at[0], place)
+    direct = [sender.make(gain_ref, gain_out.at[own], (rep, core, peer)) for peer in peers]
+    slot = code_out.at[core * 4 + own]
+    direct += [sender.make(code_ref, slot, device) for device in others]
+    whole = pl.ds(0, q_ref.shape[0])
+    q_wide, pair = GROUPS * HD, 2 * HD
+
+    def fetch(ref, at, width, blocks):
+        columns = pl.ds(at, width)
+        target = heads_out.at[own, :, columns]
+        source = column_source(ref, whole, blocks[0], width)
+        bounced = Bounce(source, target, room.at[:, columns], bounce_sems.at[min(at, 1)])
+        sends = []
+        for block, peer in zip(blocks[1:], peers):
+            source = column_source(ref, whole, block, width)
+            sends.append(sender.make(source, target, (rep, core, peer)))
+        return bounced, sends
+
+    def swap(at):
+        columns = pl.ds(at, pair)
+        copies = [sender.make(room.at[:, columns], heads_out.at[own, :, columns], others[-1])]
+        for peer in peers:
+            ref = heads_out.at[peer, :, columns]
+            copies.append(sender.make(ref, ref, others[-1]))
+        return copies
+
+    q_kept, q_sends = fetch(q_ref, 0, q_wide, [block * 2 + core for block in (own,) + peers])
+    direct += q_sends
+    first = len(sender.copies)
+    sides = []
+    for ref, at in ((k_ref, q_wide), (v_ref, q_wide + pair)):
+        kept, sends = fetch(ref, at, pair, (own,) + peers)
+        swaps = swap(at)
+        del sender.copies[first + len(sends) :]
+        sides.append((kept, sends, swaps, swap(2 * q_wide + pair - at)))
+        del sender.copies[first:]
+    local = [
+        pltpu.make_async_copy(gain_ref, gain_out.at[own], local_sems.at[1]),
+        pltpu.make_async_copy(code_ref, slot, local_sems.at[2]),
+    ]
+    move.begin()
+    for copy in direct + local + [q_kept]:
         copy.start()
-        local.append(copy)
-
-    def bounce(src, dst, room):
-        copy = Bounce(src, dst, room, bounce_sems.at[len(bounced)])
-        copy.start()
-        bounced.append(copy)
-
-    def columns(ref, block, width):
-        return ref.at[:, pl.ds(pl.multiple_of(block * width, width), width)]
-
-    def weights():
-        for peer in peers:
-            there = (rep, core, peer)
-            direct.append(sender.send(gain_ref, gain_out.at[own], there))
-            direct.append(sender.send(columns(q_ref, peer * 2 + core, 256), q_out.at[own], there))
-            direct.append(sender.send(columns(k_ref, peer, 128), k_out.at[own], there))
-            direct.append(sender.send(columns(v_ref, peer, 128), v_out.at[own], there))
-            direct.append(sender.send(code_ref, code_out.at[core * 4 + own], there))
-            other = (rep, 1 - core, peer)
-            direct.append(sender.send(code_ref, code_out.at[core * 4 + own], other))
-        direct.append(sender.send(code_ref, code_out.at[core * 4 + own], (rep, 1 - core, own)))
-        keep(gain_ref, gain_out.at[own])
-        bounce(columns(q_ref, own * 2 + core, 256), q_out.at[own], q_room)
-        bounce(columns(k_ref, own, 128), k_out.at[own], k_room)
-        bounce(columns(v_ref, own, 128), v_out.at[own], v_room)
-        keep(code_ref, code_out.at[core * 4 + own])
-
-    move = Gather(sender, x_ref, x_out, local_sems.at[0], place)
-    move.begin()
-    weights()
-    for copy in bounced:
-        copy.turn()
+    for side, (kept, sends, swaps, _) in enumerate(sides):
+
+        @pl.when(core == side)
+        def _(kept=kept, sends=sends, swaps=swaps):
+            for copy in [kept] + sends:
+                copy.start()
+            kept.turn()
+            swaps[0].start()
+
+    q_kept.turn()
     move.relay()
+    for side, (kept, sends, swaps, _) in enumerate(sides):
+
+        @pl.when(core == side)
+        def _(kept=kept, sends=sends, swaps=swaps):
+            for copy, passed in zip(sends, swaps[1:]):
+                copy.wait_recv()
+                passed.start()
+
     move.finish()
     for copy in direct:
         copy.wait_recv()
+    for side, (kept, sends, swaps, arrivals) in enumerate(sides):
+
+        @pl.when(core == side)
+        def _(kept=kept, sends=sends, swaps=swaps, arrivals=arrivals):
+            for copy in arrivals:
+                copy.wait_recv()
+            for copy in sends + swaps:
+                copy.wait_send()
+            kept.wait()
+
     sender.finish()
-    for copy in local + bounced:
+    for copy in local + [q_kept]:
         copy.wait()
 
 
 def start_plane(hidden, codes, gains, w_query, w_key, w_value, collective_id):
-    rows = w_query.shape[0]
+    heads = (w_query.shape[0], (GROUPS + 4) * HD)
     shapes = [
         ((8,) + hidden.shape, BF16),
         ((8,) + codes.shape, jnp.int32),
         ((4,) + gains.shape, BF16),
-        ((4, rows, GROUPS * HD), BF16),
-        ((4, rows, 2 * HD), BF16),
-        ((4, rows, 2 * HD), BF16),
+        ((4,) + heads, BF16),
     ]
     return pl.pallas_call(
         start_kernel,
         out_shape=[jax.ShapeDtypeStruct(s, d) for s, d in shapes],
-        in_specs=[VM] + [HBM] * 5,
-        out_specs=[HBM] * 6,
+        in_specs=[VM] * 3 + [HBM] * 3,
+        out_specs=[HBM] * 4,
         scratch_shapes=[
-            pltpu.VMEM((rows, GROUPS * HD), BF16),
-            pltpu.VMEM((rows, 2 * HD), BF16),
-            pltpu.VMEM((rows, 2 * HD), BF16),
-            pltpu.SemaphoreType.DMA((3, 2)),
+            pltpu.VMEM(heads, BF16),
+            pltpu.SemaphoreType.DMA((2, 2)),
             pltpu.SemaphoreType.DMA((3,)),
-            pltpu.SemaphoreType.DMA((32,)),
-            pltpu.SemaphoreType.DMA((32,)),
+            pltpu.SemaphoreType.DMA((40,)),
+            pltpu.SemaphoreType.DMA((40,)),
         ],
         compiler_params=params(collective_id, 60),
         cost_estimate=link_cost(60),
     )(hidden, codes, gains, w_query, w_key, w_value)
+
+
+def mlp_kernel(
+    x_ref, w_hbm, grad_hbm, x_out, product_out, act_out, down_out,
+    x_all, w_ref, product, act, grad, total, down,
+    w_sems, grad_sems, store_sems, down_sems, local_sem, send_sems, recv_sems,
+):
+    place = plane_position()
+    rep, core, own, across, down_at, corner = place
+    rows = x_ref.shape[0]
+    ff = act.shape[2]
+    tile, depth = 512, 256
+    tiles = ff // tile
+    here, there = core * 4, (1 - core) * 4
+    order = [here + own, there + own, here + across, here + down_at]
+    order += [there + across, there + down_at, here + corner, there + corner]
+    loads = []
+    for t in range(tiles):
+        for k in range(2):
+            columns = pl.ds(k * ff + t * tile, tile)
+            load = pltpu.make_async_copy(w_hbm.at[:, columns], w_ref.at[:, columns], w_sems.at[t, k])
+            load.start()
+            loads.append(load)
+    grads = [
+        pltpu.make_async_copy(grad_hbm.at[block], grad.at[n % 2], grad_sems.at[n])
+        for n, block in enumerate(order)
+    ]
+    grads[0].start()
+    grads[1].start()
+    meet([(rep, core, across), (rep, core, down_at), (rep, 1 - core, own)])
+    sender = Sender(send_sems, recv_sems)
+    move = Gather(sender, x_ref, x_all, local_sem, place)
+    move.begin()
+    pending, finals = [], []
+
+    def piece(x, slot, at):
+        gate = dot_f32(x, w_ref[:, pl.ds(at, tile)])
+        up = dot_f32(x, w_ref[:, pl.ds(ff + at, tile)])
+        product[slot, :, pl.ds(at, tile)] = gate
+        product[slot, :, pl.ds(ff + at, tile)] = up
+        act[slot, :, pl.ds(at, tile)] = (gate * jax.nn.sigmoid(gate) * up).astype(BF16)
+
+    def compute(n):
+        block, slot = order[n], n % 2
+        if n >= 2:
+            for store in pending[n - 2][:2]:
+                store.wait()
+        for t in range(tiles):
+            if n == 0:
+                loads[2 * t].wait()
+                loads[2 * t + 1].wait()
+            piece(x_all[block], slot, t * tile)
+        mine = pl.ds(pl.multiple_of(block * rows, rows), rows)
+        stores = [
+            pltpu.make_async_copy(product.at[slot], product_out.at[mine], store_sems.at[n, 0]),
+            pltpu.make_async_copy(act.at[slot], act_out.at[mine], store_sems.at[n, 1]),
+            pltpu.make_async_copy(x_all.at[block], x_out.at[block], store_sems.at[n, 2]),
+        ]
+        for store in stores:
+            store.start()
+        pending.append(stores)
+
+    def weigh(n):
+        slot = n % 2
+        grads[n].wait()
+
+        def term(at):
+            return lax.dot_general(
+                act[slot, :, pl.ds(at, depth)], grad[slot], (((0,), (0,)), ((), ())),
+                preferred_element_type=F32,
+            )
+
+        if n == 7:
+            for r in range(ff // depth):
+                at = pl.ds(r * depth, depth)
+                down[at] = (total[at] + term(r * depth)).astype(BF16)
+                final = pltpu.make_async_copy(down.at[at], down_out.at[at], down_sems.at[r])
+                final.start()
+                finals.append(final)
+        else:
+
+            @pl.loop(0, ff // depth)
+            def _(r):
+                start = pl.multiple_of(r * depth, depth)
+                at = pl.ds(start, depth)
+                total[at] = term(start) if n == 0 else total[at] + term(start)
+
+        if n + 2 < 8:
+            grads[n + 2].start()
+
+    move.mine.wait()
+    compute(0)
+    move.swap_own.wait_recv()
+    compute(1)
+    move.relay_first()
+    weigh(0)
+    weigh(1)
+    move.relay_second()
+    compute(2)
+    compute(3)
+    for swap in move.swap_near:
+        swap.wait_recv()
+    weigh(2)
+    compute(4)
+    move.pass_corner()
+    weigh(3)
+    compute(5)
+    weigh(4)
+    compute(6)
+    weigh(5)
+    for swap in move.swap_corner:
+        swap.wait_recv()
+    compute(7)
+    weigh(6)
+    weigh(7)
+    for k, stores in enumerate(pending):
+        for store in stores if k >= 6 else stores[2:]:
+            store.wait()
+    for final in finals:
+        final.wait()
+    sender.finish()
+
+
+def mlp_plane(x, w, grad, collective_id):
+    rows, width = x.shape
+    wide = w.shape[1]
+    ff = wide // 2
+    return pl.pallas_call(
+        mlp_kernel,
+        out_shape=[
+            jax.ShapeDtypeStruct((8, rows, width), BF16),
+            jax.ShapeDtypeStruct((8 * rows, wide), F32),
+            jax.ShapeDtypeStruct((8 * rows, ff), BF16),
+            jax.ShapeDtypeStruct((ff, width), BF16),
+        ],
+        in_specs=[VM, HBM, HBM],
+        out_specs=[HBM] * 4,
+        scratch_shapes=[
+            pltpu.VMEM((8, rows, width), BF16),
+            pltpu.VMEM((width, wide), BF16),
+            pltpu.VMEM((2, rows, wide), F32),
+            pltpu.VMEM((2, rows, ff), BF16),
+            pltpu.VMEM((2, rows, width), BF16),
+            pltpu.VMEM((ff, width), F32),
+            pltpu.VMEM((ff, width), BF16),
+            pltpu.SemaphoreType.DMA((ff // 512, 2)),
+            pltpu.SemaphoreType.DMA((8,)),
+            pltpu.SemaphoreType.DMA((8, 3)),
+            pltpu.SemaphoreType.DMA((ff // 256,)),
+            pltpu.SemaphoreType.DMA,
+            pltpu.SemaphoreType.DMA((13,)),
+            pltpu.SemaphoreType.DMA((13,)),
+        ],
+        compiler_params=params(collective_id, 60),
+        cost_estimate=link_cost(50),
+    )(x, w, grad)
 
 
 def product_scatter_kernel(turned, count, jobs, *refs):
@@ -940,13 +1149,21 @@
         meet([(rep, core, across), (rep, core, down), (rep, 1 - core, own)])
         move.begin()
 
-    @pl.when(at == 5)
+    @pl.when(at == 2)
     def _():
-        move.relay()
+        move.relay_first()
+
+    @pl.when(at == 4)
+    def _():
+        move.relay_second()
+
+    @pl.when(at == 6)
+    def _():
+        move.pass_corner()
 
     @pl.when(at == 7)
     def _():
-        move.finish()
+        move.arrive()
         sender.finish()
 
     @pl.loop(0, x_ref.shape[1] // 32)
@@ -955,7 +1172,12 @@
         x = x_ref[0, rows].astype(F32)
         normed_ref[0, rows] = (x * row_scale(x) * gain_ref[...]).astype(BF16)
 
-    projected = dot_f32(normed_ref[0], w_ref[...])
+    wide = dot_f32(normed_ref[0], w_ref[...])
+    keys_at, values_at = GROUPS * HD, (GROUPS + 2) * HD
+    pieces = [wide[:, :keys_at]]
+    for at in (keys_at, values_at):
+        pieces.append(jnp.where(core == 0, wide[:, at : at + HD], wide[:, at + HD : at + 2 * HD]))
+    projected = jnp.concatenate(pieces, axis=1)
     heads = turn(projected, cos_ref, sin_ref, False).astype(BF16)
     heads_ref[0] = heads
     allowed = allowed_pairs(row_ref, col_ref)
@@ -970,8 +1192,7 @@
 
 def attend(hidden, gain, qkv, tables, codes, cotangent, collective_id):
     members, length, width = hidden.shape
-    wide = qkv.shape[1]
-    q_wide = GROUPS * HD
+    wide, q_wide = (GROUPS + 2) * HD, GROUPS * HD
 
     def one(columns):
         return pl.BlockSpec((1, length, columns), lambda i: (i, 0, 0))
@@ -989,7 +1210,7 @@
             jax.ShapeDtypeStruct((8,) + cotangent.shape, BF16),
         ],
         in_specs=[
-            one(width), fixed(1, width), fixed(width, wide), fixed(length, wide),
+            one(width), fixed(1, width), fixed(*qkv.shape), fixed(length, wide),
             fixed(length, wide), pl.BlockSpec((1, 1, length), lambda i: (i, 0, 0)), one(1), VM,
         ],
         out_specs=[one(width), one(wide), one(q_wide), HBM],
@@ -1111,7 +1332,7 @@
 def cast_columns(handed, columns):
     parts, subs, owners, rows, _ = handed.shape
     wide = owners * subs * columns
-    cuts = 4
+    cuts = max(1, rows // 64)
     block = (1, subs, owners, rows // cuts, columns)
     return pl.pallas_call(
         cast_columns_kernel,
@@ -1119,6 +1340,7 @@
         out_shape=jax.ShapeDtypeStruct((parts * rows, wide), F32),
         in_specs=[pl.BlockSpec(block, lambda r, h: (r, 0, 0, h, 0))],
         out_specs=pl.BlockSpec((rows // cuts, wide), lambda r, h: (r * cuts + h, 0)),
+        compiler_params=pltpu.CompilerParams(vmem_limit_bytes=48 << 20),
         cost_estimate=link_cost(8),
     )(handed)
 
@@ -1309,23 +1531,15 @@
     mlp_out_low = (RESIDUAL_SCALE * result_grad).astype(BF16)
     if kernels:
         quarter = quarter_columns(w_gate, w_up, reps, 0)
+        gate_up = lax.all_gather(quarter, "rep", axis=1, tiled=True).reshape(width, -1)
         hidden_tied = after(hidden_in[0], quarter)
-        hidden_low, codes, gains, q_cols, k_cols, v_cols = start_plane(
+        hidden_low, codes, gains, heads_all = start_plane(
             hidden_tied, codes, gains, w_query, w_key, w_value, 1
         )
         hidden_low = hidden_low.reshape(tokens, width)
         codes = codes.reshape(members, length)
         gains = jnp.swapaxes(gains, 0, 1).reshape(2, width)
-        core_at = lax.axis_index("sub") * HD
-        qkv = jnp.concatenate(
-            [
-                q_cols,
-                lax.dynamic_slice_in_dim(k_cols, core_at, HD, axis=2),
-                lax.dynamic_slice_in_dim(v_cols, core_at, HD, axis=2),
-            ],
-            axis=2,
-        ).reshape(width, q_width + 2 * k_width)
-        gate_up = lax.all_gather(quarter, "rep", axis=1, tiled=True).reshape(width, -1)
+        heads_all = heads_all.reshape(width, -1)
     else:
         gains = lax.all_gather(gains, "fsdp", axis=1, tiled=True)
         codes = gather_tokens(codes)
@@ -1336,21 +1550,22 @@
     gain_mlp = gains[1].astype(F32)
     ff = gate_up.shape[1] // 2
 
-    cos_table, sin_table = rope_tables(length, HD)
     if kernels:
-        plain = jnp.ones((length, HD), F32)
-        tables = (
-            jnp.concatenate([cos_table] * (2 * (GROUPS + 1)) + [plain], axis=1),
-            jnp.concatenate([sin_table] * (2 * (GROUPS + 1)) + [plain * 0.0], axis=1),
-        )
+        tables = turn_tables(length)
         normed_one, heads, attended, mlp_out_grad = attend(
-            hidden_low.reshape(members, length, width), gain_attn[None], qkv, tables, codes,
+            hidden_low.reshape(members, length, width), gain_attn[None], heads_all, tables, codes,
             mlp_out_low, 9,
         )
         normed_one = normed_one.reshape(tokens, width)
         mlp_out_grad = mlp_out_grad.reshape(tokens, width)
         attended = attended.reshape(tokens, q_width)
+        heads_all = after(heads_all, normed_one)
+        core_at = lax.axis_index("sub") * HD
+        key_cols = lax.dynamic_slice_in_dim(heads_all, q_width + core_at, HD, axis=1)
+        value_cols = lax.dynamic_slice_in_dim(heads_all, q_width + 2 * HD + core_at, HD, axis=1)
+        qkv = jnp.concatenate([heads_all[:, :q_width], key_cols, value_cols], axis=1)
     else:
+        cos_table, sin_table = rope_tables(length, HD)
         hidden_all = hidden_low.astype(F32)
         normed_one = (hidden_all * row_scale(hidden_all) * gain_attn).astype(BF16)
         projected = dot_f32(normed_one, qkv)
@@ -1384,16 +1599,21 @@
     middle = hidden + RESIDUAL_SCALE * attn_branch
     scale_two = row_scale(middle)
     unit_two = middle * scale_two
-    (normed_two,) = gathered([(unit_two * gain_mlp).astype(BF16)], 3)
-    if not kernels:
-        (mlp_out_grad,) = gathered([mlp_out_low], 3)
-    gate_up_proj = dot_f32(normed_two, gate_up)
+    normed_own = (unit_two * gain_mlp).astype(BF16)
+    if kernels:
+        normed_two, gate_up_proj, mixed_act, down_w_grad = mlp_plane(
+            normed_own, gate_up, mlp_out_grad.reshape(members, length, width), 3
+        )
+        normed_two = normed_two.reshape(tokens, width)
+    else:
+        normed_two, mlp_out_grad = gathered([normed_own, mlp_out_low], 3)
+        gate_up_proj = dot_f32(normed_two, gate_up)
     gate_proj, up_proj = gate_up_proj[:, :ff], gate_up_proj[:, ff:]
     sigma = jax.nn.sigmoid(gate_proj)
     silu_gate = gate_proj * sigma
-    mixed_act = (silu_gate * up_proj).astype(BF16)
-
-    down_w_grad = contract_rows(mixed_act, mlp_out_grad).astype(BF16)
+    if not kernels:
+        mixed_act = (silu_gate * up_proj).astype(BF16)
+        down_w_grad = contract_rows(mixed_act, mlp_out_grad).astype(BF16)
     down_w_piece = sum_planes(down_w_grad)
     mixed_grad = contract_cols(after(mlp_out_grad, down_w_grad), row_block(w_down, subs))
     slope = sigma * (1.0 + gate_proj * (1.0 - sigma))
@@ -1441,8 +1661,8 @@
         )
         qkv_grad = qkv_grad.reshape(tokens, q_width + 2 * k_width).astype(BF16)
     qkv_tied = after(qkv_grad, output_w_grad)
-    gate_job = [ExchangeJob(gate_sum)] if kernels else []
-    normed_one_grad, *gate_piece = scattered([qkv_tied], qkv, True, 6, gate_job)
+    gate_job = [KeepJob(gate_sum)] if kernels else []
+    normed_one_grad, *gate_kept = scattered([qkv_tied], qkv, True, 6, gate_job)
     qkv_grad = after(qkv_grad, normed_one_grad)
     qkv_w_grad = contract_rows(normed_one, qkv_grad).astype(BF16)
     gain_attn_grad, hidden_part = norm_backward(normed_one_grad, scale_one, unit_one, gain_attn)
@@ -1456,8 +1676,8 @@
             {1: range(4), 2: range(4, 8), 3: range(8, 12), 4: range(12, 17)},
         )
         output_job = SumJob([output_w_grad], 1, 2, reps, {4: range(3)})
-        last_jobs = [KeepJob(gate_piece[0]), up_job, output_job]
-        last_jobs += [HandJob(up_job, reps, 2), HandJob(output_job, reps, 2)]
+        last_jobs = [up_job, output_job, ExchangeJob(gate_kept[0])]
+        last_jobs += [HandJob(up_job, reps, 4), HandJob(output_job, reps, 2)]
     mlp_branch, *last = scattered([mixed_tied], w_down, False, 7, last_jobs)
     result = middle + RESIDUAL_SCALE * mlp_branch
 

time: 849 us -> 808 us (0.952)
  matrix products: 93.5 us -> 58.9 us
  Pallas kernels: 665 us -> 654 us
    pallas_call x1 -> x2, Pallas kernels: 27.9 us -> 83.9 us  [the longest x1 55.9 us: mlp_plane(): pl.pallas_call(mlp_kernel, out_shape=[jax.ShapeDtypeStruct((8, rows, widt...]
    pallas_call x2 -> x1, Pallas kernels: 81.1 us -> 40 us  [gather_plane(): pl.pallas_call(functools.partial(gather_kernel, count, jobs), out_shape=[...]
    dot_general x1 -> x0, matrix products: 21.5 us -> none  [dot_f32(): return jnp.dot(left, right, preferred_element_type=F32)]
    pallas_call x4, Pallas kernels: 357 us -> 339 us  [product_scatter(): pl.pallas_call(functools.partial(product_scatter_kernel, turned, count, j...]
    dot_general x4 -> x3, matrix products: 49.9 us -> 36.8 us  [contract_rows(): return jnp.einsum('sa,sb->ab', left, right, preferred_element_type=F32)]
  transfers between devices with their start and end apart: 5 -> 5, of which waited for: 2 -> 2; matrix products, arithmetic and copies ran while one was open for 11% -> 12% of each run, Pallas kernels for 48% -> 44%
where the time goes in v5:
time: 808 us; the launch traced here: 799 us
  Pallas kernels  654 us (81%)
  matrix products  58.9 us (7%)
  waiting for transfers between devices  29.7 us (4%)
  other arithmetic  25.1 us (3%)
  local copies, waits for them, and re-layouts  16.1 us (2%)
  between operations  14.9 us (2%)
    pallas_call x4, Pallas kernels, product_scatter(): pl.pallas_call(functools.partial(product_scatter_kernel, turned, count, j...  339 us
    pallas_call x1, Pallas kernels, start_plane(): pl.pallas_call(start_kernel, out_shape=[jax.ShapeDtypeStruct(s, d) for s,...  59.5 us
    pallas_call x1, Pallas kernels, mlp_plane(): pl.pallas_call(mlp_kernel, out_shape=[jax.ShapeDtypeStruct((8, rows, widt...  55.9 us
    pallas_call x1, Pallas kernels, attend(): pl.pallas_call(attend_kernel, grid=(members,), out_shape=[jax.ShapeDtypeS...  46.4 us
    pallas_call x1, Pallas kernels, gather_plane(): pl.pallas_call(functools.partial(gather_kernel, count, jobs), out_shape=[...  40 us
    dot_general x3, matrix products, contract_rows(): return jnp.einsum('sa,sb->ab', left, right, preferred_element_type=F32)  36.8 us
    pallas_call x1, Pallas kernels, attend_back(): pl.pallas_call(attend_back_kernel, grid=(members,), out_shape=[jax.ShapeD...  31.8 us
    all_gather x2, waiting for transfers between devices, spread_planes(): spread = lax.all_gather(piece, ('rep', 'sub'), axis=0, tiled=False)  29.6 us
  transfers between devices with their start and end apart: 5, of which 2 were waited for; matrix products, arithmetic and copies ran while one was open for 12% of the time, Pallas kernels for 44%

profile of v5, /device:TPU:0, one launch (start us, length us, event | category | flops | bytes accessed | tf_op | source)
XLA Modules:
  0.0 798.9 jit_solution(5207071898499998577)
XLA Ops:
  7.2 28.0 %shard_map.238 = bf16[4,128,2048]{2,1,0:T(8,128)(2,1)} custom-call(bf16[512,8192]{1,0:T(8,128)(2,1)} %gate_ref.1, bf16[512,8192]{1,0:T(8,128)(2,1)} %up_ref.1), custom_call_target="tpu_custom_call" | custom-call | bytes 82500000 | tf_op jit(solution)/shard_map/pallas_call | solution.py:659
  37.0 59.5 %shard_map.239 = (bf16[8,256,2048]{2,1,0:T(8,128)(2,1)}, s32[8,1,256]{2,1,0:T(1,128)}, bf16[4,2,512]{2,1,0:T(2,128)(2,1)}, bf16[4,512,512]{2,1,0:T(8,128)(2,1)}) custom-call(bf16[256,2048]{1,0:T(8,128)(2,1)} %bitcast.63, s32[1,256]{1,0:T(1,128)} %get-tuple-element.100.code_ref, bf16[2,512]{1,0:T(2,128)(2,1)} %pad_maximum_fusion.1.gain_ref, ...), custom_call_target="tpu_custom_call" | custom-call | bytes 198000000 | tf_op jit(solution)/shard_map/pallas_call | solution.py:774
  101.2 46.4 %shard_map.240 = (bf16[8,256,2048]{2,1,0:T(8,128)(2,1)}, bf16[8,256,384]{2,1,0:T(8,128)(2,1)}, bf16[8,256,256]{2,1,0:T(8,128)(2,1)}, bf16[8,256,2048]{2,1,0:T(8,128)(2,1)}) custom-call(bf16[8,256,2048]{2,1,0:T(8,128)(2,1)} %get-tuple-element.45.x_ref, f32[1,2048]{1,0:T(1,128)} %bitcast.79, bf16[2048,512]{1,0:T(8,128)(2,1)} %bitcast.67, ...), custom_call_target="tpu_custom_call" | custom-call | bytes 132000000 | tf_op jit(solution)/shard_map/pallas_call | solution.py:1203
  147.6 42.0 %shard_map.241 = f32[256,2048]{1,0:T(8,128)} custom-call(bf16[2048,256]{1,0:T(8,128)(2,1)} %bitcast.57, bf16[512,2048]{1,0:T(8,128)(2,1)} %refs_1_.2), custom_call_target="tpu_custom_call" | custom-call | bytes 145200000 | tf_op jit(solution)/shard_map/pallas_call | solution.py:1078
  192.9 55.9 %shard_map.242 = (bf16[8,256,2048]{2,1,0:T(8,128)(2,1)}, f32[2048,2048]{1,0:T(8,128)}, bf16[2048,1024]{1,0:T(8,128)(2,1)}, bf16[1024,2048]{1,0:T(8,128)(2,1)}) custom-call(bf16[256,2048]{1,0:T(8,128)(2,1)} %multiply_convert_fusion.3.x_ref, bf16[2048,2048]{1,0:T(8,128)(2,1)} %bitcast.61, bf16[8,256,2048]{2,1,0:T(8,128)(2,1)} %get-tuple-element.50.grad_hbm), custom_call_target="tpu_custom_call" | custom-call | bytes 165000000 | tf_op jit(solution)/shard_map/pallas_call | solution.py:916
  248.9 22.1 %multiply_convert_fusion = (bf16[2048,1024]{1,0:T(8,128)(2,1)}, bf16[2048,1024]{1,0:T(8,128)(2,1)S(1)}) fusion(f32[2048,2048]{1,0:T(8,128)} %get-tuple-element.54, bf16[2048,2048]{1,0:T(8,128)(2,1)} %bitcast.70, bf16[2048,2048]{1,0:T(8,128)(2,1)} %refs_1_.3, s32[]{:T(128)S(6)} %select_n.18), kind=kOutput, calls=%fused_computation | convolution fusion | flops 8617197568 | bytes 37748740 | tf_op jit(solution)/shard_map/sb,ab->sa/dot_general | solution.py:69
  271.0 13.0 %convolution_convert_fusion.1 = bf16[2048,1024]{1,0:T(8,128)(2,1)S(1)} fusion(bf16[2048,2048]{1,0:T(8,128)(2,1)} %bitcast.85, bf16[2048,1024]{1,0:T(8,128)(2,1)S(1)} %get-tuple-element.56.refs_0_), kind=kOutput, calls=%fused_computation.6 | convolution fusion | flops 8592031744 | bytes 16777216 | tf_op jit(solution)/shard_map/sa,sb->ab/dot_general | solution.py:65
  286.6 14.2 %convolution_convert_fusion.refs_2_ = bf16[2048,1024]{1,0:T(8,128)(2,1)} fusion(bf16[2048,2048]{1,0:T(8,128)(2,1)} %bitcast.86, bf16[2048,1024]{1,0:T(8,128)(2,1)} %get-tuple-element.90.refs_1_), kind=kOutput, calls=%fused_computation.5 | convolution fusion | flops 8592031744 | bytes 16777216 | tf_op jit(solution)/shard_map/sa,sb->ab/dot_general | solution.py:65
  300.8 48.1 %shard_map.243 = f32[256,2048]{1,0:T(8,128)} custom-call(bf16[2048,1024]{1,0:T(8,128)(2,1)} %copy-done.13, bf16[2048,1024]{1,0:T(8,128)(2,1)} %get-tuple-element.90.refs_1_, bf16[2048,2048]{1,0:T(8,128)(2,1)} %bitcast.62), custom_call_target="tpu_custom_call" | custom-call | bytes 145200000 | tf_op jit(solution)/shard_map/pallas_call | solution.py:1078
  353.2 40.0 %shard_map.244 = (bf16[8,256,2048]{2,1,0:T(8,128)(2,1)}, bf16[256,2048]{1,0:T(8,128)(2,1)}) custom-call(bf16[256,2048]{1,0:T(8,128)(2,1)} %multiply_convert_fusion.2.refs_0_, bf16[256,2048]{1,0:T(8,128)(2,1)} %reduce-scatter.3.cloned.1.call-done.refs_1_), custom_call_target="tpu_custom_call" | custom-call | bytes 132000000 | tf_op jit(solution)/shard_map/pallas_call | solution.py:607
  400.1 31.8 %shard_map.245 = (bf16[8,256,384]{2,1,0:T(8,128)(2,1)}, bf16[256,2048]{1,0:T(8,128)(2,1)S(1)}) custom-call(bf16[8,256,2048]{2,1,0:T(8,128)(2,1)} %get-tuple-element.57.out_grad_ref, bf16[256,2048]{1,0:T(8,128)(2,1)S(1)} %constant_dynamic-slice_fusion.2.w_ref, bf16[8,256,384]{2,1,0:T(8,128)(2,1)} %get-tuple-element.58.heads_ref, ...), custom_call_target="tpu_custom_call" | custom-call | bytes 82500000 | tf_op jit(solution)/shard_map/pallas_call | solution.py:1290
  432.8 43.1 %shard_map.246 = (f32[256,2048]{1,0:T(8,128)}, bf16[512,1024]{1,0:T(8,128)(2,1)}) custom-call(bf16[2048,384]{1,0:T(8,128)(2,1)} %bitcast.73, bf16[2048,384]{1,0:T(8,128)(2,1)} %pad_maximum_fusion.refs_1_, bf16[512,1024]{1,0:T(8,128)(2,1)} %reduce-scatter.5.cloned.1.call-done.refs_2_), custom_call_target="tpu_custom_call" | custom-call | bytes 145200000 | tf_op jit(solution)/shard_map/pallas_call | solution.py:1078
  476.0 9.5 %convolution_convert_fusion.2.refs_3_ = bf16[2048,384]{1,0:T(8,128)(2,1)} fusion(bf16[2048,2048]{1,0:T(8,128)(2,1)} %bitcast.84, bf16[2048,384]{1,0:T(8,128)(2,1)} %bitcast.74), kind=kOutput, calls=%fused_computation.13 | convolution fusion | flops 3222011904 | bytes 11534336 | tf_op jit(solution)/shard_map/sa,sb->ab/dot_general | solution.py:65
  485.5 4.8 all-gather.8.cloned.1.call-done
  490.3 205.9 %shard_map.247 = (f32[256,2048]{1,0:T(8,128)}, bf16[4,128,1024]{2,1,0:T(8,128)(2,1)}, bf16[2,2,4,256,1408]{4,3,2,1,0:T(8,128)(2,1)}, bf16[2,2,1,128,2048]{4,3,2,1,0:T(8,128)(2,1)}) custom-call(bf16[2048,1024]{1,0:T(8,128)(2,1)} %get-tuple-element.67.refs_0_, bf16[2048,2048]{1,0:T(8,128)(2,1)} %refs_1_.3, bf16[2048,1024]{1,0:T(8,128)(2,1)} %convolution_convert_fusion.refs_2_, ...), custom_call_target="tpu_custom_call" | custom-call | bytes 145200000 | tf_op jit(solution)/shard_map/pallas_call | solution.py:1078
  696.9 10.5 %shard_map.252 = f32[512,8192]{1,0:T(8,128)} custom-call(bf16[2,2,4,256,1408]{4,3,2,1,0:T(8,128)(2,1)} %get-tuple-element.70.q_ref.kv_ref.x_ref), custom_call_target="tpu_custom_call" | custom-call | bytes 26400000 | tf_op jit(solution)/shard_map/pallas_call | solution.py:1337
  707.4 4.5 shard_map.249
  711.9 10.4 %shard_map.253 = f32[2048,2048]{1,0:T(8,128)} custom-call(bf16[4,2,256,2048]{3,2,1,0:T(8,128)(2,1)} %bitcast.65), custom_call_target="tpu_custom_call" | custom-call | bytes 26400000 | tf_op jit(solution)/shard_map/pallas_call | solution.py:1314
  722.3 5.4 multiply_reduce_fusion
  732.3 13.5 %shard_map.248 = f32[40,128]{1,0:T(8,128)S(1)} custom-call(f32[40,128]{1,0:T(8,128)S(1)} %pad_bitcast_fusion.x_ref), custom_call_target="tpu_custom_call" | custom-call | bytes 33000000 | tf_op jit(solution)/shard_map/pallas_call | solution.py:1420
  746.4 4.2 shard_map.250
  752.4 4.6 fusion.15
  757.1 24.8 %all-gather.10.cloned.1.call-done = bf16[32,128,1024]{2,1,0:T(8,128)(2,1)} async-done(((bf16[4,128,1024]{2,1,0:T(8,128)(2,1)}), bf16[32,128,1024]{2,1,0:T(8,128)(2,1)}) %all-gather.10.cloned.1.call-update) | async-done | bytes 8388624 | tf_op jit(solution)/shard_map/all_gather | solution.py:1470
  781.9 10.3 %shard_map.251 = f32[512,8192]{1,0:T(8,128)} custom-call(bf16[4,2,4,128,1024]{4,3,2,1,0:T(8,128)(2,1)} %bitcast.66), custom_call_target="tpu_custom_call" | custom-call | bytes 26400000 | tf_op jit(solution)/shard_map/pallas_call | solution.py:1337
  (79 shorter events, 31.4 us)
Async XLA Ops:
  7.2 185.7 %all-gather.6.cloned.1.call-start = ((), (), s32[]{:S(2)}) async-start(), calls=%async_computation.2 | async-start | bytes 10485760 | tf_op jit(solution)/shard_map/all_gather | solution.py:1534
  35.2 0.7 copy-start.15
  35.2 0.7 copy-start.16
  35.2 1.3 copy-start.17
  35.2 1.3 copy-start.18
  35.3 317.9 %reduce-scatter.3.cloned.1.call-start = ((), (), s32[]{:S(2)}) async-start(), calls=%async_computation.3 | async-start | bytes 5242880 | tf_op jit(solution)/shard_map/reduce_scatter | solution.py:1465
  37.0 62.9 %copy-start.8 = (bf16[1,256,2048]{2,1,0:T(8,128)(2,1)S(1)}, bf16[1,256,2048]{2,1,0:T(8,128)(2,1)}, u32[]{:S(2)}) copy-start(bf16[1,256,2048]{2,1,0:T(8,128)(2,1)} %param.18) | copy-start | bytes 3145732
  147.5 42.1 %copy-start.7 = (bf16[1,256,2048]{2,1,0:T(8,128)(2,1)S(1)}, bf16[1,256,2048]{2,1,0:T(8,128)(2,1)}, u32[]{:S(2)}) copy-start(bf16[1,256,2048]{2,1,0:T(8,128)(2,1)} %param.15) | copy-start | bytes 3145732
  248.8 184.0 %reduce-scatter.5.cloned.1.call-start = ((), (), s32[]{:S(2)}) async-start(), calls=%async_computation.4 | async-start | bytes 5242880 | tf_op jit(solution)/shard_map/reduce_scatter | solution.py:1465
  271.0 13.1 %copy-start.13 = (bf16[2048,1024]{1,0:T(8,128)(2,1)}, bf16[2048,1024]{1,0:T(8,128)(2,1)S(1)}, u32[]{:S(2)}) copy-start(bf16[2048,1024]{1,0:T(8,128)(2,1)S(1)} %get-tuple-element.56.refs_0_) | copy-start | bytes 12582916
  286.5 203.8 %all-gather.8.cloned.1.call-start = ((), (), s32[]{:S(2)}) async-start(), calls=%async_computation.5 | async-start | bytes 9437184 | tf_op jit(solution)/shard_map/all_gather | solution.py:1470
  348.9 2.4 copy-start.6
  348.9 2.6 copy-start.9
  393.2 388.7 %all-gather.10.cloned.1.call-start = ((), (), s32[]{:S(2)}) async-start(), calls=%async_computation.6 | async-start | bytes 9437184 | tf_op jit(solution)/shard_map/all_gather | solution.py:1470
  395.5 1.9 copy-start.10
  395.5 2.3 copy-start.12
  397.8 1.5 copy-start
  397.8 2.1 copy-start.1
  397.8 2.2 copy-start.2
  397.8 2.3 copy-start.3
  397.8 2.3 copy-start.5
  431.9 1.0 copy-start.4
  722.3 5.4 copy-start.11
  722.3 5.4 copy-start.14
Sparse Core Ops, SparseCore 0:
  35.4 149.8 all-gather.5
  249.0 77.0 reduce-scatter.2
  329.0 77.2 reduce-scatter.4
  407.7 82.5 all-gather.7
  696.4 85.4 all-gather.9

commit v6 on v5

--- a/solution.py
+++ b/solution.py
@@ -1115,7 +1115,7 @@
 
 
 def allowed_pairs(row_ref, col_ref):
-    keys, queries = row_ref[0], col_ref[0]
+    keys, queries = row_ref[...], col_ref[...]
     length = keys.shape[1]
     row_index = lax.broadcasted_iota(jnp.int32, (length, length), 0)
     col_index = lax.broadcasted_iota(jnp.int32, (length, length), 1)
@@ -1134,94 +1134,210 @@
 
 
 def attend_kernel(
-    x_ref, gain_ref, w_ref, cos_ref, sin_ref, row_ref, col_ref, cot_ref,
-    normed_ref, heads_ref, attended_ref, cot_out,
-    local_sem, send_sems, recv_sems,
+    x_hbm, gain_ref, w_ref, cos_ref, sin_ref, row_ref, col_ref, cot_ref, out_w_hbm,
+    out_ref, normed_hbm, heads_hbm, attended_hbm, cot_out,
+    x_buf, normed, heads_buf, attended, out_w, parts, from_core, from_across, from_down,
+    last_across, last_down, x_sems, w_sem, store_sems, local_sem,
+    core_send, core_recv, send_sems, recv_sems, cot_send, cot_recv,
 ):
-    at = pl.program_id(0)
     place = plane_position()
-    rep, core, own, across, down, _ = place
+    rep, core, own, across, down, corner = place
+    row, col = own // 2, own % 2
+    to_across, to_down, to_core = (rep, core, across), (rep, core, down), (rep, 1 - core, own)
+    length, wide = out_ref.shape
+    half = length // 2
+    low, high = pl.ds(0, half), pl.ds(half, half)
+    depth = out_w.shape[0]
+    tile = 512
+
+    def block_of(n):
+        k = n // 2
+        far_row = row + (k + 1) % 2 * (1 - 2 * row)
+        far_col = col + (1 - k // 2) * (1 - 2 * col)
+        near = n % 2
+        return (near * core + (1 - near) * (1 - core)) * 4 + far_row * 2 + far_col
+
+    def fetch(n):
+        slot = n % 2
+        return pltpu.make_async_copy(x_hbm.at[block_of(n)], x_buf.at[slot], x_sems.at[slot])
+
+    def stores(n):
+        slot, block = n % 2, block_of(n)
+        pairs = ((normed, normed_hbm), (heads_buf, heads_hbm), (attended, attended_hbm))
+        return [
+            pltpu.make_async_copy(src.at[slot], dst.at[block], store_sems.at[slot, i])
+            for i, (src, dst) in enumerate(pairs)
+        ]
+
+    def swap(k):
+        return pltpu.make_async_remote_copy(
+            src_ref=parts.at[0, k],
+            dst_ref=from_core.at[k],
+            send_sem=core_send.at[k],
+            recv_sem=core_recv.at[k],
+            device_id=to_core,
+            device_id_type=MESH,
+        )
+
+    rows_kept = pl.ds(pl.multiple_of(core * depth, depth), depth)
+    out_w_load = pltpu.make_async_copy(out_w_hbm.at[rows_kept], out_w, w_sem)
+    out_w_load.start()
+    fetch(0).start()
+    meet([to_across, to_down, to_core])
+    cot_sender = Sender(cot_send, cot_recv)
+    move = Gather(cot_sender, cot_ref, cot_out, local_sem, place)
+    move.begin()
     sender = Sender(send_sems, recv_sems)
-    move = Gather(sender, cot_ref, cot_out, local_sem, place)
-
-    @pl.when(at == 0)
-    def _():
-        meet([(rep, core, across), (rep, core, down), (rep, 1 - core, own)])
-        move.begin()
-
-    @pl.when(at == 2)
-    def _():
-        move.relay_first()
-
-    @pl.when(at == 4)
-    def _():
-        move.relay_second()
-
-    @pl.when(at == 6)
-    def _():
-        move.pass_corner()
-
-    @pl.when(at == 7)
-    def _():
-        move.arrive()
-        sender.finish()
-
-    @pl.loop(0, x_ref.shape[1] // 32)
-    def _(t):
-        rows = pl.ds(pl.multiple_of(t * 32, 32), 32)
-        x = x_ref[0, rows].astype(F32)
-        normed_ref[0, rows] = (x * row_scale(x) * gain_ref[...]).astype(BF16)
-
-    wide = dot_f32(normed_ref[0], w_ref[...])
-    keys_at, values_at = GROUPS * HD, (GROUPS + 2) * HD
-    pieces = [wide[:, :keys_at]]
-    for at in (keys_at, values_at):
-        pieces.append(jnp.where(core == 0, wide[:, at : at + HD], wide[:, at + HD : at + 2 * HD]))
-    projected = jnp.concatenate(pieces, axis=1)
-    heads = turn(projected, cos_ref, sin_ref, False).astype(BF16)
-    heads_ref[0] = heads
-    allowed = allowed_pairs(row_ref, col_ref)
-    keys = heads[:, GROUPS * HD : (GROUPS + 1) * HD]
-    values = heads[:, (GROUPS + 1) * HD :]
-    parts = []
-    for h in range(GROUPS):
-        probs = head_probs(heads[:, h * HD : (h + 1) * HD], keys, allowed)
-        parts.append(dot_f32(probs.astype(BF16), values))
-    attended_ref[0] = jnp.concatenate(parts, axis=1).astype(BF16)
-
-
-def attend(hidden, gain, qkv, tables, codes, cotangent, collective_id):
+    sent = [
+        sender.make(parts.at[1, 0, low], from_across.at[0], to_across),
+        sender.make(parts.at[1, 0, high], from_down.at[0], to_down),
+        sender.make(parts.at[1, 1, low], from_across.at[1], to_across),
+        sender.make(parts.at[1, 2, high], from_down.at[1], to_down),
+        sender.make(parts.at[1, 2, low], last_down, to_down),
+        sender.make(parts.at[1, 1, high], last_across, to_across),
+    ]
+    out_w_load.wait()
+
+    @pl.loop(0, 8)
+    def _(n):
+        slot, k = n % 2, n // 2
+        block = block_of(n)
+        fetch(n).wait()
+
+        @pl.when(n < 7)
+        def _():
+            fetch(n + 1).start()
+
+        @pl.when(n >= 2)
+        def _():
+            for store in stores(n - 2):
+                store.wait()
+
+        @pl.when(n == 3)
+        def _():
+            move.relay_first()
+
+        @pl.when(n == 5)
+        def _():
+            move.relay_second()
+
+        @pl.loop(0, length // 32)
+        def _(t):
+            rows = pl.ds(pl.multiple_of(t * 32, 32), 32)
+            x = x_buf[slot, rows].astype(F32)
+            normed[slot, rows] = (x * row_scale(x) * gain_ref[...]).astype(BF16)
+
+        projected = dot_f32(normed[slot], w_ref[...])
+        keys_at, values_at = GROUPS * HD, (GROUPS + 2) * HD
+        pieces = [projected[:, :keys_at]]
+        for at in (keys_at, values_at):
+            mine, other = projected[:, at : at + HD], projected[:, at + HD : at + 2 * HD]
+            pieces.append(jnp.where(core == 0, mine, other))
+        heads = turn(jnp.concatenate(pieces, axis=1), cos_ref, sin_ref, False).astype(BF16)
+        heads_buf[slot] = heads
+        allowed = allowed_pairs(row_ref.at[block], col_ref.at[block])
+        keys = heads[:, GROUPS * HD : (GROUPS + 1) * HD]
+        values = heads[:, (GROUPS + 1) * HD :]
+        outs = []
+        for h in range(GROUPS):
+            probs = head_probs(heads[:, h * HD : (h + 1) * HD], keys, allowed)
+            outs.append(dot_f32(probs.astype(BF16), values))
+        attended[slot] = jnp.concatenate(outs, axis=1).astype(BF16)
+        for store in stores(n):
+            store.start()
+
+        @pl.loop(0, wide // tile)
+        def _(t):
+            columns = pl.ds(pl.multiple_of(t * tile, tile), tile)
+            parts[slot, k, :, columns] = dot_f32(attended[slot], out_w[:, columns]).astype(BF16)
+
+        @pl.when(slot == 0)
+        def _():
+            swap(k).start()
+
+        @pl.when(slot == 1)
+        def _():
+            swap(k).wait_recv()
+            parts[1, k] = parts[1, k] + from_core[k]
+
+        @pl.when(n == 1)
+        def _():
+            sent[0].start()
+            sent[1].start()
+
+        @pl.when(n == 3)
+        def _():
+            sent[2].start()
+
+        @pl.when(n == 5)
+        def _():
+            sent[3].start()
+
+    sent[0].wait_recv()
+    parts[1, 2, low] = parts[1, 2, low] + from_across[0]
+    sent[4].start()
+    sent[1].wait_recv()
+    parts[1, 1, high] = parts[1, 1, high] + from_down[0]
+    sent[5].start()
+    move.pass_corner()
+    sent[2].wait_recv()
+    sent[3].wait_recv()
+    sent[4].wait_recv()
+    out_ref[low] = (
+        parts[1, 3, low].astype(F32) + from_across[1].astype(F32) + last_down[...].astype(F32)
+    )
+    sent[5].wait_recv()
+    out_ref[high] = (
+        parts[1, 3, high].astype(F32) + from_down[1].astype(F32) + last_across[...].astype(F32)
+    )
+    move.arrive()
+    cot_sender.finish()
+    for k in range(4):
+        swap(k).wait_send()
+    sender.finish()
+    for n in (6, 7):
+        for store in stores(n):
+            store.wait()
+
+
+def attend(hidden, gain, qkv, tables, codes, cotangent, w_output, collective_id):
     members, length, width = hidden.shape
     wide, q_wide = (GROUPS + 2) * HD, GROUPS * HD
-
-    def one(columns):
-        return pl.BlockSpec((1, length, columns), lambda i: (i, 0, 0))
-
-    def fixed(*shape):
-        return pl.BlockSpec(shape, lambda i: (0,) * len(shape))
-
+    half = length // 2
+    three = [(length, width), (length, wide), (length, q_wide)]
     return pl.pallas_call(
         attend_kernel,
-        grid=(members,),
-        out_shape=[
-            jax.ShapeDtypeStruct((members, length, width), BF16),
-            jax.ShapeDtypeStruct((members, length, wide), BF16),
-            jax.ShapeDtypeStruct((members, length, q_wide), BF16),
-            jax.ShapeDtypeStruct((8,) + cotangent.shape, BF16),
-        ],
-        in_specs=[
-            one(width), fixed(1, width), fixed(*qkv.shape), fixed(length, wide),
-            fixed(length, wide), pl.BlockSpec((1, 1, length), lambda i: (i, 0, 0)), one(1), VM,
-        ],
-        out_specs=[one(width), one(wide), one(q_wide), HBM],
-        scratch_shapes=[
+        out_shape=[jax.ShapeDtypeStruct((length, width), F32)]
+        + [jax.ShapeDtypeStruct((members,) + shape, BF16) for shape in three]
+        + [jax.ShapeDtypeStruct((8,) + cotangent.shape, BF16)],
+        in_specs=[HBM] + [VM] * 7 + [HBM],
+        out_specs=[VM] + [HBM] * 4,
+        scratch_shapes=[pltpu.VMEM((2, length, width), BF16)]
+        + [pltpu.VMEM((2,) + shape, BF16) for shape in three]
+        + [
+            pltpu.VMEM((q_wide, width), BF16),
+            pltpu.VMEM((2, 4, length, width), BF16),
+            pltpu.VMEM((4, length, width), BF16),
+            pltpu.VMEM((2, half, width), BF16),
+            pltpu.VMEM((2, half, width), BF16),
+            pltpu.VMEM((half, width), BF16),
+            pltpu.VMEM((half, width), BF16),
+            pltpu.SemaphoreType.DMA((2,)),
             pltpu.SemaphoreType.DMA,
+            pltpu.SemaphoreType.DMA((2, 3)),
+            pltpu.SemaphoreType.DMA,
+            pltpu.SemaphoreType.DMA((4,)),
+            pltpu.SemaphoreType.DMA((4,)),
+            pltpu.SemaphoreType.DMA((6,)),
+            pltpu.SemaphoreType.DMA((6,)),
             pltpu.SemaphoreType.DMA((13,)),
             pltpu.SemaphoreType.DMA((13,)),
         ],
         compiler_params=params(collective_id, 60),
-        cost_estimate=link_cost(40),
-    )(hidden, gain, qkv, *tables, codes[:, None, :], codes[:, :, None], cotangent)
+        cost_estimate=link_cost(70),
+    )(
+        hidden, gain, qkv, *tables, codes[:, None, :], codes[:, :, None], cotangent, w_output
+    )
 
 
 def attend_back_kernel(
@@ -1250,7 +1366,7 @@
     def _():
         w_grad_ref[...] = total[...].astype(BF16)
 
-    allowed = allowed_pairs(row_ref, col_ref)
+    allowed = allowed_pairs(row_ref.at[0], col_ref.at[0])
     keys = heads[:, GROUPS * HD : (GROUPS + 1) * HD]
     values = heads[:, (GROUPS + 1) * HD :]
     grads = []
@@ -1552,9 +1668,9 @@
 
     if kernels:
         tables = turn_tables(length)
-        normed_one, heads, attended, mlp_out_grad = attend(
+        attn_branch, normed_one, heads, attended, mlp_out_grad = attend(
             hidden_low.reshape(members, length, width), gain_attn[None], heads_all, tables, codes,
-            mlp_out_low, 9,
+            mlp_out_low, w_output, 9,
         )
         normed_one = normed_one.reshape(tokens, width)
         mlp_out_grad = mlp_out_grad.reshape(tokens, width)
@@ -1591,7 +1707,8 @@
         probs_low = probs.astype(BF16)
         attended = jnp.einsum("sgtu,sud->stgd", probs_low, values, preferred_element_type=F32)
         attended = attended.reshape(tokens, q_width).astype(BF16)
-    (attn_branch,) = scattered([attended], w_output, False, 2)
+    if not kernels:
+        (attn_branch,) = scattered([attended], w_output, False, 2)
 
     hidden = hidden_in[0].astype(F32)
     scale_one = row_scale(hidden)

time: 808 us -> 799 us (0.989)
  Pallas kernels: 654 us -> 641 us
    pallas_call x4 -> x3, Pallas kernels: 339 us -> 296 us  [product_scatter(): pl.pallas_call(functools.partial(product_scatter_kernel, turned, count, j...]
    pallas_call x1, Pallas kernels: 46.4 us -> 75.2 us  [attend(): pl.pallas_call(attend_kernel, out_shape=[jax.ShapeDtypeStruct((length, wi...]
  transfers between devices with their start and end apart: 5 -> 5, of which waited for: 2 -> 3; matrix products, arithmetic and copies ran while one was open for 12% -> 12% of each run, Pallas kernels for 44% -> 43%
where the time goes in v6:
time: 799 us; the launch traced here: 789 us
  Pallas kernels  641 us (80%)
  matrix products  59.3 us (7%)
  waiting for transfers between devices  32.3 us (4%)
  other arithmetic  25.1 us (3%)
  local copies, waits for them, and re-layouts  16 us (2%)
  between operations  14.9 us (2%)
    pallas_call x3, Pallas kernels, product_scatter(): pl.pallas_call(functools.partial(product_scatter_kernel, turned, count, j...  296 us
    pallas_call x1, Pallas kernels, attend(): pl.pallas_call(attend_kernel, out_shape=[jax.ShapeDtypeStruct((length, wi...  75.2 us
    pallas_call x1, Pallas kernels, start_plane(): pl.pallas_call(start_kernel, out_shape=[jax.ShapeDtypeStruct(s, d) for s,...  59.5 us
    pallas_call x1, Pallas kernels, mlp_plane(): pl.pallas_call(mlp_kernel, out_shape=[jax.ShapeDtypeStruct((8, rows, widt...  56.2 us
    pallas_call x1, Pallas kernels, gather_plane(): pl.pallas_call(functools.partial(gather_kernel, count, jobs), out_shape=[...  40.6 us
    dot_general x3, matrix products, contract_rows(): return jnp.einsum('sa,sb->ab', left, right, preferred_element_type=F32)  36.8 us
    pallas_call x1, Pallas kernels, attend_back(): pl.pallas_call(attend_back_kernel, grid=(members,), out_shape=[jax.ShapeD...  31.8 us
    pallas_call x1, Pallas kernels, quarter_columns(): pl.pallas_call(quarter_kernel, out_shape=jax.ShapeDtypeStruct((4,) + shap...  28 us
  transfers between devices with their start and end apart: 5, of which 3 were waited for; matrix products, arithmetic and copies ran while one was open for 12% of the time, Pallas kernels for 43%

profile of v6, /device:TPU:0, one launch (start us, length us, event | category | flops | bytes accessed | tf_op | source)
XLA Modules:
  0.0 788.6 jit_solution(18446061486531187790)
XLA Ops:
  7.2 28.0 %shard_map.238 = bf16[4,128,2048]{2,1,0:T(8,128)(2,1)} custom-call(bf16[512,8192]{1,0:T(8,128)(2,1)} %gate_ref.1, bf16[512,8192]{1,0:T(8,128)(2,1)} %up_ref.1), custom_call_target="tpu_custom_call" | custom-call | bytes 82500000 | tf_op jit(solution)/shard_map/pallas_call | solution.py:659
  37.0 59.5 %shard_map.239 = (bf16[8,256,2048]{2,1,0:T(8,128)(2,1)}, s32[8,1,256]{2,1,0:T(1,128)}, bf16[4,2,512]{2,1,0:T(2,128)(2,1)}, bf16[4,512,512]{2,1,0:T(8,128)(2,1)}) custom-call(bf16[256,2048]{1,0:T(8,128)(2,1)} %bitcast.61, s32[1,256]{1,0:T(1,128)} %get-tuple-element.102.code_ref, bf16[2,512]{1,0:T(2,128)(2,1)} %pad_maximum_fusion.1.gain_ref, ...), custom_call_target="tpu_custom_call" | custom-call | bytes 198000000 | tf_op jit(solution)/shard_map/pallas_call | solution.py:774
  101.2 75.2 %shard_map.240 = (f32[256,2048]{1,0:T(8,128)}, bf16[8,256,2048]{2,1,0:T(8,128)(2,1)}, bf16[8,256,384]{2,1,0:T(8,128)(2,1)}, bf16[8,256,256]{2,1,0:T(8,128)(2,1)}, bf16[8,256,2048]{2,1,0:T(8,128)(2,1)}) custom-call(bf16[8,256,2048]{2,1,0:T(8,128)(2,1)} %get-tuple-element.46.x_hbm, f32[1,2048]{1,0:T(1,128)} %bitcast.77, bf16[2048,512]{1,0:T(8,128)(2,1)} %bitcast.66, ...), custom_call_target="tpu_custom_call" | custom-call | bytes 231000000 | tf_op jit(solution)/shard_map/pallas_call | solution.py:1308
  179.7 5.6 all-gather.6.cloned.1.call-done
  185.3 56.2 %shard_map.241 = (bf16[8,256,2048]{2,1,0:T(8,128)(2,1)}, f32[2048,2048]{1,0:T(8,128)}, bf16[2048,1024]{1,0:T(8,128)(2,1)}, bf16[1024,2048]{1,0:T(8,128)(2,1)}) custom-call(bf16[256,2048]{1,0:T(8,128)(2,1)} %multiply_convert_fusion.3.x_ref, bf16[2048,2048]{1,0:T(8,128)(2,1)} %bitcast.59, bf16[8,256,2048]{2,1,0:T(8,128)(2,1)} %get-tuple-element.51.grad_hbm), custom_call_target="tpu_custom_call" | custom-call | bytes 165000000 | tf_op jit(solution)/shard_map/pallas_call | solution.py:916
  241.6 22.5 %multiply_convert_fusion = (bf16[2048,1024]{1,0:T(8,128)(2,1)}, bf16[2048,1024]{1,0:T(8,128)(2,1)S(1)}) fusion(f32[2048,2048]{1,0:T(8,128)} %get-tuple-element.55, bf16[2048,2048]{1,0:T(8,128)(2,1)} %bitcast.65, bf16[2048,2048]{1,0:T(8,128)(2,1)} %refs_1_.1, s32[]{:T(128)S(6)} %select_n.18), kind=kOutput, calls=%fused_computation | convolution fusion | flops 8617197568 | bytes 37748740 | tf_op jit(solution)/shard_map/sb,ab->sa/dot_general | solution.py:69
  264.1 13.1 %convolution_convert_fusion.1 = bf16[2048,1024]{1,0:T(8,128)(2,1)S(1)} fusion(bf16[2048,2048]{1,0:T(8,128)(2,1)} %bitcast.83, bf16[2048,1024]{1,0:T(8,128)(2,1)S(1)} %get-tuple-element.57.refs_0_), kind=kOutput, calls=%fused_computation.6 | convolution fusion | flops 8592031744 | bytes 16777216 | tf_op jit(solution)/shard_map/sa,sb->ab/dot_general | solution.py:65
  279.7 14.2 %convolution_convert_fusion.refs_2_ = bf16[2048,1024]{1,0:T(8,128)(2,1)} fusion(bf16[2048,2048]{1,0:T(8,128)(2,1)} %bitcast.84, bf16[2048,1024]{1,0:T(8,128)(2,1)} %get-tuple-element.92.refs_1_), kind=kOutput, calls=%fused_computation.5 | convolution fusion | flops 8592031744 | bytes 16777216 | tf_op jit(solution)/shard_map/sa,sb->ab/dot_general | solution.py:65
  293.9 47.6 %shard_map.242 = f32[256,2048]{1,0:T(8,128)} custom-call(bf16[2048,1024]{1,0:T(8,128)(2,1)} %copy-done.13, bf16[2048,1024]{1,0:T(8,128)(2,1)} %get-tuple-element.92.refs_1_, bf16[2048,2048]{1,0:T(8,128)(2,1)} %bitcast.60), custom_call_target="tpu_custom_call" | custom-call | bytes 145200000 | tf_op jit(solution)/shard_map/pallas_call | solution.py:1078
  345.6 40.6 %shard_map.243 = (bf16[8,256,2048]{2,1,0:T(8,128)(2,1)}, bf16[256,2048]{1,0:T(8,128)(2,1)}) custom-call(bf16[256,2048]{1,0:T(8,128)(2,1)} %multiply_convert_fusion.2.refs_0_, bf16[256,2048]{1,0:T(8,128)(2,1)} %reduce-scatter.3.cloned.1.call-done.refs_1_), custom_call_target="tpu_custom_call" | custom-call | bytes 132000000 | tf_op jit(solution)/shard_map/pallas_call | solution.py:607
  393.2 31.8 %shard_map.244 = (bf16[8,256,384]{2,1,0:T(8,128)(2,1)}, bf16[256,2048]{1,0:T(8,128)(2,1)S(1)}) custom-call(bf16[8,256,2048]{2,1,0:T(8,128)(2,1)} %get-tuple-element.58.out_grad_ref, bf16[256,2048]{1,0:T(8,128)(2,1)S(1)} %constant_dynamic-slice_fusion.2.w_ref, bf16[8,256,384]{2,1,0:T(8,128)(2,1)} %get-tuple-element.59.heads_ref, ...), custom_call_target="tpu_custom_call" | custom-call | bytes 82500000 | tf_op jit(solution)/shard_map/pallas_call | solution.py:1406
  426.0 42.7 %shard_map.245 = (f32[256,2048]{1,0:T(8,128)}, bf16[512,1024]{1,0:T(8,128)(2,1)}) custom-call(bf16[2048,384]{1,0:T(8,128)(2,1)} %bitcast.71, bf16[2048,384]{1,0:T(8,128)(2,1)} %pad_maximum_fusion.refs_1_, bf16[512,1024]{1,0:T(8,128)(2,1)} %reduce-scatter.5.cloned.1.call-done.refs_2_), custom_call_target="tpu_custom_call" | custom-call | bytes 145200000 | tf_op jit(solution)/shard_map/pallas_call | solution.py:1078
  468.7 9.6 %convolution_convert_fusion.2.refs_3_ = bf16[2048,384]{1,0:T(8,128)(2,1)} fusion(bf16[2048,2048]{1,0:T(8,128)(2,1)} %bitcast.82, bf16[2048,384]{1,0:T(8,128)(2,1)} %bitcast.72), kind=kOutput, calls=%fused_computation.13 | convolution fusion | flops 3222011904 | bytes 11534336 | tf_op jit(solution)/shard_map/sa,sb->ab/dot_general | solution.py:65
  480.0 205.8 %shard_map.246 = (f32[256,2048]{1,0:T(8,128)}, bf16[4,128,1024]{2,1,0:T(8,128)(2,1)}, bf16[2,2,4,256,1408]{4,3,2,1,0:T(8,128)(2,1)}, bf16[2,2,1,128,2048]{4,3,2,1,0:T(8,128)(2,1)}) custom-call(bf16[2048,1024]{1,0:T(8,128)(2,1)} %get-tuple-element.69.refs_0_, bf16[2048,2048]{1,0:T(8,128)(2,1)} %refs_1_.1, bf16[2048,1024]{1,0:T(8,128)(2,1)} %convolution_convert_fusion.refs_2_, ...), custom_call_target="tpu_custom_call" | custom-call | bytes 145200000 | tf_op jit(solution)/shard_map/pallas_call | solution.py:1078
  686.6 10.5 %shard_map.251 = f32[512,8192]{1,0:T(8,128)} custom-call(bf16[2,2,4,256,1408]{4,3,2,1,0:T(8,128)(2,1)} %get-tuple-element.72.q_ref.kv_ref.x_ref), custom_call_target="tpu_custom_call" | custom-call | bytes 26400000 | tf_op jit(solution)/shard_map/pallas_call | solution.py:1453
  697.0 4.5 shard_map.248
  701.5 10.4 %shard_map.252 = f32[2048,2048]{1,0:T(8,128)} custom-call(bf16[4,2,256,2048]{3,2,1,0:T(8,128)(2,1)} %bitcast.63), custom_call_target="tpu_custom_call" | custom-call | bytes 26400000 | tf_op jit(solution)/shard_map/pallas_call | solution.py:1430
  711.9 5.4 multiply_reduce_fusion
  718.0 3.9 concatenate.7
  721.9 13.5 %shard_map.247 = f32[40,128]{1,0:T(8,128)S(1)} custom-call(f32[40,128]{1,0:T(8,128)S(1)} %pad_bitcast_fusion.x_ref), custom_call_target="tpu_custom_call" | custom-call | bytes 33000000 | tf_op jit(solution)/shard_map/pallas_call | solution.py:1536
  736.0 4.2 shard_map.249
  742.1 4.6 fusion.15
  746.7 24.8 %all-gather.10.cloned.1.call-done = bf16[32,128,1024]{2,1,0:T(8,128)(2,1)} async-done(((bf16[4,128,1024]{2,1,0:T(8,128)(2,1)}), bf16[32,128,1024]{2,1,0:T(8,128)(2,1)}) %all-gather.10.cloned.1.call-update) | async-done | bytes 8388624 | tf_op jit(solution)/shard_map/all_gather | solution.py:1586
  771.5 10.3 %shard_map.250 = f32[512,8192]{1,0:T(8,128)} custom-call(bf16[4,2,4,128,1024]{4,3,2,1,0:T(8,128)(2,1)} %bitcast.64), custom_call_target="tpu_custom_call" | custom-call | bytes 26400000 | tf_op jit(solution)/shard_map/pallas_call | solution.py:1453
  (78 shorter events, 29.2 us)
Async XLA Ops:
  7.2 178.1 %all-gather.6.cloned.1.call-start = ((), (), s32[]{:S(2)}) async-start(), calls=%async_computation.2 | async-start | bytes 10485760 | tf_op jit(solution)/shard_map/all_gather | solution.py:1650
  35.2 0.7 copy-start.15
  35.2 0.7 copy-start.16
  35.2 1.3 copy-start.17
  35.2 1.3 copy-start.18
  35.3 310.4 %reduce-scatter.3.cloned.1.call-start = ((), (), s32[]{:S(2)}) async-start(), calls=%async_computation.3 | async-start | bytes 5242880 | tf_op jit(solution)/shard_map/reduce_scatter | solution.py:1581
  37.0 62.9 %copy-start.8 = (bf16[1,256,2048]{2,1,0:T(8,128)(2,1)S(1)}, bf16[1,256,2048]{2,1,0:T(8,128)(2,1)}, u32[]{:S(2)}) copy-start(bf16[1,256,2048]{2,1,0:T(8,128)(2,1)} %param.18) | copy-start | bytes 3145732
  101.2 75.3 %copy-start.7 = (bf16[1,256,2048]{2,1,0:T(8,128)(2,1)S(1)}, bf16[1,256,2048]{2,1,0:T(8,128)(2,1)}, u32[]{:S(2)}) copy-start(bf16[1,256,2048]{2,1,0:T(8,128)(2,1)} %param.15) | copy-start | bytes 3145732
  241.5 184.4 %reduce-scatter.5.cloned.1.call-start = ((), (), s32[]{:S(2)}) async-start(), calls=%async_computation.4 | async-start | bytes 5242880 | tf_op jit(solution)/shard_map/reduce_scatter | solution.py:1581
  264.1 13.1 %copy-start.13 = (bf16[2048,1024]{1,0:T(8,128)(2,1)}, bf16[2048,1024]{1,0:T(8,128)(2,1)S(1)}, u32[]{:S(2)}) copy-start(bf16[2048,1024]{1,0:T(8,128)(2,1)S(1)} %get-tuple-element.57.refs_0_) | copy-start | bytes 12582916
  279.7 200.4 %all-gather.8.cloned.1.call-start = ((), (), s32[]{:S(2)}) async-start(), calls=%async_computation.5 | async-start | bytes 9437184 | tf_op jit(solution)/shard_map/all_gather | solution.py:1586
  341.5 2.4 copy-start.6
  341.5 2.5 copy-start.9
  386.3 385.3 %all-gather.10.cloned.1.call-start = ((), (), s32[]{:S(2)}) async-start(), calls=%async_computation.6 | async-start | bytes 9437184 | tf_op jit(solution)/shard_map/all_gather | solution.py:1586
  388.6 1.9 copy-start.11
  388.6 2.3 copy-start.12
  390.9 1.5 copy-start
  390.9 1.5 copy-start.1
  390.9 1.8 copy-start.2
  390.9 2.3 copy-start.3
  390.9 2.3 copy-start.5
  425.0 1.0 copy-start.4
  711.9 5.4 copy-start.10
  711.9 5.4 copy-start.14
Sparse Core Ops, SparseCore 0:
  35.4 149.8 all-gather.5
  241.7 73.9 reduce-scatter.2
  318.7 77.2 reduce-scatter.4
  397.4 82.5 all-gather.7
  686.0 85.4 all-gather.9

commit v7 on v6

--- a/solution.py
+++ b/solution.py
@@ -285,8 +285,9 @@
 
 def column_place(place, reps):
     rep, core, own = place[:3]
-    up = (rep == 0, rep == reps - 1, (rep + 1, core, own), (rep - 1, core, own))
-    down = (rep == reps - 1, rep == 0, (rep - 1, core, own), (rep + 1, core, own))
+    above, below = ((rep + 1) % reps, core, own), ((rep + reps - 1) % reps, core, own)
+    up = (rep == 0, rep == reps - 1, above, below)
+    down = (rep == reps - 1, rep == 0, below, above)
     return (up, down)
 
 

time: 799 us -> 799 us (level)
  no operation moved by 1% of the time
where the time goes in v7:
time: 799 us; the launch traced here: 789 us
  Pallas kernels  641 us (80%)
  matrix products  59.3 us (7%)
  waiting for transfers between devices  32.3 us (4%)
  other arithmetic  25.1 us (3%)
  local copies, waits for them, and re-layouts  16 us (2%)
  between operations  14.9 us (2%)
    pallas_call x3, Pallas kernels, product_scatter(): pl.pallas_call(functools.partial(product_scatter_kernel, turned, count, j...  296 us
    pallas_call x1, Pallas kernels, attend(): pl.pallas_call(attend_kernel, out_shape=[jax.ShapeDtypeStruct((length, wi...  75.2 us
    pallas_call x1, Pallas kernels, start_plane(): pl.pallas_call(start_kernel, out_shape=[jax.ShapeDtypeStruct(s, d) for s,...  59.5 us
    pallas_call x1, Pallas kernels, mlp_plane(): pl.pallas_call(mlp_kernel, out_shape=[jax.ShapeDtypeStruct((8, rows, widt...  56.2 us
    pallas_call x1, Pallas kernels, gather_plane(): pl.pallas_call(functools.partial(gather_kernel, count, jobs), out_shape=[...  40.6 us
    dot_general x3, matrix products, contract_rows(): return jnp.einsum('sa,sb->ab', left, right, preferred_element_type=F32)  36.8 us
    pallas_call x1, Pallas kernels, attend_back(): pl.pallas_call(attend_back_kernel, grid=(members,), out_shape=[jax.ShapeD...  31.8 us
    pallas_call x1, Pallas kernels, quarter_columns(): pl.pallas_call(quarter_kernel, out_shape=jax.ShapeDtypeStruct((4,) + shap...  28 us
  transfers between devices with their start and end apart: 5, of which 3 were waited for; matrix products, arithmetic and copies ran while one was open for 12% of the time, Pallas kernels for 43%

profile of v7, /device:TPU:0, one launch (start us, length us, event | category | flops | bytes accessed | tf_op | source)
XLA Modules:
  0.0 788.6 jit_solution(6732346943366182974)
XLA Ops:
  7.2 28.0 %shard_map.238 = bf16[4,128,2048]{2,1,0:T(8,128)(2,1)} custom-call(bf16[512,8192]{1,0:T(8,128)(2,1)} %gate_ref.1, bf16[512,8192]{1,0:T(8,128)(2,1)} %up_ref.1), custom_call_target="tpu_custom_call" | custom-call | bytes 82500000 | tf_op jit(solution)/shard_map/pallas_call | solution.py:660
  37.0 59.5 %shard_map.239 = (bf16[8,256,2048]{2,1,0:T(8,128)(2,1)}, s32[8,1,256]{2,1,0:T(1,128)}, bf16[4,2,512]{2,1,0:T(2,128)(2,1)}, bf16[4,512,512]{2,1,0:T(8,128)(2,1)}) custom-call(bf16[256,2048]{1,0:T(8,128)(2,1)} %bitcast.61, s32[1,256]{1,0:T(1,128)} %get-tuple-element.102.code_ref, bf16[2,512]{1,0:T(2,128)(2,1)} %pad_maximum_fusion.1.gain_ref, ...), custom_call_target="tpu_custom_call" | custom-call | bytes 198000000 | tf_op jit(solution)/shard_map/pallas_call | solution.py:775
  101.2 75.2 %shard_map.240 = (f32[256,2048]{1,0:T(8,128)}, bf16[8,256,2048]{2,1,0:T(8,128)(2,1)}, bf16[8,256,384]{2,1,0:T(8,128)(2,1)}, bf16[8,256,256]{2,1,0:T(8,128)(2,1)}, bf16[8,256,2048]{2,1,0:T(8,128)(2,1)}) custom-call(bf16[8,256,2048]{2,1,0:T(8,128)(2,1)} %get-tuple-element.46.x_hbm, f32[1,2048]{1,0:T(1,128)} %bitcast.77, bf16[2048,512]{1,0:T(8,128)(2,1)} %bitcast.66, ...), custom_call_target="tpu_custom_call" | custom-call | bytes 231000000 | tf_op jit(solution)/shard_map/pallas_call | solution.py:1309
  179.7 5.6 all-gather.6.cloned.1.call-done
  185.3 56.2 %shard_map.241 = (bf16[8,256,2048]{2,1,0:T(8,128)(2,1)}, f32[2048,2048]{1,0:T(8,128)}, bf16[2048,1024]{1,0:T(8,128)(2,1)}, bf16[1024,2048]{1,0:T(8,128)(2,1)}) custom-call(bf16[256,2048]{1,0:T(8,128)(2,1)} %multiply_convert_fusion.3.x_ref, bf16[2048,2048]{1,0:T(8,128)(2,1)} %bitcast.59, bf16[8,256,2048]{2,1,0:T(8,128)(2,1)} %get-tuple-element.51.grad_hbm), custom_call_target="tpu_custom_call" | custom-call | bytes 165000000 | tf_op jit(solution)/shard_map/pallas_call | solution.py:917
  241.6 22.5 %multiply_convert_fusion = (bf16[2048,1024]{1,0:T(8,128)(2,1)}, bf16[2048,1024]{1,0:T(8,128)(2,1)S(1)}) fusion(f32[2048,2048]{1,0:T(8,128)} %get-tuple-element.55, bf16[2048,2048]{1,0:T(8,128)(2,1)} %bitcast.65, bf16[2048,2048]{1,0:T(8,128)(2,1)} %refs_1_.1, s32[]{:T(128)S(6)} %select_n.18), kind=kOutput, calls=%fused_computation | convolution fusion | flops 8617197568 | bytes 37748740 | tf_op jit(solution)/shard_map/sb,ab->sa/dot_general | solution.py:69
  264.1 13.1 %convolution_convert_fusion.1 = bf16[2048,1024]{1,0:T(8,128)(2,1)S(1)} fusion(bf16[2048,2048]{1,0:T(8,128)(2,1)} %bitcast.83, bf16[2048,1024]{1,0:T(8,128)(2,1)S(1)} %get-tuple-element.57.refs_0_), kind=kOutput, calls=%fused_computation.6 | convolution fusion | flops 8592031744 | bytes 16777216 | tf_op jit(solution)/shard_map/sa,sb->ab/dot_general | solution.py:65
  279.7 14.2 %convolution_convert_fusion.refs_2_ = bf16[2048,1024]{1,0:T(8,128)(2,1)} fusion(bf16[2048,2048]{1,0:T(8,128)(2,1)} %bitcast.84, bf16[2048,1024]{1,0:T(8,128)(2,1)} %get-tuple-element.92.refs_1_), kind=kOutput, calls=%fused_computation.5 | convolution fusion | flops 8592031744 | bytes 16777216 | tf_op jit(solution)/shard_map/sa,sb->ab/dot_general | solution.py:65
  293.9 47.6 %shard_map.242 = f32[256,2048]{1,0:T(8,128)} custom-call(bf16[2048,1024]{1,0:T(8,128)(2,1)} %copy-done.13, bf16[2048,1024]{1,0:T(8,128)(2,1)} %get-tuple-element.92.refs_1_, bf16[2048,2048]{1,0:T(8,128)(2,1)} %bitcast.60), custom_call_target="tpu_custom_call" | custom-call | bytes 145200000 | tf_op jit(solution)/shard_map/pallas_call | solution.py:1079
  345.6 40.6 %shard_map.243 = (bf16[8,256,2048]{2,1,0:T(8,128)(2,1)}, bf16[256,2048]{1,0:T(8,128)(2,1)}) custom-call(bf16[256,2048]{1,0:T(8,128)(2,1)} %multiply_convert_fusion.2.refs_0_, bf16[256,2048]{1,0:T(8,128)(2,1)} %reduce-scatter.3.cloned.1.call-done.refs_1_), custom_call_target="tpu_custom_call" | custom-call | bytes 132000000 | tf_op jit(solution)/shard_map/pallas_call | solution.py:608
  393.2 31.8 %shard_map.244 = (bf16[8,256,384]{2,1,0:T(8,128)(2,1)}, bf16[256,2048]{1,0:T(8,128)(2,1)S(1)}) custom-call(bf16[8,256,2048]{2,1,0:T(8,128)(2,1)} %get-tuple-element.58.out_grad_ref, bf16[256,2048]{1,0:T(8,128)(2,1)S(1)} %constant_dynamic-slice_fusion.2.w_ref, bf16[8,256,384]{2,1,0:T(8,128)(2,1)} %get-tuple-element.59.heads_ref, ...), custom_call_target="tpu_custom_call" | custom-call | bytes 82500000 | tf_op jit(solution)/shard_map/pallas_call | solution.py:1407
  426.0 42.7 %shard_map.245 = (f32[256,2048]{1,0:T(8,128)}, bf16[512,1024]{1,0:T(8,128)(2,1)}) custom-call(bf16[2048,384]{1,0:T(8,128)(2,1)} %bitcast.71, bf16[2048,384]{1,0:T(8,128)(2,1)} %pad_maximum_fusion.refs_1_, bf16[512,1024]{1,0:T(8,128)(2,1)} %reduce-scatter.5.cloned.1.call-done.refs_2_), custom_call_target="tpu_custom_call" | custom-call | bytes 145200000 | tf_op jit(solution)/shard_map/pallas_call | solution.py:1079
  468.7 9.6 %convolution_convert_fusion.2.refs_3_ = bf16[2048,384]{1,0:T(8,128)(2,1)} fusion(bf16[2048,2048]{1,0:T(8,128)(2,1)} %bitcast.82, bf16[2048,384]{1,0:T(8,128)(2,1)} %bitcast.72), kind=kOutput, calls=%fused_computation.13 | convolution fusion | flops 3222011904 | bytes 11534336 | tf_op jit(solution)/shard_map/sa,sb->ab/dot_general | solution.py:65
  480.0 205.8 %shard_map.246 = (f32[256,2048]{1,0:T(8,128)}, bf16[4,128,1024]{2,1,0:T(8,128)(2,1)}, bf16[2,2,4,256,1408]{4,3,2,1,0:T(8,128)(2,1)}, bf16[2,2,1,128,2048]{4,3,2,1,0:T(8,128)(2,1)}) custom-call(bf16[2048,1024]{1,0:T(8,128)(2,1)} %get-tuple-element.69.refs_0_, bf16[2048,2048]{1,0:T(8,128)(2,1)} %refs_1_.1, bf16[2048,1024]{1,0:T(8,128)(2,1)} %convolution_convert_fusion.refs_2_, ...), custom_call_target="tpu_custom_call" | custom-call | bytes 145200000 | tf_op jit(solution)/shard_map/pallas_call | solution.py:1079
  686.6 10.5 %shard_map.251 = f32[512,8192]{1,0:T(8,128)} custom-call(bf16[2,2,4,256,1408]{4,3,2,1,0:T(8,128)(2,1)} %get-tuple-element.72.q_ref.kv_ref.x_ref), custom_call_target="tpu_custom_call" | custom-call | bytes 26400000 | tf_op jit(solution)/shard_map/pallas_call | solution.py:1454
  697.1 4.5 shard_map.248
  701.5 10.4 %shard_map.252 = f32[2048,2048]{1,0:T(8,128)} custom-call(bf16[4,2,256,2048]{3,2,1,0:T(8,128)(2,1)} %bitcast.63), custom_call_target="tpu_custom_call" | custom-call | bytes 26400000 | tf_op jit(solution)/shard_map/pallas_call | solution.py:1431
  711.9 5.4 multiply_reduce_fusion
  718.0 3.9 concatenate.7
  721.9 13.5 %shard_map.247 = f32[40,128]{1,0:T(8,128)S(1)} custom-call(f32[40,128]{1,0:T(8,128)S(1)} %pad_bitcast_fusion.x_ref), custom_call_target="tpu_custom_call" | custom-call | bytes 33000000 | tf_op jit(solution)/shard_map/pallas_call | solution.py:1537
  736.1 4.2 shard_map.249
  742.1 4.6 fusion.15
  746.7 24.8 %all-gather.10.cloned.1.call-done = bf16[32,128,1024]{2,1,0:T(8,128)(2,1)} async-done(((bf16[4,128,1024]{2,1,0:T(8,128)(2,1)}), bf16[32,128,1024]{2,1,0:T(8,128)(2,1)}) %all-gather.10.cloned.1.call-update) | async-done | bytes 8388624 | tf_op jit(solution)/shard_map/all_gather | solution.py:1587
  771.6 10.3 %shard_map.250 = f32[512,8192]{1,0:T(8,128)} custom-call(bf16[4,2,4,128,1024]{4,3,2,1,0:T(8,128)(2,1)} %bitcast.64), custom_call_target="tpu_custom_call" | custom-call | bytes 26400000 | tf_op jit(solution)/shard_map/pallas_call | solution.py:1454
  (78 shorter events, 29.2 us)
Async XLA Ops:
  7.2 178.1 %all-gather.6.cloned.1.call-start = ((), (), s32[]{:S(2)}) async-start(), calls=%async_computation.2 | async-start | bytes 10485760 | tf_op jit(solution)/shard_map/all_gather | solution.py:1651
  35.2 0.7 copy-start.15
  35.2 0.7 copy-start.16
  35.2 1.3 copy-start.17
  35.2 1.3 copy-start.18
  35.3 310.4 %reduce-scatter.3.cloned.1.call-start = ((), (), s32[]{:S(2)}) async-start(), calls=%async_computation.3 | async-start | bytes 5242880 | tf_op jit(solution)/shard_map/reduce_scatter | solution.py:1582
  37.0 62.9 %copy-start.8 = (bf16[1,256,2048]{2,1,0:T(8,128)(2,1)S(1)}, bf16[1,256,2048]{2,1,0:T(8,128)(2,1)}, u32[]{:S(2)}) copy-start(bf16[1,256,2048]{2,1,0:T(8,128)(2,1)} %param.18) | copy-start | bytes 3145732
  101.2 75.3 %copy-start.7 = (bf16[1,256,2048]{2,1,0:T(8,128)(2,1)S(1)}, bf16[1,256,2048]{2,1,0:T(8,128)(2,1)}, u32[]{:S(2)}) copy-start(bf16[1,256,2048]{2,1,0:T(8,128)(2,1)} %param.15) | copy-start | bytes 3145732
  241.5 184.4 %reduce-scatter.5.cloned.1.call-start = ((), (), s32[]{:S(2)}) async-start(), calls=%async_computation.4 | async-start | bytes 5242880 | tf_op jit(solution)/shard_map/reduce_scatter | solution.py:1582
  264.1 13.1 %copy-start.13 = (bf16[2048,1024]{1,0:T(8,128)(2,1)}, bf16[2048,1024]{1,0:T(8,128)(2,1)S(1)}, u32[]{:S(2)}) copy-start(bf16[2048,1024]{1,0:T(8,128)(2,1)S(1)} %get-tuple-element.57.refs_0_) | copy-start | bytes 12582916
  279.7 200.4 %all-gather.8.cloned.1.call-start = ((), (), s32[]{:S(2)}) async-start(), calls=%async_computation.5 | async-start | bytes 9437184 | tf_op jit(solution)/shard_map/all_gather | solution.py:1587
  341.5 2.4 copy-start.6
  341.5 2.5 copy-start.9
  386.3 385.3 %all-gather.10.cloned.1.call-start = ((), (), s32[]{:S(2)}) async-start(), calls=%async_computation.6 | async-start | bytes 9437184 | tf_op jit(solution)/shard_map/all_gather | solution.py:1587
  388.6 1.9 copy-start.11
  388.6 2.3 copy-start.12
  390.9 1.5 copy-start
  390.9 1.5 copy-start.1
  390.9 1.8 copy-start.2
  390.9 2.3 copy-start.3
  390.9 2.3 copy-start.5
  425.0 1.0 copy-start.4
  711.9 5.4 copy-start.10
  711.9 5.4 copy-start.14
Sparse Core Ops, SparseCore 0:
  35.4 149.8 all-gather.5
  241.7 73.9 reduce-scatter.2
  318.7 77.2 reduce-scatter.4
  397.4 82.5 all-gather.7
  686.0 85.5 all-gather.9
